TPU v7x, 512 devices: a whole 4x8x8 slice. The times are simulated.
512 devices in a mesh: frame: 64 (over x, y_hi, z), group: 8 (over y_lo, core).
Axes of the slice: x: 4, y: 8 (y_hi: 2, y_lo: 4; y = y_hi * 4 + y_lo), z: 8, core: 2. Of those that a mesh axis runs over, the one named last changes fastest.
Arguments:
- queries: bfloat16 [8192, 8192], P('frame', 'group'), may hold values from -6 to 6
- keys: bfloat16 [8192, 1024], P('frame', 'group'), may hold values from -50 to 50
- values: bfloat16 [8192, 1024], P('frame', 'group'), may hold values from -6 to 6
- q_gain: float32 [128], replicated, may hold values from 0.4 to 2.5
- frame_bounds: int32 [2, 8192], P(None, 'frame'), may hold values from 0 to 64, as said below
- output_weight: bfloat16 [8, 1024, 4096], P('group', 'frame'), may hold values from -0.25 to 0.25
- attn_gate: float32 [1], replicated, may hold values from 0.4 to 1.6
Outputs:
- projected: bfloat16 [8192, 4096], P('frame', 'group')
Inputs may be any that keep to these rules, and one draw needn't show every extreme that they name: `frame_bounds`: row 0 is below row 1 for every text token.
All inputs are finite; a program needn't handle non-finite values.
Results may differ from a plain program's by a relative error of at most 0.008.
The roundings to bfloat16 on the way count: a program that leaves them out, or rounds other values in their place, can miss the bound.
Values may be sent and summed in bfloat16 or wider, within the bound.
No kernel may reach another device: no remote copies, remote signals or barrier semaphores. Data moves between devices by JAX's collectives and lax.ppermute only.
A program may use at most 64 MiB of HBM per device.

v0:
```python
import math

import jax
import jax.numpy as jnp
from jax import lax
from jax.experimental import pallas as pl
from jax.experimental.pallas import tpu as pltpu
from jax.sharding import Mesh, PartitionSpec as P


D = 128
HEADS = 8
TOK = 128
ROWS = HEADS * TOK
SUB = 8
KEYS = 4
WIDE = 256
LOW = -1e30
EXP2_SCALE = math.log2(math.e) / math.sqrt(D)


def shift(value, axis, steps):
    count = lax.axis_size(axis)
    return lax.ppermute(value, axis, [(s, (s + steps) % count) for s in range(count)])


def attention_kernel(n_chunks, first, last, ids_ref, *refs):
    refs = list(refs)
    bounds_ref = refs.pop(0)
    chunks = [refs.pop(0) for _ in range(n_chunks)]
    if first:
        q_ref, gain_ref = refs.pop(0), refs.pop(0)
    else:
        nq_in, m_in, l_in, acc_in = [refs.pop(0) for _ in range(4)]
    if last:
        out_ref = refs.pop(0)
    else:
        nq_out, m_out, l_out, acc_out = [refs.pop(0) for _ in range(4)]
    if first:
        nq_ref = nq_out
        for h in range(HEADS):
            x = q_ref[:, h * D : (h + 1) * D].astype(jnp.float32)
            mean = jnp.mean(x * x, axis=-1, keepdims=True)
            x = x * lax.rsqrt(mean + 1e-05) * gain_ref[...]
            nq_ref[h * TOK : (h + 1) * TOK, :] = x.astype(jnp.bfloat16)
    else:
        nq_ref = nq_in
    lower = jnp.concatenate([bounds_ref[0:1, :]] * (WIDE // TOK), axis=1)
    upper = jnp.concatenate([bounds_ref[1:2, :]] * (WIDE // TOK), axis=1)
    cols = [slice(w * WIDE, (w + 1) * WIDE) for w in range(ROWS // WIDE)]
    if first:
        state = [
            (
                jnp.full((1, WIDE), LOW, jnp.float32),
                jnp.zeros((8, WIDE), jnp.float32),
                jnp.zeros((D, WIDE), jnp.float32),
            )
            for _ in cols
        ]
    else:
        state = [(m_in[:, c], l_in[:, c], acc_in[:, c]) for c in cols]
    units = [
        (c, i, w)
        for c in range(n_chunks)
        for i in range(SUB // KEYS)
        for w in range(len(cols))
    ]

    def score(unit):
        c, i, w = unit
        k = chunks[c][i * KEYS : (i + 1) * KEYS, 0].reshape(KEYS * D, D)
        return lax.dot_general(
            k,
            nq_ref[cols[w], :],
            (((1,), (1,)), ((), ())),
            preferred_element_type=jnp.float32,
        )

    def soften(unit, s, m, l):
        c, i, _ = unit
        allowed = []
        new = m
        for j in range(KEYS):
            block = ids_ref[c * SUB + i * KEYS + j]
            ok = (lower <= block) & (block < upper)
            top = jnp.max(s[j * D : (j + 1) * D], axis=0, keepdims=True)
            new = jnp.maximum(new, jnp.where(ok, top, LOW))
            allowed.append(ok)
        factor = jnp.exp2((m - new) * EXP2_SCALE)
        l = l * factor
        parts = []
        for j in range(KEYS):
            base = jnp.where(allowed[j], new * EXP2_SCALE, -LOW)
            p = jnp.exp2(s[j * D : (j + 1) * D] * EXP2_SCALE - base)
            l = l + jnp.sum(p.reshape(D // 8, 8, WIDE), axis=0)
            parts.append(p.astype(jnp.bfloat16))
        return jnp.concatenate(parts, axis=0), new, l, factor

    def gather(unit, p, acc, factor):
        c, i, _ = unit
        v = chunks[c][i * KEYS : (i + 1) * KEYS, 1].reshape(KEYS * D, D)
        return acc * factor + lax.dot_general(
            v, p, (((0,), (0,)), ((), ())), preferred_element_type=jnp.float32
        )

    ahead = score(units[0])
    pending = None
    for at, unit in enumerate(units):
        s = ahead
        if at + 1 < len(units):
            ahead = score(units[at + 1])
        w = unit[2]
        m, l, acc = state[w]
        p, m, l, factor = soften(unit, s, m, l)
        if pending is not None:
            u, p0, f0 = pending
            m0, l0, acc0 = state[u[2]]
            state[u[2]] = (m0, l0, gather(u, p0, acc0, f0))
        state[w] = (m, l, state[w][2])
        pending = (unit, p, factor)
    u, p0, f0 = pending
    m0, l0, acc0 = state[u[2]]
    state[u[2]] = (m0, l0, gather(u, p0, acc0, f0))

    for w, (m, l, acc) in enumerate(state):
        if last:
            o = acc / jnp.sum(l, axis=0, keepdims=True)
            for u in range(WIDE // TOK):
                head = w * (WIDE // TOK) + u
                out_ref[:, head * D : (head + 1) * D] = (
                    o[:, u * TOK : (u + 1) * TOK].T.astype(jnp.bfloat16)
                )
        else:
            m_out[:, cols[w]] = m
            l_out[:, cols[w]] = l
            acc_out[:, cols[w]] = acc
    if not first and not last:
        nq_out[...] = nq_in[...]


def attend(ids, bounds, chunks, start, state, last):
    first = state is None
    vm = pl.BlockSpec(memory_space=pltpu.VMEM)
    carried = (
        jax.ShapeDtypeStruct((ROWS, D), jnp.bfloat16),
        jax.ShapeDtypeStruct((1, ROWS), jnp.float32),
        jax.ShapeDtypeStruct((8, ROWS), jnp.float32),
        jax.ShapeDtypeStruct((D, ROWS), jnp.float32),
    )
    out_shape = jax.ShapeDtypeStruct((TOK, ROWS), jnp.bfloat16) if last else carried
    extra = start if first else state
    n_keys = len(chunks) * SUB * D

    def body(*refs):
        attention_kernel(len(chunks), first, last, *refs)

    return pl.pallas_call(
        body,
        out_shape=out_shape,
        in_specs=[pl.BlockSpec(memory_space=pltpu.SMEM)]
        + [vm] * (1 + len(chunks) + len(extra)),
        out_specs=vm if last else (vm,) * 4,
        cost_estimate=pl.CostEstimate(
            flops=4 * ROWS * n_keys * D,
            bytes_accessed=n_keys * D * 4 + ROWS * D * 12,
            transcendentals=ROWS * n_keys,
        ),
        compiler_params=pltpu.CompilerParams(vmem_limit_bytes=40 << 20),
    )(ids, bounds, *chunks, *extra)


def project_kernel(col_ref, a_ref, w_ref, out_ref):
    total = None
    for x in range(4):
        w = jnp.concatenate([w_ref[:, 0, x], w_ref[:, 1, x]]).reshape(256, 512)
        part = jnp.dot(
            a_ref[:, x * 256 : (x + 1) * 256], w, preferred_element_type=jnp.float32
        )
        total = part if total is None else total + part
    out_ref[...] = total.reshape(4, TOK, 512)


def project(column, attended, weight):
    return pl.pallas_call(
        project_kernel,
        grid_spec=pltpu.PrefetchScalarGridSpec(
            num_scalar_prefetch=1,
            grid=(1,),
            in_specs=[
                pl.BlockSpec((4 * TOK, ROWS), lambda i, col: (0, 0)),
                pl.BlockSpec((8, 2, 4, 16, 512), lambda i, col: (0, 0, 0, 0, col[0])),
            ],
            out_specs=pl.BlockSpec((4, TOK, 512), lambda i, col: (0, 0, 0)),
        ),
        out_shape=jax.ShapeDtypeStruct((4, TOK, 512), jnp.float32),
        cost_estimate=pl.CostEstimate(
            flops=512 * 1024 * 1024, bytes_accessed=3 << 20, transcendentals=0
        ),
        compiler_params=pltpu.CompilerParams(vmem_limit_bytes=32 << 20),
    )(column, attended, weight)


def work(queries, keys, values, q_gain, frame_bounds, output_weight, attn_gate):
    ax, ay, az = lax.axis_index("x"), lax.axis_index("yh"), lax.axis_index("z")
    core = lax.axis_index("c")

    own = jnp.stack([keys, values])[None]
    other = shift(own, "yh", 1)
    quarter = output_weight[0].reshape(16, 4, 1024).transpose(1, 0, 2)
    quarter = lax.all_to_all(
        quarter.reshape(64, 1024), "x", split_axis=0, concat_axis=0, tiled=True
    )
    partner = shift(quarter, "yh", 1)
    both = jnp.stack(
        [jnp.where(ay == 0, quarter, partner), jnp.where(ay == 0, partner, quarter)]
    )
    weight = lax.all_gather(both.reshape(128, 1024), "z", axis=0, tiled=True)
    weight = weight.reshape(8, 2, 4, 16, 1024)

    pair = jnp.concatenate([own, other])
    chunk = jnp.concatenate(
        [pair, shift(pair, "x", 1), shift(pair, "x", -1), shift(pair, "x", 2)]
    )
    hops = ([0, -1, 1, 2], [0, -1, 1, -2, 2, -3, 3, -4])
    in_chunk = jnp.stack(
        [((ax + h) % 4) * 16 + ((ay + y) % 2) * 8 for h in hops[0] for y in (0, 1)]
    ).astype(jnp.int32)
    ids = [in_chunk + (az + h) % 8 for h in hops[1]]

    right, left = [chunk], [chunk]
    for s in range(1, 5):
        right.append(shift(right[-1], "z", 1))
        if s < 4:
            left.append(shift(left[-1], "z", -1))
    start = (queries, q_gain[None, :])
    state = attend(ids[0], frame_bounds, [chunk], start, None, False)
    for s in range(1, 4):
        state = attend(
            jnp.concatenate(ids[2 * s - 1 : 2 * s + 1]),
            frame_bounds,
            [right[s], left[s]],
            start,
            state,
            False,
        )
    attended = attend(ids[7], frame_bounds, [right[4]], start, state, True)

    rel = [0, -1, 1, 2]
    gathered = jnp.concatenate(
        [attended] + [shift(attended, "x", -r) for r in rel[1:]], axis=0
    )
    core = core.astype(jnp.int32)[None]
    for_other = project(1 - core, gathered, weight)
    from_other = shift(for_other, "c", 1)
    for_own = project(core, gathered, weight)
    partial = (for_own + from_other).astype(jnp.bfloat16).reshape(512, 512)
    pieces = lax.all_to_all(partial, "yl", split_axis=0, concat_axis=0, tiled=True)
    combined = jnp.sum(pieces.reshape(4, TOK, 512).astype(jnp.float32), axis=0)
    result = (jnp.tanh(attn_gate[0]) * combined).astype(jnp.bfloat16)
    pairs = [
        (x * 4 + y, ((x + rel[y]) % 4) * 4 + x) for x in range(4) for y in range(4)
    ]
    return lax.ppermute(result, ("x", "yl"), pairs)


def solution(mesh):
    fine = Mesh(mesh.devices.reshape(4, 2, 8, 4, 2), ("x", "yh", "z", "yl", "c"))
    frame, group = ("x", "yh", "z"), ("yl", "c")
    placed = (
        P(frame, group),
        P(frame, group),
        P(frame, group),
        P(),
        P(None, frame),
        P(group, frame, None),
        P(),
    )
    return jax.shard_map(
        work, mesh=fine, in_specs=placed, out_specs=P(frame, group), check_vma=False
    )
```

profile of v0, /device:TPU:7, one launch (start us, length us, event | category | flops | bytes accessed | tf_op | source)
XLA Modules:
  0.0 196.9 jit_solution(3001854731554010368)
XLA Ops:
  6.6 1.1 reshape_squeeze.3
  7.7 7.1 %all_to_all.15 = bf16[4,16,1024]{2,1,0:T(8,128)(2,1)S(1)} all-to-all(bf16[4,16,1024]{2,1,0:T(8,128)(2,1)S(1)} %copy.9), channel_id=1, replica_groups=mesh['x'=4,'yh'=2,'z'=8,'yl'=4,'c'=2] {'x'}, dimensions={0} | all-to-all | bytes 262144 | tf_op jit(solution)/shard_map/all_to_all | solution.py:210
  14.8 7.4 %collective-permute-start.14 = (bf16[64,1024]{1,0:T(8,128)(2,1)S(1)}, bf16[64,1024]{1,0:T(8,128)(2,1)S(1)}, u32[]{:S(2)}, u32[]{:S(2)}) collective-permute-start(bf16[64,1024]{1,0:T(8,128)(2,1)S(1)} %bitcast.31), channel_id=1, source_target_pairs={{0,64},{64,0},{1,65},{65,1},{2,66},{66,2},{3,67},{67,3},{4,68},{68... | collective-permute-start | bytes 393224 | tf_op jit(solution)/shard_map/ppermute | solution.py:24
  22.2 2.4 %collective-permute-done.14 = bf16[64,1024]{1,0:T(8,128)(2,1)S(1)} collective-permute-done((bf16[64,1024]{1,0:T(8,128)(2,1)S(1)}, bf16[64,1024]{1,0:T(8,128)(2,1)S(1)}, u32[]{:S(2)}, u32[]{:S(2)}) %collective-permute-start.14) | collective-permute-done | bytes 131104 | tf_op jit(solution)/shard_map/ppermute | solution.py:24
  24.7 0.7 pad_maximum_fusion.1
  25.5 10.4 %collective-permute-start = (bf16[1,2,128,128]{3,2,1,0:T(8,128)(2,1)S(1)}, bf16[1,2,128,128]{3,2,1,0:T(8,128)(2,1)S(1)}, u32[]{:S(2)}, u32[]{:S(2)}) collective-permute-start(bf16[1,2,128,128]{3,2,1,0:T(8,128)(2,1)S(1)} %maximum_bitcast_fusion), channel_id=1, source_target_pairs={{0,64},{64,0},{1,65},{65,1},{2,66},{66,2},{3,67},{67,3},{4,68},{68... | collective-permute-start | bytes 196616 | tf_op jit(solution)/shard_map/ppermute | solution.py:24
  35.9 2.4 %collective-permute-done = bf16[1,2,128,128]{3,2,1,0:T(8,128)(2,1)S(1)} collective-permute-done((bf16[1,2,128,128]{3,2,1,0:T(8,128)(2,1)S(1)}, bf16[1,2,128,128]{3,2,1,0:T(8,128)(2,1)S(1)}, u32[]{:S(2)}, u32[]{:S(2)}) %collective-permute-start) | collective-permute-done | bytes 65568 | tf_op jit(solution)/shard_map/ppermute | solution.py:24
  38.3 3.7 %collective-permute-start.1 = (bf16[2,2,128,128]{3,2,1,0:T(8,128)(2,1)S(1)}, bf16[2,2,128,128]{3,2,1,0:T(8,128)(2,1)S(1)}, u32[]{:S(2)}, u32[]{:S(2)}) collective-permute-start(bf16[2,2,128,128]{3,2,1,0:T(8,128)(2,1)S(1)} %pad_maximum_fusion.2), channel_id=1, source_target_pairs={{0,128},{128,256},{256,384},{384,0},{1,129},{129,257},{257,385},{3... | collective-permute-start | bytes 393224 | tf_op jit(solution)/shard_map/ppermute | solution.py:24
  42.1 1.9 collective-permute-start.2
  44.0 3.4 %collective-permute-start.3 = (bf16[2,2,128,128]{3,2,1,0:T(8,128)(2,1)S(1)}, bf16[2,2,128,128]{3,2,1,0:T(8,128)(2,1)S(1)}, u32[]{:S(2)}, u32[]{:S(2)}) collective-permute-start(bf16[2,2,128,128]{3,2,1,0:T(8,128)(2,1)S(1)} %pad_maximum_fusion.2), channel_id=1, source_target_pairs={{0,256},{128,384},{256,0},{384,128},{1,257},{129,385},{257,1},{385... | collective-permute-start | bytes 393224 | tf_op jit(solution)/shard_map/ppermute | solution.py:24
  47.4 1.6 collective-permute-done.2
  49.0 2.2 %collective-permute-done.3 = bf16[2,2,128,128]{3,2,1,0:T(8,128)(2,1)S(1)} collective-permute-done((bf16[2,2,128,128]{3,2,1,0:T(8,128)(2,1)S(1)}, bf16[2,2,128,128]{3,2,1,0:T(8,128)(2,1)S(1)}, u32[]{:S(2)}, u32[]{:S(2)}) %collective-permute-start.3) | collective-permute-done | bytes 131104 | tf_op jit(solution)/shard_map/ppermute | solution.py:24
  51.2 1.9 collective-permute-start.4
  53.2 7.8 %collective-permute-start.8 = (bf16[8,2,128,128]{3,2,1,0:T(8,128)(2,1)S(1)}, bf16[8,2,128,128]{3,2,1,0:T(8,128)(2,1)S(1)}, u32[]{:S(2)}, u32[]{:S(2)}) collective-permute-start(bf16[8,2,128,128]{3,2,1,0:T(8,128)(2,1)S(1)} %constant_dynamic-update-slice_fusion.refs_2_), channel_id=1, source_target_pairs={{0,56},{8,0},{16,8},{24,16},{32,24},{40,32},{48,40},{56,48},{1,57}... | collective-permute-start | bytes 1572872 | tf_op jit(solution)/shard_map/ppermute | solution.py:24
  61.0 19.3 %collective-permute-done.4.refs_2_ = bf16[8,2,128,128]{3,2,1,0:T(8,128)(2,1)S(1)} collective-permute-done((bf16[8,2,128,128]{3,2,1,0:T(8,128)(2,1)S(1)}, bf16[8,2,128,128]{3,2,1,0:T(8,128)(2,1)S(1)}, u32[]{:S(2)}, u32[]{:S(2)}) %collective-permute-start.4) | collective-permute-done | bytes 524320 | tf_op jit(solution)/shard_map/ppermute | solution.py:24
  80.2 1.9 collective-permute-start.5
  82.1 4.6 %collective-permute-start.9 = (bf16[8,2,128,128]{3,2,1,0:T(8,128)(2,1)S(1)}, bf16[8,2,128,128]{3,2,1,0:T(8,128)(2,1)S(1)}, u32[]{:S(2)}, u32[]{:S(2)}) collective-permute-start(bf16[8,2,128,128]{3,2,1,0:T(8,128)(2,1)S(1)} %collective-permute-done.8.refs_3_), channel_id=1, source_target_pairs={{0,56},{8,0},{16,8},{24,16},{32,24},{40,32},{48,40},{56,48},{1,57}... | collective-permute-start | bytes 1572872 | tf_op jit(solution)/shard_map/ppermute | solution.py:24
  86.7 5.4 %collective-permute-done.5.refs_2_ = bf16[8,2,128,128]{3,2,1,0:T(8,128)(2,1)S(1)} collective-permute-done((bf16[8,2,128,128]{3,2,1,0:T(8,128)(2,1)S(1)}, bf16[8,2,128,128]{3,2,1,0:T(8,128)(2,1)S(1)}, u32[]{:S(2)}, u32[]{:S(2)}) %collective-permute-start.5) | collective-permute-done | bytes 524320 | tf_op jit(solution)/shard_map/ppermute | solution.py:24
  92.1 1.9 collective-permute-start.6
  94.2 0.1 stack.53
  94.3 4.6 %collective-permute-start.10 = (bf16[8,2,128,128]{3,2,1,0:T(8,128)(2,1)S(1)}, bf16[8,2,128,128]{3,2,1,0:T(8,128)(2,1)S(1)}, u32[]{:S(2)}, u32[]{:S(2)}) collective-permute-start(bf16[8,2,128,128]{3,2,1,0:T(8,128)(2,1)S(1)} %collective-permute-done.9.refs_3_), channel_id=1, source_target_pairs={{0,56},{8,0},{16,8},{24,16},{32,24},{40,32},{48,40},{56,48},{1,57}... | collective-permute-start | bytes 1572872 | tf_op jit(solution)/shard_map/ppermute | solution.py:24
  98.9 0.1 pad_add_fusion.2.refs_0_
  99.0 4.3 %collective-permute-done.6.refs_2_ = bf16[8,2,128,128]{3,2,1,0:T(8,128)(2,1)S(1)} collective-permute-done((bf16[8,2,128,128]{3,2,1,0:T(8,128)(2,1)S(1)}, bf16[8,2,128,128]{3,2,1,0:T(8,128)(2,1)S(1)}, u32[]{:S(2)}, u32[]{:S(2)}) %collective-permute-start.6) | collective-permute-done | bytes 524320 | tf_op jit(solution)/shard_map/ppermute | solution.py:24
  103.2 1.9 collective-permute-start.7
  105.2 0.1 pad_add_fusion.1.refs_0_
  105.2 0.1 pad_add_fusion.refs_0_
  105.3 2.4 %shard_map.73 = (bf16[1024,128]{1,0:T(8,128)(2,1)S(1)}, f32[1,1024]{1,0:T(1,128)S(1)}, f32[8,1024]{1,0:T(8,128)S(1)}, f32[128,1024]{1,0:T(8,128)S(1)}) custom-call(s32[8]{0:T(128)S(1)} %get-tuple-element.39.refs_0_, s32[2,128]{1,0:T(2,128)S(1)} %copy-done.3, bf16[8,2,128,128]{3,2,1,0:T(8,128)(2,1)S(1)} %constant_dynamic-update-slice_fusion.refs_2_, ...), custom_call_target="tpu_custom_call" | custom-call | flops 536870912 | bytes 2097152 | tf_op jit(solution)/shard_map/pallas_call | solution.py:157
  107.7 3.6 %shard_map.74 = (bf16[1024,128]{1,0:T(8,128)(2,1)S(1)}, f32[1,1024]{1,0:T(1,128)S(1)}, f32[8,1024]{1,0:T(8,128)S(1)}, f32[128,1024]{1,0:T(8,128)S(1)}) custom-call(s32[16]{0:T(128)S(1)} %pad_add_fusion.2.refs_0_, s32[2,128]{1,0:T(2,128)S(1)} %copy-done.3, bf16[8,2,128,128]{3,2,1,0:T(8,128)(2,1)S(1)} %collective-permute-done.4.refs_2_, ...), custom_call_target="tpu_custom_call" | custom-call | flops 1073741824 | bytes 2621440 | tf_op jit(solution)/shard_map/pallas_call | solution.py:157
  111.3 3.6 %shard_map.75 = (bf16[1024,128]{1,0:T(8,128)(2,1)S(1)}, f32[1,1024]{1,0:T(1,128)S(1)}, f32[8,1024]{1,0:T(8,128)S(1)}, f32[128,1024]{1,0:T(8,128)S(1)}) custom-call(s32[16]{0:T(128)S(1)} %pad_add_fusion.1.refs_0_, s32[2,128]{1,0:T(2,128)S(1)} %copy-done.3, bf16[8,2,128,128]{3,2,1,0:T(8,128)(2,1)S(1)} %collective-permute-done.5.refs_2_, ...), custom_call_target="tpu_custom_call" | custom-call | flops 1073741824 | bytes 2621440 | tf_op jit(solution)/shard_map/pallas_call | solution.py:157
  115.0 3.6 %shard_map.76 = (bf16[1024,128]{1,0:T(8,128)(2,1)S(1)}, f32[1,1024]{1,0:T(1,128)S(1)}, f32[8,1024]{1,0:T(8,128)S(1)}, f32[128,1024]{1,0:T(8,128)S(1)}) custom-call(s32[16]{0:T(128)S(1)} %pad_add_fusion.refs_0_, s32[2,128]{1,0:T(2,128)S(1)} %copy-done.3, bf16[8,2,128,128]{3,2,1,0:T(8,128)(2,1)S(1)} %collective-permute-done.6.refs_2_, ...), custom_call_target="tpu_custom_call" | custom-call | flops 1073741824 | bytes 2621440 | tf_op jit(solution)/shard_map/pallas_call | solution.py:157
  118.6 2.3 %shard_map.77 = bf16[128,1024]{1,0:T(8,128)(2,1)S(1)} custom-call(s32[8]{0:T(128)S(1)} %get-tuple-element.46.refs_0_, s32[2,128]{1,0:T(2,128)S(1)} %copy-done.3, bf16[8,2,128,128]{3,2,1,0:T(8,128)(2,1)S(1)} %collective-permute-done.7.refs_2_, bf16[1024,128]{1,0:T(8,128)(2,1)S(1)} %get-tuple-element.33.refs_3_, f32[1,1024]{1,0:T(1,128)S(1)} %get-tuple-element.34.refs_4_, ...), custom_call_target="tpu_custom_call" | custom-call | flops 536870912 | bytes 2097152 | tf_op jit(solution)/shard_map/pallas_call | solution.py:157
  120.9 6.6 %collective-permute-start.11 = (bf16[128,1024]{1,0:T(8,128)(2,1)S(1)}, bf16[128,1024]{1,0:T(8,128)(2,1)S(1)}, u32[]{:S(2)}, u32[]{:S(2)}) collective-permute-start(bf16[128,1024]{1,0:T(8,128)(2,1)S(1)} %shard_map.77), channel_id=1, source_target_pairs={{0,128},{128,256},{256,384},{384,0},{1,129},{129,257},{257,385},{3... | collective-permute-start | bytes 786440 | tf_op jit(solution)/shard_map/ppermute | solution.py:24
  127.4 1.9 collective-permute-start.12
  129.4 3.1 %collective-permute-start.13 = (bf16[128,1024]{1,0:T(8,128)(2,1)S(1)}, bf16[128,1024]{1,0:T(8,128)(2,1)S(1)}, u32[]{:S(2)}, u32[]{:S(2)}) collective-permute-start(bf16[128,1024]{1,0:T(8,128)(2,1)S(1)} %shard_map.77), channel_id=1, source_target_pairs={{0,256},{128,384},{256,0},{384,128},{1,257},{129,385},{257,1},{385... | collective-permute-start | bytes 786440 | tf_op jit(solution)/shard_map/ppermute | solution.py:24
  132.5 5.5 %collective-permute-done.12 = bf16[128,1024]{1,0:T(8,128)(2,1)S(1)} collective-permute-done((bf16[128,1024]{1,0:T(8,128)(2,1)S(1)}, bf16[128,1024]{1,0:T(8,128)(2,1)S(1)}, u32[]{:S(2)}, u32[]{:S(2)}) %collective-permute-start.12) | collective-permute-done | bytes 262176 | tf_op jit(solution)/shard_map/ppermute | solution.py:24
  138.0 1.2 collective-permute-done.13
  139.2 0.1 pad_maximum_fusion.a_ref
  139.3 1.6 copy-done
  140.9 0.7 shard_map.79
  141.6 8.0 %collective-permute-start.15 = (f32[4,128,512]{2,1,0:T(8,128)S(1)}, f32[4,128,512]{2,1,0:T(8,128)S(1)}, u32[]{:S(2)}, u32[]{:S(2)}) collective-permute-start(f32[4,128,512]{2,1,0:T(8,128)S(1)} %shard_map.79), channel_id=1, source_target_pairs={{0,1},{1,0},{2,3},{3,2},{4,5},{5,4},{6,7},{7,6},{8,9},{9,8},{10,11... | collective-permute-start | bytes 3145736 | tf_op jit(solution)/shard_map/ppermute | solution.py:24
  149.6 0.7 shard_map.78
  150.3 1.5 collective-permute-done.15
  151.8 1.0 add_convert_fusion
  152.8 7.4 %all-to-all-start.1 = ((bf16[4,128,512]{2,1,0:T(8,128)(2,1)}), bf16[4,128,512]{2,1,0:T(8,128)(2,1)S(1)}, u32[]{:S(2)}, u32[]{:S(2)}) async-start(bf16[4,128,512]{2,1,0:T(8,128)(2,1)} %add_convert_fusion), calls=%async_computation.1 | async-start | bytes 1048576 | tf_op jit(solution)/shard_map/all_to_all | solution.py:257
  160.9 13.4 %all-to-all-done.1 = bf16[4,128,512]{2,1,0:T(8,128)(2,1)S(1)} async-done(((bf16[4,128,512]{2,1,0:T(8,128)(2,1)}), bf16[4,128,512]{2,1,0:T(8,128)(2,1)S(1)}, u32[]{:S(2)}, u32[]{:S(2)}) %all-to-all-start.1) | async-done | bytes 524320 | tf_op jit(solution)/shard_map/all_to_all | solution.py:257
  174.4 3.0 %collective-permute-start.16 = (bf16[128,512]{1,0:T(8,128)(2,1)S(1)}, bf16[128,512]{1,0:T(8,128)(2,1)S(1)}, u32[]{:S(2)}, u32[]{:S(2)}) collective-permute-start(bf16[128,512]{1,0:T(8,128)(2,1)S(1)} %multiply_convert_fusion), channel_id=1, source_target_pairs={{0,0},{2,384},{4,128},{6,256},{128,130},{130,2},{132,258},{134,386... | collective-permute-start | bytes 393224 | tf_op jit(solution)/shard_map/ppermute | solution.py:263
  177.4 12.0 %collective-permute-done.16 = bf16[128,512]{1,0:T(8,128)(2,1)S(1)} collective-permute-done((bf16[128,512]{1,0:T(8,128)(2,1)S(1)}, bf16[128,512]{1,0:T(8,128)(2,1)S(1)}, u32[]{:S(2)}, u32[]{:S(2)}) %collective-permute-start.16) | collective-permute-done | bytes 131104 | tf_op jit(solution)/shard_map/ppermute | solution.py:263
  189.4 0.7 copy.16
  (34 shorter events, 0.4 us)
Async XLA Ops:
  6.5 18.9 %copy-start.6 = (bf16[128,128]{1,0:T(8,128)(2,1)S(1)}, bf16[128,128]{1,0:T(8,128)(2,1)}, u32[]{:S(2)}) copy-start(bf16[128,128]{1,0:T(8,128)(2,1)} %param.8) | copy-start | bytes 98308
  6.5 18.9 %copy-start.5 = (bf16[128,128]{1,0:T(8,128)(2,1)S(1)}, bf16[128,128]{1,0:T(8,128)(2,1)}, u32[]{:S(2)}) copy-start(bf16[128,128]{1,0:T(8,128)(2,1)} %param.9) | copy-start | bytes 98308
  6.5 98.8 %copy-start.4 = (f32[128]{0:T(128)S(1)}, f32[128]{0:T(128)}, u32[]{:S(2)}) copy-start(f32[128]{0:T(128)} %param.10) | copy-start | bytes 1540
  6.5 98.8 %copy-start.3 = (s32[2,128]{1,0:T(2,128)S(1)}, s32[2,128]{1,0:T(2,128)}, u32[]{:S(2)}) copy-start(s32[2,128]{1,0:T(2,128)} %refs_1_.9) | copy-start | bytes 3076
  6.5 98.8 %copy-start.2 = (bf16[128,1024]{1,0:T(8,128)(2,1)S(1)}, bf16[128,1024]{1,0:T(8,128)(2,1)}, u32[]{:S(2)}) copy-start(bf16[128,1024]{1,0:T(8,128)(2,1)} %refs_3_.1) | copy-start | bytes 786436
  6.5 132.7 %all-gather.2.cloned.1.call-start = ((), (), s32[]{:S(2)}) async-start(), calls=%async_computation.2 | async-start | bytes 2359296 | tf_op jit(solution)/shard_map/all_gather | solution.py:217
  14.8 9.9 %collective-permute-start.14 = (bf16[64,1024]{1,0:T(8,128)(2,1)S(1)}, bf16[64,1024]{1,0:T(8,128)(2,1)S(1)}, u32[]{:S(2)}, u32[]{:S(2)}) collective-permute-start(bf16[64,1024]{1,0:T(8,128)(2,1)S(1)} %bitcast.31), channel_id=1, source_target_pairs={{0,64},{64,0},{1,65},{65,1},{2,66},{66,2},{3,67},{67,3},{4,68},{68... | collective-permute-start | bytes 393224 | tf_op jit(solution)/shard_map/ppermute | solution.py:24
  25.5 12.9 %collective-permute-start = (bf16[1,2,128,128]{3,2,1,0:T(8,128)(2,1)S(1)}, bf16[1,2,128,128]{3,2,1,0:T(8,128)(2,1)S(1)}, u32[]{:S(2)}, u32[]{:S(2)}) collective-permute-start(bf16[1,2,128,128]{3,2,1,0:T(8,128)(2,1)S(1)} %maximum_bitcast_fusion), channel_id=1, source_target_pairs={{0,64},{64,0},{1,65},{65,1},{2,66},{66,2},{3,67},{67,3},{4,68},{68... | collective-permute-start | bytes 196616 | tf_op jit(solution)/shard_map/ppermute | solution.py:24
  38.3 9.0 %collective-permute-start.1 = (bf16[2,2,128,128]{3,2,1,0:T(8,128)(2,1)S(1)}, bf16[2,2,128,128]{3,2,1,0:T(8,128)(2,1)S(1)}, u32[]{:S(2)}, u32[]{:S(2)}) collective-permute-start(bf16[2,2,128,128]{3,2,1,0:T(8,128)(2,1)S(1)} %pad_maximum_fusion.2), channel_id=1, source_target_pairs={{0,128},{128,256},{256,384},{384,0},{1,129},{129,257},{257,385},{3... | collective-permute-start | bytes 393224 | tf_op jit(solution)/shard_map/ppermute | solution.py:24
  42.1 6.9 %collective-permute-start.2 = (bf16[2,2,128,128]{3,2,1,0:T(8,128)(2,1)S(1)}, bf16[2,2,128,128]{3,2,1,0:T(8,128)(2,1)S(1)}, u32[]{:S(2)}, u32[]{:S(2)}) collective-permute-start(bf16[2,2,128,128]{3,2,1,0:T(8,128)(2,1)S(1)} %pad_maximum_fusion.2), channel_id=1, source_target_pairs={{0,384},{128,0},{256,128},{384,256},{1,385},{129,1},{257,129},{385... | collective-permute-start | bytes 393224 | tf_op jit(solution)/shard_map/ppermute | solution.py:24
  44.0 7.2 %collective-permute-start.3 = (bf16[2,2,128,128]{3,2,1,0:T(8,128)(2,1)S(1)}, bf16[2,2,128,128]{3,2,1,0:T(8,128)(2,1)S(1)}, u32[]{:S(2)}, u32[]{:S(2)}) collective-permute-start(bf16[2,2,128,128]{3,2,1,0:T(8,128)(2,1)S(1)} %pad_maximum_fusion.2), channel_id=1, source_target_pairs={{0,256},{128,384},{256,0},{384,128},{1,257},{129,385},{257,1},{385... | collective-permute-start | bytes 393224 | tf_op jit(solution)/shard_map/ppermute | solution.py:24
  51.2 29.0 %collective-permute-start.4 = (bf16[8,2,128,128]{3,2,1,0:T(8,128)(2,1)S(1)}, bf16[8,2,128,128]{3,2,1,0:T(8,128)(2,1)S(1)}, u32[]{:S(2)}, u32[]{:S(2)}) collective-permute-start(bf16[8,2,128,128]{3,2,1,0:T(8,128)(2,1)S(1)} %constant_dynamic-update-slice_fusion.refs_2_), channel_id=1, source_target_pairs={{0,8},{8,16},{16,24},{24,32},{32,40},{40,48},{48,56},{56,0},{1,9},... | collective-permute-start | bytes 1572872 | tf_op jit(solution)/shard_map/ppermute | solution.py:24
  53.2 29.0 %collective-permute-start.8 = (bf16[8,2,128,128]{3,2,1,0:T(8,128)(2,1)S(1)}, bf16[8,2,128,128]{3,2,1,0:T(8,128)(2,1)S(1)}, u32[]{:S(2)}, u32[]{:S(2)}) collective-permute-start(bf16[8,2,128,128]{3,2,1,0:T(8,128)(2,1)S(1)} %constant_dynamic-update-slice_fusion.refs_2_), channel_id=1, source_target_pairs={{0,56},{8,0},{16,8},{24,16},{32,24},{40,32},{48,40},{56,48},{1,57}... | collective-permute-start | bytes 1572872 | tf_op jit(solution)/shard_map/ppermute | solution.py:24
  80.2 11.9 %collective-permute-start.5 = (bf16[8,2,128,128]{3,2,1,0:T(8,128)(2,1)S(1)}, bf16[8,2,128,128]{3,2,1,0:T(8,128)(2,1)S(1)}, u32[]{:S(2)}, u32[]{:S(2)}) collective-permute-start(bf16[8,2,128,128]{3,2,1,0:T(8,128)(2,1)S(1)} %collective-permute-done.4.refs_2_), channel_id=1, source_target_pairs={{0,8},{8,16},{16,24},{24,32},{32,40},{40,48},{48,56},{56,0},{1,9},... | collective-permute-start | bytes 1572872 | tf_op jit(solution)/shard_map/ppermute | solution.py:24
  82.1 12.2 %collective-permute-start.9 = (bf16[8,2,128,128]{3,2,1,0:T(8,128)(2,1)S(1)}, bf16[8,2,128,128]{3,2,1,0:T(8,128)(2,1)S(1)}, u32[]{:S(2)}, u32[]{:S(2)}) collective-permute-start(bf16[8,2,128,128]{3,2,1,0:T(8,128)(2,1)S(1)} %collective-permute-done.8.refs_3_), channel_id=1, source_target_pairs={{0,56},{8,0},{16,8},{24,16},{32,24},{40,32},{48,40},{56,48},{1,57}... | collective-permute-start | bytes 1572872 | tf_op jit(solution)/shard_map/ppermute | solution.py:24
  92.1 11.1 %collective-permute-start.6 = (bf16[8,2,128,128]{3,2,1,0:T(8,128)(2,1)S(1)}, bf16[8,2,128,128]{3,2,1,0:T(8,128)(2,1)S(1)}, u32[]{:S(2)}, u32[]{:S(2)}) collective-permute-start(bf16[8,2,128,128]{3,2,1,0:T(8,128)(2,1)S(1)} %collective-permute-done.5.refs_2_), channel_id=1, source_target_pairs={{0,8},{8,16},{16,24},{24,32},{32,40},{40,48},{48,56},{56,0},{1,9},... | collective-permute-start | bytes 1572872 | tf_op jit(solution)/shard_map/ppermute | solution.py:24
  94.3 20.6 %collective-permute-start.10 = (bf16[8,2,128,128]{3,2,1,0:T(8,128)(2,1)S(1)}, bf16[8,2,128,128]{3,2,1,0:T(8,128)(2,1)S(1)}, u32[]{:S(2)}, u32[]{:S(2)}) collective-permute-start(bf16[8,2,128,128]{3,2,1,0:T(8,128)(2,1)S(1)} %collective-permute-done.9.refs_3_), channel_id=1, source_target_pairs={{0,56},{8,0},{16,8},{24,16},{32,24},{40,32},{48,40},{56,48},{1,57}... | collective-permute-start | bytes 1572872 | tf_op jit(solution)/shard_map/ppermute | solution.py:24
  103.2 15.3 %collective-permute-start.7 = (bf16[8,2,128,128]{3,2,1,0:T(8,128)(2,1)S(1)}, bf16[8,2,128,128]{3,2,1,0:T(8,128)(2,1)S(1)}, u32[]{:S(2)}, u32[]{:S(2)}) collective-permute-start(bf16[8,2,128,128]{3,2,1,0:T(8,128)(2,1)S(1)} %collective-permute-done.6.refs_2_), channel_id=1, source_target_pairs={{0,8},{8,16},{16,24},{24,32},{32,40},{40,48},{48,56},{56,0},{1,9},... | collective-permute-start | bytes 1572872 | tf_op jit(solution)/shard_map/ppermute | solution.py:24
  120.9 11.6 %collective-permute-start.11 = (bf16[128,1024]{1,0:T(8,128)(2,1)S(1)}, bf16[128,1024]{1,0:T(8,128)(2,1)S(1)}, u32[]{:S(2)}, u32[]{:S(2)}) collective-permute-start(bf16[128,1024]{1,0:T(8,128)(2,1)S(1)} %shard_map.77), channel_id=1, source_target_pairs={{0,128},{128,256},{256,384},{384,0},{1,129},{129,257},{257,385},{3... | collective-permute-start | bytes 786440 | tf_op jit(solution)/shard_map/ppermute | solution.py:24
  127.4 10.5 %collective-permute-start.12 = (bf16[128,1024]{1,0:T(8,128)(2,1)S(1)}, bf16[128,1024]{1,0:T(8,128)(2,1)S(1)}, u32[]{:S(2)}, u32[]{:S(2)}) collective-permute-start(bf16[128,1024]{1,0:T(8,128)(2,1)S(1)} %shard_map.77), channel_id=1, source_target_pairs={{0,384},{128,0},{256,128},{384,256},{1,385},{129,1},{257,129},{385... | collective-permute-start | bytes 786440 | tf_op jit(solution)/shard_map/ppermute | solution.py:24
  129.4 9.8 %collective-permute-start.13 = (bf16[128,1024]{1,0:T(8,128)(2,1)S(1)}, bf16[128,1024]{1,0:T(8,128)(2,1)S(1)}, u32[]{:S(2)}, u32[]{:S(2)}) collective-permute-start(bf16[128,1024]{1,0:T(8,128)(2,1)S(1)} %shard_map.77), channel_id=1, source_target_pairs={{0,256},{128,384},{256,0},{384,128},{1,257},{129,385},{257,1},{385... | collective-permute-start | bytes 786440 | tf_op jit(solution)/shard_map/ppermute | solution.py:24
  139.3 1.6 copy-start
  140.9 8.7 %copy-start.1 = (bf16[1024,1024]{1,0:T(8,128)(2,1)S(1)}, bf16[1024,1024]{1,0:T(8,128)(2,1)}, u32[]{:S(2)}) copy-start(bf16[1024,1024]{1,0:T(8,128)(2,1)} %all-gather.2.cloned.1.call-done) | copy-start | bytes 6291460
  141.6 10.2 %collective-permute-start.15 = (f32[4,128,512]{2,1,0:T(8,128)S(1)}, f32[4,128,512]{2,1,0:T(8,128)S(1)}, u32[]{:S(2)}, u32[]{:S(2)}) collective-permute-start(f32[4,128,512]{2,1,0:T(8,128)S(1)} %shard_map.79), channel_id=1, source_target_pairs={{0,1},{1,0},{2,3},{3,2},{4,5},{5,4},{6,7},{7,6},{8,9},{9,8},{10,11... | collective-permute-start | bytes 3145736 | tf_op jit(solution)/shard_map/ppermute | solution.py:24
  152.8 21.5 %all-to-all-start.1 = ((bf16[4,128,512]{2,1,0:T(8,128)(2,1)}), bf16[4,128,512]{2,1,0:T(8,128)(2,1)S(1)}, u32[]{:S(2)}, u32[]{:S(2)}) async-start(bf16[4,128,512]{2,1,0:T(8,128)(2,1)} %add_convert_fusion), calls=%async_computation.1 | async-start | bytes 1048576 | tf_op jit(solution)/shard_map/all_to_all | solution.py:257
  174.4 15.0 %collective-permute-start.16 = (bf16[128,512]{1,0:T(8,128)(2,1)S(1)}, bf16[128,512]{1,0:T(8,128)(2,1)S(1)}, u32[]{:S(2)}, u32[]{:S(2)}) collective-permute-start(bf16[128,512]{1,0:T(8,128)(2,1)S(1)} %multiply_convert_fusion), channel_id=1, source_target_pairs={{0,0},{2,384},{4,128},{6,256},{128,130},{130,2},{132,258},{134,386... | collective-permute-start | bytes 393224 | tf_op jit(solution)/shard_map/ppermute | solution.py:263
Sparse Core Ops, SparseCore 0:
  25.6 56.6 all-gather.1
where the time goes:
time: 198 us; the launch traced here: 197 us
  starting transfers between devices  81.4 us (41%)
  waiting for transfers between devices  71.2 us (36%)
  Pallas kernels  16.9 us (9%)
  between operations  14.6 us (7%)
  blocking collectives  7.05 us (4%)
  local copies, waits for them, and re-layouts  3.51 us (2%)
  other arithmetic  2.17 us (1%)
    ppermute x16, starting transfers between devices, shift(): lax.ppermute(value, axis, [(s, (s + steps) % count) for s in range(count)])  71 us
    ppermute x16, waiting for transfers between devices, shift(): lax.ppermute(value, axis, [(s, (s + steps) % count) for s in range(count)])  45.8 us
    pallas_call x5, Pallas kernels, attend(): pl.pallas_call(body, out_shape=out_shape, in_specs=[pl.BlockSpec(memory_s...  15.5 us
    all_to_all x1, waiting for transfers between devices, work(): lax.all_to_all(partial, 'yl', split_axis=0, concat_axis=0, tiled=True)  13.4 us
    ppermute x1, waiting for transfers between devices, work(): return lax.ppermute(result, ('x', 'yl'), pairs)  12 us
    all_to_all x1, starting transfers between devices, work(): lax.all_to_all(partial, 'yl', split_axis=0, concat_axis=0, tiled=True)  7.43 us
    all_to_all x1, blocking collectives, work(): lax.all_to_all(quarter.reshape(64, 1024), 'x', split_axis=0, concat_axis=...  7.05 us
  transfers between devices with their start and end apart: 19, of which 12 were waited for; matrix products, arithmetic and copies ran while one was open for 0% of the time, Pallas kernels for 8%

commit v1 on v0

v1 whole, which is shorter than its diff:
```python
import math

import jax
import jax.numpy as jnp
from jax import lax
from jax.experimental import pallas as pl
from jax.experimental.pallas import tpu as pltpu
from jax.sharding import Mesh, PartitionSpec as P


D = 128
HEADS = 8
TOK = 128
ROWS = HEADS * TOK
BLOCKS = 4
WIDE = 256
PACK = TOK + 16
LOW = -1e30
EXP2_SCALE = math.log2(math.e) / math.sqrt(D)
VMEM = pl.BlockSpec(memory_space=pltpu.VMEM)
SMEM = pl.BlockSpec(memory_space=pltpu.SMEM)
FRAMES = ("x", "yh", "z")


def shift(value, axis, steps):
    count = lax.axis_size(axis)
    return lax.ppermute(value, axis, [(s, (s + steps) % count) for s in range(count)])


def attention_kernel(n_chunks, first, half, ids_ref, *refs):
    refs = list(refs)
    packs = [refs.pop(0) for _ in range(2)]
    chunks = [refs.pop(0) for _ in range(n_chunks)]
    if first:
        gain_ref = refs.pop(0)
    else:
        nq_ref, m_in, l_in, acc_in = [refs.pop(0) for _ in range(4)]
    if half is not None:
        out_ref = refs.pop(0)
    elif first:
        nq_ref, m_out, l_out, acc_out = [refs.pop(0) for _ in range(4)]
    else:
        m_out, l_out, acc_out = [refs.pop(0) for _ in range(3)]
    if first:
        for b, pack in enumerate(packs):
            for h in range(HEADS):
                x = pack[0:TOK, h * D : (h + 1) * D].astype(jnp.float32)
                mean = jnp.mean(x * x, axis=-1, keepdims=True)
                x = x * lax.rsqrt(mean + 1e-05) * gain_ref[...]
                at = b * ROWS + h * TOK
                nq_ref[at : at + TOK, :] = x.astype(jnp.bfloat16)
    limits = []
    for pack in packs:
        rows = pack[TOK:PACK, 0:TOK].astype(jnp.float32)
        rows = jnp.concatenate([rows] * (WIDE // TOK), axis=1)
        limits.append((rows[0:1], rows[1:2]))
    per = ROWS // WIDE
    ws = range(2 * per) if half is None else range(half * per, (half + 1) * per)
    cols = {w: slice(w * WIDE, (w + 1) * WIDE) for w in ws}
    if first:
        state = {
            w: (
                jnp.full((1, WIDE), LOW, jnp.float32),
                jnp.zeros((8, WIDE), jnp.float32),
                jnp.zeros((D, WIDE), jnp.float32),
            )
            for w in ws
        }
    else:
        state = {w: (m_in[:, cols[w]], l_in[:, cols[w]], acc_in[:, cols[w]]) for w in ws}
    units = [(c, w) for c in range(n_chunks) for w in ws]

    def score(unit):
        c, w = unit
        k = chunks[c][:, 0].reshape(BLOCKS * D, D)
        return lax.dot_general(
            k,
            nq_ref[cols[w], :],
            (((1,), (1,)), ((), ())),
            preferred_element_type=jnp.float32,
        )

    def soften(unit, s, m, l):
        c, w = unit
        lower, upper = limits[w // per]
        allowed = []
        new = m
        for j in range(BLOCKS):
            block = ids_ref[c * BLOCKS + j].astype(jnp.float32)
            ok = (lower <= block) & (block < upper)
            top = jnp.max(s[j * D : (j + 1) * D], axis=0, keepdims=True)
            new = jnp.maximum(new, jnp.where(ok, top, LOW))
            allowed.append(ok)
        factor = jnp.exp2((m - new) * EXP2_SCALE)
        l = l * factor
        parts = []
        for j in range(BLOCKS):
            base = jnp.where(allowed[j], new * EXP2_SCALE, -LOW)
            p = jnp.exp2(s[j * D : (j + 1) * D] * EXP2_SCALE - base)
            l = l + jnp.sum(p.reshape(D // 8, 8, WIDE), axis=0)
            parts.append(p.astype(jnp.bfloat16))
        return jnp.concatenate(parts, axis=0), new, l, factor

    def collect(unit, p, acc, factor):
        c, _ = unit
        v = chunks[c][:, 1].reshape(BLOCKS * D, D)
        return acc * factor + lax.dot_general(
            v, p, (((0,), (0,)), ((), ())), preferred_element_type=jnp.float32
        )

    ahead = score(units[0])
    pending = None
    for at, unit in enumerate(units):
        s = ahead
        if at + 1 < len(units):
            ahead = score(units[at + 1])
        w = unit[1]
        m, l, acc = state[w]
        p, m, l, factor = soften(unit, s, m, l)
        if pending is not None:
            u, p0, f0 = pending
            m0, l0, acc0 = state[u[1]]
            state[u[1]] = (m0, l0, collect(u, p0, acc0, f0))
        state[w] = (m, l, state[w][2])
        pending = (unit, p, factor)
    u, p0, f0 = pending
    m0, l0, acc0 = state[u[1]]
    state[u[1]] = (m0, l0, collect(u, p0, acc0, f0))

    for w in ws:
        m, l, acc = state[w]
        if half is not None:
            at = slice((w % per) * WIDE, (w % per + 1) * WIDE)
            out_ref[0:D, at] = acc
            out_ref[D : D + 8, at] = l
            out_ref[D + 8 : D + 16, at] = jnp.broadcast_to(m, (8, WIDE))
        else:
            m_out[:, cols[w]] = m
            l_out[:, cols[w]] = l
            acc_out[:, cols[w]] = acc


def attend(ids, packs, chunks, gain, state, half=None):
    first = state is None
    sums = (
        jax.ShapeDtypeStruct((1, 2 * ROWS), jnp.float32),
        jax.ShapeDtypeStruct((8, 2 * ROWS), jnp.float32),
        jax.ShapeDtypeStruct((D, 2 * ROWS), jnp.float32),
    )
    if half is not None:
        out_shape = jax.ShapeDtypeStruct((D + 16, ROWS), jnp.float32)
    elif first:
        out_shape = (jax.ShapeDtypeStruct((2 * ROWS, D), jnp.bfloat16),) + sums
    else:
        out_shape = sums
    extra = (gain,) if first else state
    n_keys = len(chunks) * BLOCKS * D
    rows = 2 * ROWS if half is None else ROWS

    def body(*refs):
        attention_kernel(len(chunks), first, half, *refs)

    out = pl.pallas_call(
        body,
        out_shape=out_shape,
        in_specs=[SMEM] + [VMEM] * (2 + len(chunks) + len(extra)),
        out_specs=VMEM if half is not None else (VMEM,) * len(out_shape),
        cost_estimate=pl.CostEstimate(
            flops=4 * rows * n_keys * D,
            bytes_accessed=n_keys * D * 4 + rows * D * 12,
            transcendentals=rows * n_keys,
        ),
        compiler_params=pltpu.CompilerParams(vmem_limit_bytes=40 << 20),
    )(ids, *packs, *chunks, *extra)
    if half is not None or first:
        return out
    return (state[0],) + tuple(out)


def merge_kernel(a_ref, b_ref, out_ref):
    a, b = a_ref[...], b_ref[...]
    top = jnp.maximum(a[D + 8 : D + 9], b[D + 8 : D + 9])
    fa = jnp.exp2((a[D + 8 : D + 9] - top) * EXP2_SCALE)
    fb = jnp.exp2((b[D + 8 : D + 9] - top) * EXP2_SCALE)
    total = jnp.sum(a[D : D + 8], axis=0, keepdims=True) * fa
    total = total + jnp.sum(b[D : D + 8], axis=0, keepdims=True) * fb
    o = (a[0:D] * fa + b[0:D] * fb) / total
    for h in range(HEADS):
        at = slice(h * TOK, (h + 1) * TOK)
        out_ref[:, at] = o[:, at].T.astype(jnp.bfloat16)


def merge(a, b):
    return pl.pallas_call(
        merge_kernel,
        out_shape=jax.ShapeDtypeStruct((TOK, ROWS), jnp.bfloat16),
        in_specs=[VMEM, VMEM],
        out_specs=VMEM,
        cost_estimate=pl.CostEstimate(
            flops=6 * ROWS * D, bytes_accessed=ROWS * D * 10, transcendentals=0
        ),
        compiler_params=pltpu.CompilerParams(vmem_limit_bytes=32 << 20),
    )(a, b)


def project_kernel(col_ref, core_ref, a0, a1, a2, a3, w_ref, out_ref):
    total = None
    a = jnp.concatenate([a0[...], a1[...], a2[...], a3[...]], axis=0)
    for x in range(4):
        w = jnp.concatenate([w_ref[:, 0, x], w_ref[:, 1, x]]).reshape(256, 512)
        part = jnp.dot(
            a[:, x * 256 : (x + 1) * 256], w, preferred_element_type=jnp.float32
        )
        total = part if total is None else total + part
    for k in range(4):
        out_ref[(core_ref[0] + k) % 4] = total[k * TOK : (k + 1) * TOK]


def project(column, core, slots, weight):
    return pl.pallas_call(
        project_kernel,
        grid_spec=pltpu.PrefetchScalarGridSpec(
            num_scalar_prefetch=2,
            grid=(1,),
            in_specs=[pl.BlockSpec((TOK, ROWS), lambda i, col, core: (0, 0))] * 4
            + [
                pl.BlockSpec(
                    (8, 2, 4, 16, 512), lambda i, col, core: (0, 0, 0, 0, col[0])
                ),
            ],
            out_specs=pl.BlockSpec((4, TOK, 512), lambda i, col, core: (0, 0, 0)),
        ),
        out_shape=jax.ShapeDtypeStruct((4, TOK, 512), jnp.float32),
        cost_estimate=pl.CostEstimate(
            flops=512 * 1024 * 1024, bytes_accessed=3 << 20, transcendentals=0
        ),
        compiler_params=pltpu.CompilerParams(vmem_limit_bytes=32 << 20),
    )(column, core, *slots, weight)


def work(queries, keys, values, q_gain, frame_bounds, output_weight, attn_gate):
    ax, ay, az = lax.axis_index("x"), lax.axis_index("yh"), lax.axis_index("z")
    core = lax.axis_index("c")

    def trade(value, di=0, dy=0):
        pairs = []
        for i in range(2):
            for y in range(2):
                for a in range(2):
                    for c in range(2):
                        source = ((2 * i + a) * 2 + y) * 2 + c
                        x = 2 * ((i + di) % 2) + c
                        pairs.append((source, (x * 2 + (y + dy) % 2) * 2 + a))
        return lax.ppermute(value, ("x", "yh", "c"), pairs)

    own = jnp.stack([keys, values])[None]
    chunk = jnp.concatenate(
        [trade(own), trade(own, di=1), trade(own, dy=1), trade(own, di=1, dy=1)]
    )
    block_x = 2 * (ax // 2) + core
    in_chunk = jnp.stack(
        [
            ((block_x + 2 * di) % 4) * 16 + ((ay + dy) % 2) * 8
            for dy in (0, 1)
            for di in (0, 1)
        ]
    ).astype(jnp.int32)
    hops = [0, -1, 1, -2, 2, -3, 3, -4]
    ids = [in_chunk + (az + h) % 8 for h in hops]

    bounds = jnp.pad(frame_bounds.astype(jnp.bfloat16), ((0, 14), (0, ROWS - TOK)))
    near = trade(jnp.concatenate([queries, bounds]))
    far = shift(near, "c", 1)
    packs = (near, far)

    quarter = output_weight[0].reshape(16, 4, 1024).transpose(1, 0, 2)
    quarter = lax.all_to_all(
        quarter.reshape(64, 1024), "x", split_axis=0, concat_axis=0, tiled=True
    )
    partner = shift(quarter, "yh", 1)
    both = jnp.stack(
        [jnp.where(ay == 0, quarter, partner), jnp.where(ay == 0, partner, quarter)]
    )
    weight = lax.all_gather(both.reshape(128, 1024), "z", axis=0, tiled=True)
    weight = weight.reshape(8, 2, 4, 16, 1024)

    right, left = [chunk], [chunk]
    for s in range(1, 5):
        right.append(shift(right[-1], "z", 1))
        if s < 4:
            left.append(shift(left[-1], "z", -1))
    gain = q_gain[None, :]
    state = attend(ids[0], packs, [chunk], gain, None)
    for s in range(1, 4):
        state = attend(
            jnp.concatenate(ids[2 * s - 1 : 2 * s + 1]),
            packs,
            [right[s], left[s]],
            gain,
            state,
        )
    send = attend(ids[7], packs, [right[4]], gain, state, half=1)
    received = shift(send, "c", 1)
    keep = attend(ids[7], packs, [right[4]], gain, state, half=0)
    attended = merge(keep, received)

    slots = []
    for k in range(4):
        pairs = [
            (x * 2 + c, ((x + k + c) % 4) * 2 + x % 2) for x in range(4) for c in range(2)
        ]
        slots.append(lax.ppermute(attended, ("x", "c"), pairs))
    core = core.astype(jnp.int32)[None]
    for_other = project(1 - core, core, slots, weight)
    from_other = shift(for_other, "c", 1)
    for_own = project(core, core, slots, weight)
    partial = (for_own + from_other).astype(jnp.bfloat16).reshape(512, 512)
    pieces = lax.all_to_all(partial, "yl", split_axis=0, concat_axis=0, tiled=True)
    combined = jnp.sum(pieces.reshape(4, TOK, 512).astype(jnp.float32), axis=0)
    result = (jnp.tanh(attn_gate[0]) * combined).astype(jnp.bfloat16)
    pairs = [(x * 4 + y, ((x - y) % 4) * 4 + x) for x in range(4) for y in range(4)]
    return lax.ppermute(result, ("x", "yl"), pairs)


def solution(mesh):
    fine = Mesh(mesh.devices.reshape(4, 2, 8, 4, 2), ("x", "yh", "z", "yl", "c"))
    group = ("yl", "c")
    placed = (
        P(FRAMES, group),
        P(FRAMES, group),
        P(FRAMES, group),
        P(),
        P(None, FRAMES),
        P(group, FRAMES, None),
        P(),
    )
    return jax.shard_map(
        work, mesh=fine, in_specs=placed, out_specs=P(FRAMES, group), check_vma=False
    )
```

time: 198 us -> 188 us (0.949)
  the two profiles are of different devices: /device:TPU:7 before, /device:TPU:6 now
where the time goes in v1:
time: 188 us; the launch traced here: 187 us
  starting transfers between devices  80.5 us (43%)
  waiting for transfers between devices  56.4 us (30%)
  Pallas kernels  18.1 us (10%)
  between operations  14.7 us (8%)
  blocking collectives  12.1 us (6%)
  local copies, waits for them, and re-layouts  3.4 us (2%)
  other arithmetic  2.14 us (1%)
    ppermute x11, starting transfers between devices, shift(): lax.ppermute(value, axis, [(s, (s + steps) % count) for s in range(count)])  39.1 us
    ppermute x5, starting transfers between devices, trade(): return lax.ppermute(value, ('x', 'yh', 'c'), pairs)  19.6 us
    ppermute x11, waiting for transfers between devices, shift(): lax.ppermute(value, axis, [(s, (s + steps) % count) for s in range(count)])  18 us
    pallas_call x6, Pallas kernels, attend(): pl.pallas_call(body, out_shape=out_shape, in_specs=[SMEM] + [VMEM] * (2 +...  16.5 us
    ppermute x4, starting transfers between devices, work(): slots.append(lax.ppermute(attended, ('x', 'c'), pairs))  14.9 us
    all_to_all x1, waiting for transfers between devices, work(): lax.all_to_all(partial, 'yl', split_axis=0, concat_axis=0, tiled=True)  14.3 us
    all_to_all x1, blocking collectives, work(): lax.all_to_all(quarter.reshape(64, 1024), 'x', split_axis=0, concat_axis=...  12.1 us
    ppermute x1, waiting for transfers between devices, work(): return lax.ppermute(result, ('x', 'yl'), pairs)  10.9 us
  transfers between devices with their start and end apart: 23, of which 12 were waited for; matrix products, arithmetic and copies ran while one was open for 0% of the time, Pallas kernels for 9%

profile of v1, /device:TPU:6, one launch (start us, length us, event | category | flops | bytes accessed | tf_op | source)
XLA Modules:
  0.0 187.4 jit_solution(13470436412018281855)
XLA Ops:
  6.6 1.0 reshape_squeeze.3
  7.7 12.1 %all_to_all.15 = bf16[4,16,1024]{2,1,0:T(8,128)(2,1)S(1)} all-to-all(bf16[4,16,1024]{2,1,0:T(8,128)(2,1)S(1)} %copy.9), channel_id=1, replica_groups=mesh['x'=4,'yh'=2,'z'=8,'yl'=4,'c'=2] {'x'}, dimensions={0} | all-to-all | bytes 262144 | tf_op jit(solution)/shard_map/all_to_all | solution.py:277
  19.8 4.1 %collective-permute-start.18 = (bf16[64,1024]{1,0:T(8,128)(2,1)S(1)}, bf16[64,1024]{1,0:T(8,128)(2,1)S(1)}, u32[]{:S(2)}, u32[]{:S(2)}) collective-permute-start(bf16[64,1024]{1,0:T(8,128)(2,1)S(1)} %bitcast.25), channel_id=1, source_target_pairs={{0,64},{64,0},{1,65},{65,1},{2,66},{66,2},{3,67},{67,3},{4,68},{68... | collective-permute-start | bytes 393224 | tf_op jit(solution)/shard_map/ppermute | solution.py:27
  23.9 8.1 %collective-permute-done.18 = bf16[64,1024]{1,0:T(8,128)(2,1)S(1)} collective-permute-done((bf16[64,1024]{1,0:T(8,128)(2,1)S(1)}, bf16[64,1024]{1,0:T(8,128)(2,1)S(1)}, u32[]{:S(2)}, u32[]{:S(2)}) %collective-permute-start.18) | collective-permute-done | bytes 131104 | tf_op jit(solution)/shard_map/ppermute | solution.py:27
  32.0 0.7 pad_maximum_fusion
  32.8 1.9 %collective-permute-start.2 = (bf16[1,2,128,128]{3,2,1,0:T(8,128)(2,1)S(1)}, bf16[1,2,128,128]{3,2,1,0:T(8,128)(2,1)S(1)}, u32[]{:S(2)}, u32[]{:S(2)}) collective-permute-start(bf16[1,2,128,128]{3,2,1,0:T(8,128)(2,1)S(1)} %maximum_bitcast_fusion), channel_id=1, source_target_pairs={{0,0},{1,128},{128,1},{129,129},{64,64},{65,192},{192,65},{193,193... | collective-permute-start | bytes 196616 | tf_op jit(solution)/shard_map/ppermute | solution.py:254
  34.7 4.3 %collective-permute-start.3 = (bf16[1,2,128,128]{3,2,1,0:T(8,128)(2,1)S(1)}, bf16[1,2,128,128]{3,2,1,0:T(8,128)(2,1)S(1)}, u32[]{:S(2)}, u32[]{:S(2)}) collective-permute-start(bf16[1,2,128,128]{3,2,1,0:T(8,128)(2,1)S(1)} %maximum_bitcast_fusion), channel_id=1, source_target_pairs={{0,256},{1,384},{128,257},{129,385},{64,320},{65,448},{192,321},{1... | collective-permute-start | bytes 196616 | tf_op jit(solution)/shard_map/ppermute | solution.py:254
  39.0 3.2 %collective-permute-start.4 = (bf16[1,2,128,128]{3,2,1,0:T(8,128)(2,1)S(1)}, bf16[1,2,128,128]{3,2,1,0:T(8,128)(2,1)S(1)}, u32[]{:S(2)}, u32[]{:S(2)}) collective-permute-start(bf16[1,2,128,128]{3,2,1,0:T(8,128)(2,1)S(1)} %maximum_bitcast_fusion), channel_id=1, source_target_pairs={{0,64},{1,192},{128,65},{129,193},{64,0},{65,128},{192,1},{193,129... | collective-permute-start | bytes 196616 | tf_op jit(solution)/shard_map/ppermute | solution.py:254
  42.1 7.2 %collective-permute-start.5 = (bf16[1,2,128,128]{3,2,1,0:T(8,128)(2,1)S(1)}, bf16[1,2,128,128]{3,2,1,0:T(8,128)(2,1)S(1)}, u32[]{:S(2)}, u32[]{:S(2)}) collective-permute-start(bf16[1,2,128,128]{3,2,1,0:T(8,128)(2,1)S(1)} %maximum_bitcast_fusion), channel_id=1, source_target_pairs={{0,320},{1,448},{128,321},{129,449},{64,256},{65,384},{192,257},{1... | collective-permute-start | bytes 196616 | tf_op jit(solution)/shard_map/ppermute | solution.py:254
  49.4 4.5 %collective-permute-done.5 = bf16[1,2,128,128]{3,2,1,0:T(8,128)(2,1)S(1)} collective-permute-done((bf16[1,2,128,128]{3,2,1,0:T(8,128)(2,1)S(1)}, bf16[1,2,128,128]{3,2,1,0:T(8,128)(2,1)S(1)}, u32[]{:S(2)}, u32[]{:S(2)}) %collective-permute-start.5) | collective-permute-done | bytes 65568 | tf_op jit(solution)/shard_map/ppermute | solution.py:254
  54.0 4.5 %collective-permute-start.6 = (bf16[4,2,128,128]{3,2,1,0:T(8,128)(2,1)S(1)}, bf16[4,2,128,128]{3,2,1,0:T(8,128)(2,1)S(1)}, u32[]{:S(2)}, u32[]{:S(2)}) collective-permute-start(bf16[4,2,128,128]{3,2,1,0:T(8,128)(2,1)S(1)} %constant_dynamic-update-slice_fusion.refs_3_), channel_id=1, source_target_pairs={{0,8},{8,16},{16,24},{24,32},{32,40},{40,48},{48,56},{56,0},{1,9},... | collective-permute-start | bytes 786440 | tf_op jit(solution)/shard_map/ppermute | solution.py:27
  58.5 8.6 %collective-permute-start.10 = (bf16[4,2,128,128]{3,2,1,0:T(8,128)(2,1)S(1)}, bf16[4,2,128,128]{3,2,1,0:T(8,128)(2,1)S(1)}, u32[]{:S(2)}, u32[]{:S(2)}) collective-permute-start(bf16[4,2,128,128]{3,2,1,0:T(8,128)(2,1)S(1)} %constant_dynamic-update-slice_fusion.refs_3_), channel_id=1, source_target_pairs={{0,56},{8,0},{16,8},{24,16},{32,24},{40,32},{48,40},{56,48},{1,57}... | collective-permute-start | bytes 786440 | tf_op jit(solution)/shard_map/ppermute | solution.py:27
  67.1 3.1 %collective-permute-start = (bf16[144,1024]{1,0:T(8,128)(2,1)S(1)}, bf16[144,1024]{1,0:T(8,128)(2,1)S(1)}, u32[]{:S(2)}, u32[]{:S(2)}) collective-permute-start(bf16[144,1024]{1,0:T(8,128)(2,1)S(1)} %fusion.1), channel_id=1, source_target_pairs={{0,0},{1,128},{128,1},{129,129},{64,64},{65,192},{192,65},{193,193... | collective-permute-start | bytes 884744 | tf_op jit(solution)/shard_map/ppermute | solution.py:254
  70.5 5.5 %collective-permute-done.6.refs_3_ = bf16[4,2,128,128]{3,2,1,0:T(8,128)(2,1)S(1)} collective-permute-done((bf16[4,2,128,128]{3,2,1,0:T(8,128)(2,1)S(1)}, bf16[4,2,128,128]{3,2,1,0:T(8,128)(2,1)S(1)}, u32[]{:S(2)}, u32[]{:S(2)}) %collective-permute-start.6) | collective-permute-done | bytes 262176 | tf_op jit(solution)/shard_map/ppermute | solution.py:27
  76.0 1.9 %collective-permute-start.7 = (bf16[4,2,128,128]{3,2,1,0:T(8,128)(2,1)S(1)}, bf16[4,2,128,128]{3,2,1,0:T(8,128)(2,1)S(1)}, u32[]{:S(2)}, u32[]{:S(2)}) collective-permute-start(bf16[4,2,128,128]{3,2,1,0:T(8,128)(2,1)S(1)} %collective-permute-done.6.refs_3_), channel_id=1, source_target_pairs={{0,8},{8,16},{16,24},{24,32},{32,40},{40,48},{48,56},{56,0},{1,9},... | collective-permute-start | bytes 786440 | tf_op jit(solution)/shard_map/ppermute | solution.py:27
  77.9 5.1 %collective-permute-start.11 = (bf16[4,2,128,128]{3,2,1,0:T(8,128)(2,1)S(1)}, bf16[4,2,128,128]{3,2,1,0:T(8,128)(2,1)S(1)}, u32[]{:S(2)}, u32[]{:S(2)}) collective-permute-start(bf16[4,2,128,128]{3,2,1,0:T(8,128)(2,1)S(1)} %collective-permute-done.10.refs_4_), channel_id=1, source_target_pairs={{0,56},{8,0},{16,8},{24,16},{32,24},{40,32},{48,40},{56,48},{1,57}... | collective-permute-start | bytes 786440 | tf_op jit(solution)/shard_map/ppermute | solution.py:27
  83.1 1.9 %collective-permute-start.1 = (bf16[144,1024]{1,0:T(8,128)(2,1)S(1)}, bf16[144,1024]{1,0:T(8,128)(2,1)S(1)}, u32[]{:S(2)}, u32[]{:S(2)}) collective-permute-start(bf16[144,1024]{1,0:T(8,128)(2,1)S(1)} %collective-permute-done.refs_1_), channel_id=1, source_target_pairs={{0,1},{1,0},{2,3},{3,2},{4,5},{5,4},{6,7},{7,6},{8,9},{9,8},{10,11... | collective-permute-start | bytes 884744 | tf_op jit(solution)/shard_map/ppermute | solution.py:27
  85.1 0.4 collective-permute-done.7.refs_3_
  85.4 1.9 %collective-permute-start.8 = (bf16[4,2,128,128]{3,2,1,0:T(8,128)(2,1)S(1)}, bf16[4,2,128,128]{3,2,1,0:T(8,128)(2,1)S(1)}, u32[]{:S(2)}, u32[]{:S(2)}) collective-permute-start(bf16[4,2,128,128]{3,2,1,0:T(8,128)(2,1)S(1)} %collective-permute-done.7.refs_3_), channel_id=1, source_target_pairs={{0,8},{8,16},{16,24},{24,32},{32,40},{40,48},{48,56},{56,0},{1,9},... | collective-permute-start | bytes 786440 | tf_op jit(solution)/shard_map/ppermute | solution.py:27
  87.4 5.1 %collective-permute-start.12 = (bf16[4,2,128,128]{3,2,1,0:T(8,128)(2,1)S(1)}, bf16[4,2,128,128]{3,2,1,0:T(8,128)(2,1)S(1)}, u32[]{:S(2)}, u32[]{:S(2)}) collective-permute-start(bf16[4,2,128,128]{3,2,1,0:T(8,128)(2,1)S(1)} %collective-permute-done.11.refs_4_), channel_id=1, source_target_pairs={{0,56},{8,0},{16,8},{24,16},{32,24},{40,32},{48,40},{56,48},{1,57}... | collective-permute-start | bytes 786440 | tf_op jit(solution)/shard_map/ppermute | solution.py:27
  92.6 2.4 %shard_map.73 = (bf16[2048,128]{1,0:T(8,128)(2,1)S(1)}, f32[1,2048]{1,0:T(1,128)S(1)}, f32[8,2048]{1,0:T(8,128)S(1)}, f32[128,2048]{1,0:T(8,128)S(1)}) custom-call(s32[4]{0:T(128)S(1)} %get-tuple-element.40.refs_0_, bf16[144,1024]{1,0:T(8,128)(2,1)S(1)} %collective-permute-done.refs_1_, bf16[144,1024]{1,0:T(8,128)(2,1)S(1)} %collective-permute-done.1.refs_2_, ...), custom_call_target="tpu_custom_call" | custom-call | flops 536870912 | bytes 3407872 | tf_op jit(solution)/shard_map/pallas_call | solution.py:163
  95.1 1.8 collective-permute-done.8.refs_3_
  96.9 2.1 %collective-permute-start.9 = (bf16[4,2,128,128]{3,2,1,0:T(8,128)(2,1)S(1)}, bf16[4,2,128,128]{3,2,1,0:T(8,128)(2,1)S(1)}, u32[]{:S(2)}, u32[]{:S(2)}) collective-permute-start(bf16[4,2,128,128]{3,2,1,0:T(8,128)(2,1)S(1)} %collective-permute-done.8.refs_3_), channel_id=1, source_target_pairs={{0,8},{8,16},{16,24},{24,32},{32,40},{40,48},{48,56},{56,0},{1,9},... | collective-permute-start | bytes 786440 | tf_op jit(solution)/shard_map/ppermute | solution.py:27
  99.0 3.6 %shard_map.74 = (f32[1,2048]{1,0:T(1,128)S(1)}, f32[8,2048]{1,0:T(8,128)S(1)}, f32[128,2048]{1,0:T(8,128)S(1)}) custom-call(s32[8]{0:T(128)S(1)} %pad_add_fusion.3.refs_0_, bf16[144,1024]{1,0:T(8,128)(2,1)S(1)} %collective-permute-done.refs_1_, bf16[144,1024]{1,0:T(8,128)(2,1)S(1)} %collective-permute-done.1.refs_2_, ...), custom_call_target="tpu_custom_call" | custom-call | flops 1073741824 | bytes 3670016 | tf_op jit(solution)/shard_map/pallas_call | solution.py:163
  102.6 3.6 %shard_map.75 = (f32[1,2048]{1,0:T(1,128)S(1)}, f32[8,2048]{1,0:T(8,128)S(1)}, f32[128,2048]{1,0:T(8,128)S(1)}) custom-call(s32[8]{0:T(128)S(1)} %pad_add_fusion.2.refs_0_, bf16[144,1024]{1,0:T(8,128)(2,1)S(1)} %collective-permute-done.refs_1_, bf16[144,1024]{1,0:T(8,128)(2,1)S(1)} %collective-permute-done.1.refs_2_, ...), custom_call_target="tpu_custom_call" | custom-call | flops 1073741824 | bytes 3670016 | tf_op jit(solution)/shard_map/pallas_call | solution.py:163
  106.2 3.6 %shard_map.76 = (f32[1,2048]{1,0:T(1,128)S(1)}, f32[8,2048]{1,0:T(8,128)S(1)}, f32[128,2048]{1,0:T(8,128)S(1)}) custom-call(s32[8]{0:T(128)S(1)} %pad_add_fusion.1.refs_0_, bf16[144,1024]{1,0:T(8,128)(2,1)S(1)} %collective-permute-done.refs_1_, bf16[144,1024]{1,0:T(8,128)(2,1)S(1)} %collective-permute-done.1.refs_2_, ...), custom_call_target="tpu_custom_call" | custom-call | flops 1073741824 | bytes 3670016 | tf_op jit(solution)/shard_map/pallas_call | solution.py:163
  109.8 1.6 shard_map.78
  111.5 1.9 %collective-permute-start.13 = (f32[144,1024]{1,0:T(8,128)S(1)}, f32[144,1024]{1,0:T(8,128)S(1)}, u32[]{:S(2)}, u32[]{:S(2)}) collective-permute-start(f32[144,1024]{1,0:T(8,128)S(1)} %shard_map.78), channel_id=1, source_target_pairs={{0,1},{1,0},{2,3},{3,2},{4,5},{5,4},{6,7},{7,6},{8,9},{9,8},{10,11... | collective-permute-start | bytes 1769480 | tf_op jit(solution)/shard_map/ppermute | solution.py:27
  113.4 1.6 shard_map.77.a_ref
  115.0 0.3 collective-permute-done.13.b_ref
  115.6 2.1 %collective-permute-start.14 = (bf16[128,1024]{1,0:T(8,128)(2,1)S(1)}, bf16[128,1024]{1,0:T(8,128)(2,1)S(1)}, u32[]{:S(2)}, u32[]{:S(2)}) collective-permute-start(bf16[128,1024]{1,0:T(8,128)(2,1)S(1)} %shard_map.79), channel_id=1, source_target_pairs={{0,0},{1,128},{128,129},{129,257},{256,256},{257,384},{384,385},{3... | collective-permute-start | bytes 786440 | tf_op jit(solution)/shard_map/ppermute | solution.py:312
  117.7 6.0 %collective-permute-start.15 = (bf16[128,1024]{1,0:T(8,128)(2,1)S(1)}, bf16[128,1024]{1,0:T(8,128)(2,1)S(1)}, u32[]{:S(2)}, u32[]{:S(2)}) collective-permute-start(bf16[128,1024]{1,0:T(8,128)(2,1)S(1)} %shard_map.79), channel_id=1, source_target_pairs={{0,128},{1,256},{128,257},{129,385},{256,384},{257,0},{384,1},{385... | collective-permute-start | bytes 786440 | tf_op jit(solution)/shard_map/ppermute | solution.py:312
  123.7 4.9 %collective-permute-start.16 = (bf16[128,1024]{1,0:T(8,128)(2,1)S(1)}, bf16[128,1024]{1,0:T(8,128)(2,1)S(1)}, u32[]{:S(2)}, u32[]{:S(2)}) collective-permute-start(bf16[128,1024]{1,0:T(8,128)(2,1)S(1)} %shard_map.79), channel_id=1, source_target_pairs={{0,256},{1,384},{128,385},{129,1},{256,0},{257,128},{384,129},{385... | collective-permute-start | bytes 786440 | tf_op jit(solution)/shard_map/ppermute | solution.py:312
  128.6 1.9 %collective-permute-start.17 = (bf16[128,1024]{1,0:T(8,128)(2,1)S(1)}, bf16[128,1024]{1,0:T(8,128)(2,1)S(1)}, u32[]{:S(2)}, u32[]{:S(2)}) collective-permute-start(bf16[128,1024]{1,0:T(8,128)(2,1)S(1)} %shard_map.79), channel_id=1, source_target_pairs={{0,384},{1,0},{128,1},{129,129},{256,128},{257,256},{384,257},{385... | collective-permute-start | bytes 786440 | tf_op jit(solution)/shard_map/ppermute | solution.py:312
  130.5 3.0 %collective-permute-done.15.a1 = bf16[128,1024]{1,0:T(8,128)(2,1)S(1)} collective-permute-done((bf16[128,1024]{1,0:T(8,128)(2,1)S(1)}, bf16[128,1024]{1,0:T(8,128)(2,1)S(1)}, u32[]{:S(2)}, u32[]{:S(2)}) %collective-permute-start.15) | collective-permute-done | bytes 262176 | tf_op jit(solution)/shard_map/ppermute | solution.py:312
  133.5 2.8 %collective-permute-done.16.a2 = bf16[128,1024]{1,0:T(8,128)(2,1)S(1)} collective-permute-done((bf16[128,1024]{1,0:T(8,128)(2,1)S(1)}, bf16[128,1024]{1,0:T(8,128)(2,1)S(1)}, u32[]{:S(2)}, u32[]{:S(2)}) %collective-permute-start.16) | collective-permute-done | bytes 262176 | tf_op jit(solution)/shard_map/ppermute | solution.py:312
  136.4 2.7 %collective-permute-done.17.a3 = bf16[128,1024]{1,0:T(8,128)(2,1)S(1)} collective-permute-done((bf16[128,1024]{1,0:T(8,128)(2,1)S(1)}, bf16[128,1024]{1,0:T(8,128)(2,1)S(1)}, u32[]{:S(2)}, u32[]{:S(2)}) %collective-permute-start.17) | collective-permute-done | bytes 262176 | tf_op jit(solution)/shard_map/ppermute | solution.py:312
  139.1 1.6 copy-done
  140.7 0.7 shard_map.81
  141.4 1.9 %collective-permute-start.19 = (f32[4,128,512]{2,1,0:T(8,128)S(1)}, f32[4,128,512]{2,1,0:T(8,128)S(1)}, u32[]{:S(2)}, u32[]{:S(2)}) collective-permute-start(f32[4,128,512]{2,1,0:T(8,128)S(1)} %shard_map.81), channel_id=1, source_target_pairs={{0,1},{1,0},{2,3},{3,2},{4,5},{5,4},{6,7},{7,6},{8,9},{9,8},{10,11... | collective-permute-start | bytes 3145736 | tf_op jit(solution)/shard_map/ppermute | solution.py:27
  143.4 0.7 shard_map.80
  144.1 1.9 %collective-permute-done.19 = f32[4,128,512]{2,1,0:T(8,128)S(1)} collective-permute-done((f32[4,128,512]{2,1,0:T(8,128)S(1)}, f32[4,128,512]{2,1,0:T(8,128)S(1)}, u32[]{:S(2)}, u32[]{:S(2)}) %collective-permute-start.19) | collective-permute-done | bytes 1048608 | tf_op jit(solution)/shard_map/ppermute | solution.py:27
  146.0 1.0 add_convert_fusion
  146.9 3.5 %all-to-all-start.1 = ((bf16[4,128,512]{2,1,0:T(8,128)(2,1)}), bf16[4,128,512]{2,1,0:T(8,128)(2,1)S(1)}, u32[]{:S(2)}, u32[]{:S(2)}) async-start(bf16[4,128,512]{2,1,0:T(8,128)(2,1)} %add_convert_fusion), calls=%async_computation.1 | async-start | bytes 1048576 | tf_op jit(solution)/shard_map/all_to_all | solution.py:318
  151.1 14.3 %all-to-all-done.1 = bf16[4,128,512]{2,1,0:T(8,128)(2,1)S(1)} async-done(((bf16[4,128,512]{2,1,0:T(8,128)(2,1)}), bf16[4,128,512]{2,1,0:T(8,128)(2,1)S(1)}, u32[]{:S(2)}, u32[]{:S(2)}) %all-to-all-start.1) | async-done | bytes 524320 | tf_op jit(solution)/shard_map/all_to_all | solution.py:318
  165.6 3.4 %collective-permute-start.20 = (bf16[128,512]{1,0:T(8,128)(2,1)S(1)}, bf16[128,512]{1,0:T(8,128)(2,1)S(1)}, u32[]{:S(2)}, u32[]{:S(2)}) collective-permute-start(bf16[128,512]{1,0:T(8,128)(2,1)S(1)} %multiply_convert_fusion), channel_id=1, source_target_pairs={{0,0},{2,384},{4,256},{6,128},{128,130},{130,2},{132,386},{134,258... | collective-permute-start | bytes 393224 | tf_op jit(solution)/shard_map/ppermute | solution.py:322
  168.9 10.9 %collective-permute-done.20 = bf16[128,512]{1,0:T(8,128)(2,1)S(1)} collective-permute-done((bf16[128,512]{1,0:T(8,128)(2,1)S(1)}, bf16[128,512]{1,0:T(8,128)(2,1)S(1)}, u32[]{:S(2)}, u32[]{:S(2)}) %collective-permute-start.20) | collective-permute-done | bytes 131104 | tf_op jit(solution)/shard_map/ppermute | solution.py:322
  179.9 0.7 copy.15
  (41 shorter events, 0.9 us)
Async XLA Ops:
  6.5 26.2 %copy-start.3 = (bf16[128,128]{1,0:T(8,128)(2,1)S(1)}, bf16[128,128]{1,0:T(8,128)(2,1)}, u32[]{:S(2)}) copy-start(bf16[128,128]{1,0:T(8,128)(2,1)} %param.9) | copy-start | bytes 98308
  6.5 26.2 %copy-start.4 = (bf16[128,128]{1,0:T(8,128)(2,1)S(1)}, bf16[128,128]{1,0:T(8,128)(2,1)}, u32[]{:S(2)}) copy-start(bf16[128,128]{1,0:T(8,128)(2,1)} %param.8) | copy-start | bytes 98308
  6.5 60.5 %copy-start.5 = (s32[2,128]{1,0:T(2,128)S(1)}, s32[2,128]{1,0:T(2,128)}, u32[]{:S(2)}) copy-start(s32[2,128]{1,0:T(2,128)} %param.11) | copy-start | bytes 3076
  6.5 60.5 %copy-start.2 = (bf16[128,1024]{1,0:T(8,128)(2,1)S(1)}, bf16[128,1024]{1,0:T(8,128)(2,1)}, u32[]{:S(2)}) copy-start(bf16[128,1024]{1,0:T(8,128)(2,1)} %param.7) | copy-start | bytes 786436
  6.5 86.1 %copy-start.1 = (f32[128]{0:T(128)S(1)}, f32[128]{0:T(128)}, u32[]{:S(2)}) copy-start(f32[128]{0:T(128)} %param.10) | copy-start | bytes 1540
  6.5 132.6 %all-gather.2.cloned.1.call-start = ((), (), s32[]{:S(2)}) async-start(), calls=%async_computation.2 | async-start | bytes 2359296 | tf_op jit(solution)/shard_map/all_gather | solution.py:284
  19.8 12.2 %collective-permute-start.18 = (bf16[64,1024]{1,0:T(8,128)(2,1)S(1)}, bf16[64,1024]{1,0:T(8,128)(2,1)S(1)}, u32[]{:S(2)}, u32[]{:S(2)}) collective-permute-start(bf16[64,1024]{1,0:T(8,128)(2,1)S(1)} %bitcast.25), channel_id=1, source_target_pairs={{0,64},{64,0},{1,65},{65,1},{2,66},{66,2},{3,67},{67,3},{4,68},{68... | collective-permute-start | bytes 393224 | tf_op jit(solution)/shard_map/ppermute | solution.py:27
  32.8 16.6 %collective-permute-start.2 = (bf16[1,2,128,128]{3,2,1,0:T(8,128)(2,1)S(1)}, bf16[1,2,128,128]{3,2,1,0:T(8,128)(2,1)S(1)}, u32[]{:S(2)}, u32[]{:S(2)}) collective-permute-start(bf16[1,2,128,128]{3,2,1,0:T(8,128)(2,1)S(1)} %maximum_bitcast_fusion), channel_id=1, source_target_pairs={{0,0},{1,128},{128,1},{129,129},{64,64},{65,192},{192,65},{193,193... | collective-permute-start | bytes 196616 | tf_op jit(solution)/shard_map/ppermute | solution.py:254
  34.7 14.7 %collective-permute-start.3 = (bf16[1,2,128,128]{3,2,1,0:T(8,128)(2,1)S(1)}, bf16[1,2,128,128]{3,2,1,0:T(8,128)(2,1)S(1)}, u32[]{:S(2)}, u32[]{:S(2)}) collective-permute-start(bf16[1,2,128,128]{3,2,1,0:T(8,128)(2,1)S(1)} %maximum_bitcast_fusion), channel_id=1, source_target_pairs={{0,256},{1,384},{128,257},{129,385},{64,320},{65,448},{192,321},{1... | collective-permute-start | bytes 196616 | tf_op jit(solution)/shard_map/ppermute | solution.py:254
  39.0 10.4 %collective-permute-start.4 = (bf16[1,2,128,128]{3,2,1,0:T(8,128)(2,1)S(1)}, bf16[1,2,128,128]{3,2,1,0:T(8,128)(2,1)S(1)}, u32[]{:S(2)}, u32[]{:S(2)}) collective-permute-start(bf16[1,2,128,128]{3,2,1,0:T(8,128)(2,1)S(1)} %maximum_bitcast_fusion), channel_id=1, source_target_pairs={{0,64},{1,192},{128,65},{129,193},{64,0},{65,128},{192,1},{193,129... | collective-permute-start | bytes 196616 | tf_op jit(solution)/shard_map/ppermute | solution.py:254
  42.1 11.8 %collective-permute-start.5 = (bf16[1,2,128,128]{3,2,1,0:T(8,128)(2,1)S(1)}, bf16[1,2,128,128]{3,2,1,0:T(8,128)(2,1)S(1)}, u32[]{:S(2)}, u32[]{:S(2)}) collective-permute-start(bf16[1,2,128,128]{3,2,1,0:T(8,128)(2,1)S(1)} %maximum_bitcast_fusion), channel_id=1, source_target_pairs={{0,320},{1,448},{128,321},{129,449},{64,256},{65,384},{192,257},{1... | collective-permute-start | bytes 196616 | tf_op jit(solution)/shard_map/ppermute | solution.py:254
  54.0 22.0 %collective-permute-start.6 = (bf16[4,2,128,128]{3,2,1,0:T(8,128)(2,1)S(1)}, bf16[4,2,128,128]{3,2,1,0:T(8,128)(2,1)S(1)}, u32[]{:S(2)}, u32[]{:S(2)}) collective-permute-start(bf16[4,2,128,128]{3,2,1,0:T(8,128)(2,1)S(1)} %constant_dynamic-update-slice_fusion.refs_3_), channel_id=1, source_target_pairs={{0,8},{8,16},{16,24},{24,32},{32,40},{40,48},{48,56},{56,0},{1,9},... | collective-permute-start | bytes 786440 | tf_op jit(solution)/shard_map/ppermute | solution.py:27
  58.5 19.4 %collective-permute-start.10 = (bf16[4,2,128,128]{3,2,1,0:T(8,128)(2,1)S(1)}, bf16[4,2,128,128]{3,2,1,0:T(8,128)(2,1)S(1)}, u32[]{:S(2)}, u32[]{:S(2)}) collective-permute-start(bf16[4,2,128,128]{3,2,1,0:T(8,128)(2,1)S(1)} %constant_dynamic-update-slice_fusion.refs_3_), channel_id=1, source_target_pairs={{0,56},{8,0},{16,8},{24,16},{32,24},{40,32},{48,40},{56,48},{1,57}... | collective-permute-start | bytes 786440 | tf_op jit(solution)/shard_map/ppermute | solution.py:27
  67.1 15.9 %collective-permute-start = (bf16[144,1024]{1,0:T(8,128)(2,1)S(1)}, bf16[144,1024]{1,0:T(8,128)(2,1)S(1)}, u32[]{:S(2)}, u32[]{:S(2)}) collective-permute-start(bf16[144,1024]{1,0:T(8,128)(2,1)S(1)} %fusion.1), channel_id=1, source_target_pairs={{0,0},{1,128},{128,1},{129,129},{64,64},{65,192},{192,65},{193,193... | collective-permute-start | bytes 884744 | tf_op jit(solution)/shard_map/ppermute | solution.py:254
  76.0 9.5 %collective-permute-start.7 = (bf16[4,2,128,128]{3,2,1,0:T(8,128)(2,1)S(1)}, bf16[4,2,128,128]{3,2,1,0:T(8,128)(2,1)S(1)}, u32[]{:S(2)}, u32[]{:S(2)}) collective-permute-start(bf16[4,2,128,128]{3,2,1,0:T(8,128)(2,1)S(1)} %collective-permute-done.6.refs_3_), channel_id=1, source_target_pairs={{0,8},{8,16},{16,24},{24,32},{32,40},{40,48},{48,56},{56,0},{1,9},... | collective-permute-start | bytes 786440 | tf_op jit(solution)/shard_map/ppermute | solution.py:27
  77.9 9.5 %collective-permute-start.11 = (bf16[4,2,128,128]{3,2,1,0:T(8,128)(2,1)S(1)}, bf16[4,2,128,128]{3,2,1,0:T(8,128)(2,1)S(1)}, u32[]{:S(2)}, u32[]{:S(2)}) collective-permute-start(bf16[4,2,128,128]{3,2,1,0:T(8,128)(2,1)S(1)} %collective-permute-done.10.refs_4_), channel_id=1, source_target_pairs={{0,56},{8,0},{16,8},{24,16},{32,24},{40,32},{48,40},{56,48},{1,57}... | collective-permute-start | bytes 786440 | tf_op jit(solution)/shard_map/ppermute | solution.py:27
  83.1 9.6 %collective-permute-start.1 = (bf16[144,1024]{1,0:T(8,128)(2,1)S(1)}, bf16[144,1024]{1,0:T(8,128)(2,1)S(1)}, u32[]{:S(2)}, u32[]{:S(2)}) collective-permute-start(bf16[144,1024]{1,0:T(8,128)(2,1)S(1)} %collective-permute-done.refs_1_), channel_id=1, source_target_pairs={{0,1},{1,0},{2,3},{3,2},{4,5},{5,4},{6,7},{7,6},{8,9},{9,8},{10,11... | collective-permute-start | bytes 884744 | tf_op jit(solution)/shard_map/ppermute | solution.py:27
  85.4 11.4 %collective-permute-start.8 = (bf16[4,2,128,128]{3,2,1,0:T(8,128)(2,1)S(1)}, bf16[4,2,128,128]{3,2,1,0:T(8,128)(2,1)S(1)}, u32[]{:S(2)}, u32[]{:S(2)}) collective-permute-start(bf16[4,2,128,128]{3,2,1,0:T(8,128)(2,1)S(1)} %collective-permute-done.7.refs_3_), channel_id=1, source_target_pairs={{0,8},{8,16},{16,24},{24,32},{32,40},{40,48},{48,56},{56,0},{1,9},... | collective-permute-start | bytes 786440 | tf_op jit(solution)/shard_map/ppermute | solution.py:27
  87.4 18.7 %collective-permute-start.12 = (bf16[4,2,128,128]{3,2,1,0:T(8,128)(2,1)S(1)}, bf16[4,2,128,128]{3,2,1,0:T(8,128)(2,1)S(1)}, u32[]{:S(2)}, u32[]{:S(2)}) collective-permute-start(bf16[4,2,128,128]{3,2,1,0:T(8,128)(2,1)S(1)} %collective-permute-done.11.refs_4_), channel_id=1, source_target_pairs={{0,56},{8,0},{16,8},{24,16},{32,24},{40,32},{48,40},{56,48},{1,57}... | collective-permute-start | bytes 786440 | tf_op jit(solution)/shard_map/ppermute | solution.py:27
  96.9 12.9 %collective-permute-start.9 = (bf16[4,2,128,128]{3,2,1,0:T(8,128)(2,1)S(1)}, bf16[4,2,128,128]{3,2,1,0:T(8,128)(2,1)S(1)}, u32[]{:S(2)}, u32[]{:S(2)}) collective-permute-start(bf16[4,2,128,128]{3,2,1,0:T(8,128)(2,1)S(1)} %collective-permute-done.8.refs_3_), channel_id=1, source_target_pairs={{0,8},{8,16},{16,24},{24,32},{32,40},{40,48},{48,56},{56,0},{1,9},... | collective-permute-start | bytes 786440 | tf_op jit(solution)/shard_map/ppermute | solution.py:27
  111.5 3.9 %collective-permute-start.13 = (f32[144,1024]{1,0:T(8,128)S(1)}, f32[144,1024]{1,0:T(8,128)S(1)}, u32[]{:S(2)}, u32[]{:S(2)}) collective-permute-start(f32[144,1024]{1,0:T(8,128)S(1)} %shard_map.78), channel_id=1, source_target_pairs={{0,1},{1,0},{2,3},{3,2},{4,5},{5,4},{6,7},{7,6},{8,9},{9,8},{10,11... | collective-permute-start | bytes 1769480 | tf_op jit(solution)/shard_map/ppermute | solution.py:27
  115.6 15.0 %collective-permute-start.14 = (bf16[128,1024]{1,0:T(8,128)(2,1)S(1)}, bf16[128,1024]{1,0:T(8,128)(2,1)S(1)}, u32[]{:S(2)}, u32[]{:S(2)}) collective-permute-start(bf16[128,1024]{1,0:T(8,128)(2,1)S(1)} %shard_map.79), channel_id=1, source_target_pairs={{0,0},{1,128},{128,129},{129,257},{256,256},{257,384},{384,385},{3... | collective-permute-start | bytes 786440 | tf_op jit(solution)/shard_map/ppermute | solution.py:312
  117.7 15.9 %collective-permute-start.15 = (bf16[128,1024]{1,0:T(8,128)(2,1)S(1)}, bf16[128,1024]{1,0:T(8,128)(2,1)S(1)}, u32[]{:S(2)}, u32[]{:S(2)}) collective-permute-start(bf16[128,1024]{1,0:T(8,128)(2,1)S(1)} %shard_map.79), channel_id=1, source_target_pairs={{0,128},{1,256},{128,257},{129,385},{256,384},{257,0},{384,1},{385... | collective-permute-start | bytes 786440 | tf_op jit(solution)/shard_map/ppermute | solution.py:312
  123.7 12.7 %collective-permute-start.16 = (bf16[128,1024]{1,0:T(8,128)(2,1)S(1)}, bf16[128,1024]{1,0:T(8,128)(2,1)S(1)}, u32[]{:S(2)}, u32[]{:S(2)}) collective-permute-start(bf16[128,1024]{1,0:T(8,128)(2,1)S(1)} %shard_map.79), channel_id=1, source_target_pairs={{0,256},{1,384},{128,385},{129,1},{256,0},{257,128},{384,129},{385... | collective-permute-start | bytes 786440 | tf_op jit(solution)/shard_map/ppermute | solution.py:312
  128.6 10.5 %collective-permute-start.17 = (bf16[128,1024]{1,0:T(8,128)(2,1)S(1)}, bf16[128,1024]{1,0:T(8,128)(2,1)S(1)}, u32[]{:S(2)}, u32[]{:S(2)}) collective-permute-start(bf16[128,1024]{1,0:T(8,128)(2,1)S(1)} %shard_map.79), channel_id=1, source_target_pairs={{0,384},{1,0},{128,1},{129,129},{256,128},{257,256},{384,257},{385... | collective-permute-start | bytes 786440 | tf_op jit(solution)/shard_map/ppermute | solution.py:312
  139.1 1.6 copy-start
  141.4 4.6 %collective-permute-start.19 = (f32[4,128,512]{2,1,0:T(8,128)S(1)}, f32[4,128,512]{2,1,0:T(8,128)S(1)}, u32[]{:S(2)}, u32[]{:S(2)}) collective-permute-start(f32[4,128,512]{2,1,0:T(8,128)S(1)} %shard_map.81), channel_id=1, source_target_pairs={{0,1},{1,0},{2,3},{3,2},{4,5},{5,4},{6,7},{7,6},{8,9},{9,8},{10,11... | collective-permute-start | bytes 3145736 | tf_op jit(solution)/shard_map/ppermute | solution.py:27
  146.9 18.5 %all-to-all-start.1 = ((bf16[4,128,512]{2,1,0:T(8,128)(2,1)}), bf16[4,128,512]{2,1,0:T(8,128)(2,1)S(1)}, u32[]{:S(2)}, u32[]{:S(2)}) async-start(bf16[4,128,512]{2,1,0:T(8,128)(2,1)} %add_convert_fusion), calls=%async_computation.1 | async-start | bytes 1048576 | tf_op jit(solution)/shard_map/all_to_all | solution.py:318
  165.6 14.3 %collective-permute-start.20 = (bf16[128,512]{1,0:T(8,128)(2,1)S(1)}, bf16[128,512]{1,0:T(8,128)(2,1)S(1)}, u32[]{:S(2)}, u32[]{:S(2)}) collective-permute-start(bf16[128,512]{1,0:T(8,128)(2,1)S(1)} %multiply_convert_fusion), channel_id=1, source_target_pairs={{0,0},{2,384},{4,256},{6,128},{128,130},{130,2},{132,386},{134,258... | collective-permute-start | bytes 393224 | tf_op jit(solution)/shard_map/ppermute | solution.py:322
Sparse Core Ops, SparseCore 0:
  32.9 49.2 all-gather.1

commit v2 on v1

--- a/solution.py
+++ b/solution.py
@@ -72,7 +72,7 @@
 
     def score(unit):
         c, w = unit
-        k = chunks[c][:, 0].reshape(BLOCKS * D, D)
+        k = chunks[c][0:BLOCKS, 0].reshape(BLOCKS * D, D)
         return lax.dot_general(
             k,
             nq_ref[cols[w], :],
@@ -103,7 +103,7 @@
 
     def collect(unit, p, acc, factor):
         c, _ = unit
-        v = chunks[c][:, 1].reshape(BLOCKS * D, D)
+        v = chunks[c][0:BLOCKS, 1].reshape(BLOCKS * D, D)
         return acc * factor + lax.dot_general(
             v, p, (((0,), (0,)), ((), ())), preferred_element_type=jnp.float32
         )
@@ -170,7 +170,7 @@
             bytes_accessed=n_keys * D * 4 + rows * D * 12,
             transcendentals=rows * n_keys,
         ),
-        compiler_params=pltpu.CompilerParams(vmem_limit_bytes=40 << 20),
+        compiler_params=pltpu.CompilerParams(vmem_limit_bytes=16 << 20),
     )(ids, *packs, *chunks, *extra)
     if half is not None or first:
         return out
@@ -199,43 +199,74 @@
         cost_estimate=pl.CostEstimate(
             flops=6 * ROWS * D, bytes_accessed=ROWS * D * 10, transcendentals=0
         ),
-        compiler_params=pltpu.CompilerParams(vmem_limit_bytes=32 << 20),
+        compiler_params=pltpu.CompilerParams(vmem_limit_bytes=16 << 20),
     )(a, b)
 
 
-def project_kernel(col_ref, core_ref, a0, a1, a2, a3, w_ref, out_ref):
+def assemble_kernel(at_ref, *refs):
+    chunks, first_ref, second_ref, out_ref = refs[:8], refs[8], refs[9], refs[10]
+    for p in range(8):
+        for y in range(2):
+            if y == 0:
+                source, base = chunks[p], BLOCKS
+            elif p < 5:
+                source, base = first_ref, 2 * p
+            else:
+                source, base = second_ref, 2 * (p - 5)
+            slot = at_ref[2 * p + y]
+            for x in range(4):
+                block = source[base + x // 2, x % 2]
+                for t in range(8):
+                    out_ref[x, slot, :, t * 128 : (t + 1) * 128] = block[
+                        t * 16 : (t + 1) * 16
+                    ]
+
+
+def assemble(at, chunks, first, second):
+    return pl.pallas_call(
+        assemble_kernel,
+        out_shape=jax.ShapeDtypeStruct((4, 16, 16, 1024), jnp.bfloat16),
+        in_specs=[SMEM] + [VMEM] * 10,
+        out_specs=VMEM,
+        cost_estimate=pl.CostEstimate(
+            flops=0, bytes_accessed=4 << 20, transcendentals=0
+        ),
+        compiler_params=pltpu.CompilerParams(vmem_limit_bytes=16 << 20),
+    )(at, *chunks, first, second)
+
+
+def project_kernel(col_ref, turn_ref, a0, a1, a2, a3, w_ref, out_ref):
     total = None
     a = jnp.concatenate([a0[...], a1[...], a2[...], a3[...]], axis=0)
     for x in range(4):
-        w = jnp.concatenate([w_ref[:, 0, x], w_ref[:, 1, x]]).reshape(256, 512)
         part = jnp.dot(
-            a[:, x * 256 : (x + 1) * 256], w, preferred_element_type=jnp.float32
+            a[:, x * 256 : (x + 1) * 256],
+            w_ref[x].reshape(256, 512),
+            preferred_element_type=jnp.float32,
         )
         total = part if total is None else total + part
     for k in range(4):
-        out_ref[(core_ref[0] + k) % 4] = total[k * TOK : (k + 1) * TOK]
-
-
-def project(column, core, slots, weight):
+        out_ref[(turn_ref[0] + k) % 4] = total[k * TOK : (k + 1) * TOK]
+
+
+def project(column, turn, slots, weight):
     return pl.pallas_call(
         project_kernel,
         grid_spec=pltpu.PrefetchScalarGridSpec(
             num_scalar_prefetch=2,
             grid=(1,),
-            in_specs=[pl.BlockSpec((TOK, ROWS), lambda i, col, core: (0, 0))] * 4
+            in_specs=[pl.BlockSpec((TOK, ROWS), lambda i, col, turn: (0, 0))] * 4
             + [
-                pl.BlockSpec(
-                    (8, 2, 4, 16, 512), lambda i, col, core: (0, 0, 0, 0, col[0])
-                ),
+                pl.BlockSpec((4, 16, 16, 512), lambda i, col, turn: (0, 0, 0, col[0])),
             ],
-            out_specs=pl.BlockSpec((4, TOK, 512), lambda i, col, core: (0, 0, 0)),
+            out_specs=pl.BlockSpec((4, TOK, 512), lambda i, col, turn: (0, 0, 0)),
         ),
         out_shape=jax.ShapeDtypeStruct((4, TOK, 512), jnp.float32),
         cost_estimate=pl.CostEstimate(
             flops=512 * 1024 * 1024, bytes_accessed=3 << 20, transcendentals=0
         ),
-        compiler_params=pltpu.CompilerParams(vmem_limit_bytes=32 << 20),
-    )(column, core, *slots, weight)
+        compiler_params=pltpu.CompilerParams(vmem_limit_bytes=16 << 20),
+    )(column, turn, *slots, weight)
 
 
 def work(queries, keys, values, q_gain, frame_bounds, output_weight, attn_gate):
@@ -253,9 +284,19 @@
                         pairs.append((source, (x * 2 + (y + dy) % 2) * 2 + a))
         return lax.ppermute(value, ("x", "yh", "c"), pairs)
 
+    quarter = output_weight[0].reshape(16, 4, 8, 128).transpose(1, 2, 0, 3)
+    quarter = lax.all_to_all(
+        quarter.reshape(512, 128), "x", split_axis=0, concat_axis=0, tiled=True
+    )
     own = jnp.stack([keys, values])[None]
     chunk = jnp.concatenate(
-        [trade(own), trade(own, di=1), trade(own, dy=1), trade(own, di=1, dy=1)]
+        [
+            trade(own),
+            trade(own, di=1),
+            trade(own, dy=1),
+            trade(own, di=1, dy=1),
+            quarter.reshape(2, 2, 128, 128),
+        ]
     )
     block_x = 2 * (ax // 2) + core
     in_chunk = jnp.stack(
@@ -272,17 +313,6 @@
     near = trade(jnp.concatenate([queries, bounds]))
     far = shift(near, "c", 1)
     packs = (near, far)
-
-    quarter = output_weight[0].reshape(16, 4, 1024).transpose(1, 0, 2)
-    quarter = lax.all_to_all(
-        quarter.reshape(64, 1024), "x", split_axis=0, concat_axis=0, tiled=True
-    )
-    partner = shift(quarter, "yh", 1)
-    both = jnp.stack(
-        [jnp.where(ay == 0, quarter, partner), jnp.where(ay == 0, partner, quarter)]
-    )
-    weight = lax.all_gather(both.reshape(128, 1024), "z", axis=0, tiled=True)
-    weight = weight.reshape(8, 2, 4, 16, 1024)
 
     right, left = [chunk], [chunk]
     for s in range(1, 5):
@@ -310,16 +340,28 @@
             (x * 2 + c, ((x + k + c) % 4) * 2 + x % 2) for x in range(4) for c in range(2)
         ]
         slots.append(lax.ppermute(attended, ("x", "c"), pairs))
+    parts = [chunk, right[1], left[1], right[2], left[2], right[3], left[3], right[4]]
+    first = shift(jnp.concatenate([c[BLOCKS:] for c in parts[:5]]), "yh", 1)
+    second = shift(jnp.concatenate([c[BLOCKS:] for c in parts[5:]]), "yh", 1)
+    at = jnp.stack(
+        [((ay + dy) % 2) * 8 + (az + h) % 8 for h in hops for dy in (0, 1)]
+    ).astype(jnp.int32)
+    weight = assemble(at, parts, first, second)
+
     core = core.astype(jnp.int32)[None]
-    for_other = project(1 - core, core, slots, weight)
+    turn = (core + 4 - lax.axis_index("yl")) % 4
+    for_other = project(1 - core, turn, slots, weight)
     from_other = shift(for_other, "c", 1)
-    for_own = project(core, core, slots, weight)
-    partial = (for_own + from_other).astype(jnp.bfloat16).reshape(512, 512)
-    pieces = lax.all_to_all(partial, "yl", split_axis=0, concat_axis=0, tiled=True)
-    combined = jnp.sum(pieces.reshape(4, TOK, 512).astype(jnp.float32), axis=0)
-    result = (jnp.tanh(attn_gate[0]) * combined).astype(jnp.bfloat16)
-    pairs = [(x * 4 + y, ((x - y) % 4) * 4 + x) for x in range(4) for y in range(4)]
-    return lax.ppermute(result, ("x", "yl"), pairs)
+    for_own = project(core, turn, slots, weight)
+    combined = None
+    for s in range(4):
+        pairs = [
+            (x * 4 + y, ((x - y - s) % 4) * 4 + x) for x in range(4) for y in range(4)
+        ]
+        part = (for_own[s] + from_other[s]).astype(jnp.bfloat16)
+        part = lax.ppermute(part, ("x", "yl"), pairs).astype(jnp.float32)
+        combined = part if combined is None else combined + part
+    return (jnp.tanh(attn_gate[0]) * combined).astype(jnp.bfloat16)
 
 
 def solution(mesh):

time: 188 us -> 185 us (0.984)
  the two profiles are of different devices: /device:TPU:6 before, /device:TPU:38 now
where the time goes in v2:
time: 185 us; the launch traced here: 183 us
  starting transfers between devices  92.4 us (50%)
  waiting for transfers between devices  59.1 us (32%)
  Pallas kernels  20.2 us (11%)
  local copies, waits for them, and re-layouts  5.86 us (3%)
  other arithmetic  4.55 us (2%)
    ppermute x12, starting transfers between devices, shift(): lax.ppermute(value, axis, [(s, (s + steps) % count) for s in range(count)])  43.7 us
    ppermute x12, waiting for transfers between devices, shift(): lax.ppermute(value, axis, [(s, (s + steps) % count) for s in range(count)])  28.5 us
    ppermute x4, waiting for transfers between devices, work(): part = lax.ppermute(part, ('x', 'yl'), pairs).astype(jnp.float32)  26.1 us
    ppermute x5, starting transfers between devices, trade(): return lax.ppermute(value, ('x', 'yh', 'c'), pairs)  18.7 us
    pallas_call x6, Pallas kernels, attend(): pl.pallas_call(body, out_shape=out_shape, in_specs=[SMEM] + [VMEM] * (2 +...  16.5 us
    ppermute x4, starting transfers between devices, work(): part = lax.ppermute(part, ('x', 'yl'), pairs).astype(jnp.float32)  13 us
    ppermute x4, starting transfers between devices, work(): slots.append(lax.ppermute(attended, ('x', 'c'), pairs))  12.5 us
    unnamed x23, local copies, waits for them, and re-layouts  5.01 us
  transfers between devices with their start and end apart: 26, of which 8 were waited for; matrix products, arithmetic and copies ran while one was open for 3% of the time, Pallas kernels for 11%

profile of v2, /device:TPU:38, one launch (start us, length us, event | category | flops | bytes accessed | tf_op | source)
XLA Modules:
  0.0 183.3 jit_solution(18374915471057679002)
XLA Ops:
  0.8 2.2 %collective-permute-start.2 = (bf16[1,2,128,128]{3,2,1,0:T(8,128)(2,1)S(1)}, bf16[1,2,128,128]{3,2,1,0:T(8,128)(2,1)S(1)}, u32[]{:S(2)}, u32[]{:S(2)}) collective-permute-start(bf16[1,2,128,128]{3,2,1,0:T(8,128)(2,1)S(1)} %maximum_bitcast_fusion), channel_id=1, source_target_pairs={{0,0},{1,128},{128,1},{129,129},{64,64},{65,192},{192,65},{193,193... | collective-permute-start | bytes 196616 | tf_op jit(solution)/shard_map/ppermute | solution.py:285
  3.0 3.3 %collective-permute-start.3 = (bf16[1,2,128,128]{3,2,1,0:T(8,128)(2,1)S(1)}, bf16[1,2,128,128]{3,2,1,0:T(8,128)(2,1)S(1)}, u32[]{:S(2)}, u32[]{:S(2)}) collective-permute-start(bf16[1,2,128,128]{3,2,1,0:T(8,128)(2,1)S(1)} %maximum_bitcast_fusion), channel_id=1, source_target_pairs={{0,256},{1,384},{128,257},{129,385},{64,320},{65,448},{192,321},{1... | collective-permute-start | bytes 196616 | tf_op jit(solution)/shard_map/ppermute | solution.py:285
  6.3 1.9 %collective-permute-start.4 = (bf16[1,2,128,128]{3,2,1,0:T(8,128)(2,1)S(1)}, bf16[1,2,128,128]{3,2,1,0:T(8,128)(2,1)S(1)}, u32[]{:S(2)}, u32[]{:S(2)}) collective-permute-start(bf16[1,2,128,128]{3,2,1,0:T(8,128)(2,1)S(1)} %maximum_bitcast_fusion), channel_id=1, source_target_pairs={{0,64},{1,192},{128,65},{129,193},{64,0},{65,128},{192,1},{193,129... | collective-permute-start | bytes 196616 | tf_op jit(solution)/shard_map/ppermute | solution.py:285
  8.2 9.1 %collective-permute-start.5 = (bf16[1,2,128,128]{3,2,1,0:T(8,128)(2,1)S(1)}, bf16[1,2,128,128]{3,2,1,0:T(8,128)(2,1)S(1)}, u32[]{:S(2)}, u32[]{:S(2)}) collective-permute-start(bf16[1,2,128,128]{3,2,1,0:T(8,128)(2,1)S(1)} %maximum_bitcast_fusion), channel_id=1, source_target_pairs={{0,320},{1,448},{128,321},{129,449},{64,256},{65,384},{192,257},{1... | collective-permute-start | bytes 196616 | tf_op jit(solution)/shard_map/ppermute | solution.py:285
  18.0 1.0 fusion.1
  19.0 2.2 %collective-permute-start = (bf16[144,1024]{1,0:T(8,128)(2,1)S(1)}, bf16[144,1024]{1,0:T(8,128)(2,1)S(1)}, u32[]{:S(2)}, u32[]{:S(2)}) collective-permute-start(bf16[144,1024]{1,0:T(8,128)(2,1)S(1)} %fusion.1), channel_id=1, source_target_pairs={{0,0},{1,128},{128,1},{129,129},{64,64},{65,192},{192,65},{193,193... | collective-permute-start | bytes 884744 | tf_op jit(solution)/shard_map/ppermute | solution.py:285
  21.2 0.9 copy.9
  22.8 4.5 %all-to-all-start = ((bf16[4,128,128]{2,1,0:T(8,128)(2,1)}), bf16[4,128,128]{2,1,0:T(8,128)(2,1)S(1)}, u32[]{:S(2)}, u32[]{:S(2)}) async-start(bf16[4,128,128]{2,1,0:T(8,128)(2,1)} %bitcast.11), calls=%async_computation | async-start | bytes 262144 | tf_op jit(solution)/shard_map/all_to_all | solution.py:288
  27.4 4.4 %all-to-all-done = bf16[4,128,128]{2,1,0:T(8,128)(2,1)S(1)} async-done(((bf16[4,128,128]{2,1,0:T(8,128)(2,1)}), bf16[4,128,128]{2,1,0:T(8,128)(2,1)S(1)}, u32[]{:S(2)}, u32[]{:S(2)}) %all-to-all-start) | async-done | bytes 131104 | tf_op jit(solution)/shard_map/all_to_all | solution.py:288
  31.9 4.3 %collective-permute-start.6 = (bf16[6,2,128,128]{3,2,1,0:T(8,128)(2,1)S(1)}, bf16[6,2,128,128]{3,2,1,0:T(8,128)(2,1)S(1)}, u32[]{:S(2)}, u32[]{:S(2)}) collective-permute-start(bf16[6,2,128,128]{3,2,1,0:T(8,128)(2,1)S(1)} %get-tuple-element.38.refs_3_.refs_0_), channel_id=1, source_target_pairs={{0,8},{8,16},{16,24},{24,32},{32,40},{40,48},{48,56},{56,0},{1,9},... | collective-permute-start | bytes 1179656 | tf_op jit(solution)/shard_map/ppermute | solution.py:27
  36.3 8.6 %collective-permute-start.10 = (bf16[6,2,128,128]{3,2,1,0:T(8,128)(2,1)S(1)}, bf16[6,2,128,128]{3,2,1,0:T(8,128)(2,1)S(1)}, u32[]{:S(2)}, u32[]{:S(2)}) collective-permute-start(bf16[6,2,128,128]{3,2,1,0:T(8,128)(2,1)S(1)} %get-tuple-element.38.refs_3_.refs_0_), channel_id=1, source_target_pairs={{0,56},{8,0},{16,8},{24,16},{32,24},{40,32},{48,40},{56,48},{1,57}... | collective-permute-start | bytes 1179656 | tf_op jit(solution)/shard_map/ppermute | solution.py:27
  45.0 7.3 %collective-permute-done.6.refs_3_.refs_1_ = bf16[6,2,128,128]{3,2,1,0:T(8,128)(2,1)S(1)} collective-permute-done((bf16[6,2,128,128]{3,2,1,0:T(8,128)(2,1)S(1)}, bf16[6,2,128,128]{3,2,1,0:T(8,128)(2,1)S(1)}, u32[]{:S(2)}, u32[]{:S(2)}) %collective-permute-start.6) | collective-permute-done | bytes 393248 | tf_op jit(solution)/shard_map/ppermute | solution.py:27
  52.3 1.9 %collective-permute-start.7 = (bf16[6,2,128,128]{3,2,1,0:T(8,128)(2,1)S(1)}, bf16[6,2,128,128]{3,2,1,0:T(8,128)(2,1)S(1)}, u32[]{:S(2)}, u32[]{:S(2)}) collective-permute-start(bf16[6,2,128,128]{3,2,1,0:T(8,128)(2,1)S(1)} %collective-permute-done.6.refs_3_.refs_1_), channel_id=1, source_target_pairs={{0,8},{8,16},{16,24},{24,32},{32,40},{40,48},{48,56},{56,0},{1,9},... | collective-permute-start | bytes 1179656 | tf_op jit(solution)/shard_map/ppermute | solution.py:27
  54.4 1.9 %collective-permute-start.1 = (bf16[144,1024]{1,0:T(8,128)(2,1)S(1)}, bf16[144,1024]{1,0:T(8,128)(2,1)S(1)}, u32[]{:S(2)}, u32[]{:S(2)}) collective-permute-start(bf16[144,1024]{1,0:T(8,128)(2,1)S(1)} %collective-permute-done.refs_1_), channel_id=1, source_target_pairs={{0,1},{1,0},{2,3},{3,2},{4,5},{5,4},{6,7},{7,6},{8,9},{9,8},{10,11... | collective-permute-start | bytes 884744 | tf_op jit(solution)/shard_map/ppermute | solution.py:27
  56.3 5.1 %collective-permute-start.11 = (bf16[6,2,128,128]{3,2,1,0:T(8,128)(2,1)S(1)}, bf16[6,2,128,128]{3,2,1,0:T(8,128)(2,1)S(1)}, u32[]{:S(2)}, u32[]{:S(2)}) collective-permute-start(bf16[6,2,128,128]{3,2,1,0:T(8,128)(2,1)S(1)} %collective-permute-done.10.refs_4_.refs_2_), channel_id=1, source_target_pairs={{0,56},{8,0},{16,8},{24,16},{32,24},{40,32},{48,40},{56,48},{1,57}... | collective-permute-start | bytes 1179656 | tf_op jit(solution)/shard_map/ppermute | solution.py:27
  61.4 4.5 %collective-permute-done.7.refs_3_ = bf16[6,2,128,128]{3,2,1,0:T(8,128)(2,1)S(1)} collective-permute-done((bf16[6,2,128,128]{3,2,1,0:T(8,128)(2,1)S(1)}, bf16[6,2,128,128]{3,2,1,0:T(8,128)(2,1)S(1)}, u32[]{:S(2)}, u32[]{:S(2)}) %collective-permute-start.7) | collective-permute-done | bytes 393248 | tf_op jit(solution)/shard_map/ppermute | solution.py:27
  65.9 1.9 %collective-permute-start.8 = (bf16[6,2,128,128]{3,2,1,0:T(8,128)(2,1)S(1)}, bf16[6,2,128,128]{3,2,1,0:T(8,128)(2,1)S(1)}, u32[]{:S(2)}, u32[]{:S(2)}) collective-permute-start(bf16[6,2,128,128]{3,2,1,0:T(8,128)(2,1)S(1)} %collective-permute-done.7.refs_3_), channel_id=1, source_target_pairs={{0,8},{8,16},{16,24},{24,32},{32,40},{40,48},{48,56},{56,0},{1,9},... | collective-permute-start | bytes 1179656 | tf_op jit(solution)/shard_map/ppermute | solution.py:27
  67.9 2.4 %shard_map.73 = (bf16[2048,128]{1,0:T(8,128)(2,1)S(1)}, f32[1,2048]{1,0:T(1,128)S(1)}, f32[8,2048]{1,0:T(8,128)S(1)}, f32[128,2048]{1,0:T(8,128)S(1)}) custom-call(s32[4]{0:T(128)S(1)} %get-tuple-element.44.refs_0_, bf16[144,1024]{1,0:T(8,128)(2,1)S(1)} %collective-permute-done.refs_1_, bf16[144,1024]{1,0:T(8,128)(2,1)S(1)} %collective-permute-done.1.refs_2_, ...), custom_call_target="tpu_custom_call" | custom-call | flops 536870912 | bytes 3407872 | tf_op jit(solution)/shard_map/pallas_call | solution.py:163
  70.3 3.6 %shard_map.74 = (f32[1,2048]{1,0:T(1,128)S(1)}, f32[8,2048]{1,0:T(8,128)S(1)}, f32[128,2048]{1,0:T(8,128)S(1)}) custom-call(s32[8]{0:T(128)S(1)} %pad_add_fusion.3.refs_0_, bf16[144,1024]{1,0:T(8,128)(2,1)S(1)} %collective-permute-done.refs_1_, bf16[144,1024]{1,0:T(8,128)(2,1)S(1)} %collective-permute-done.1.refs_2_, ...), custom_call_target="tpu_custom_call" | custom-call | flops 1073741824 | bytes 3670016 | tf_op jit(solution)/shard_map/pallas_call | solution.py:163
  73.9 5.1 %collective-permute-start.12 = (bf16[6,2,128,128]{3,2,1,0:T(8,128)(2,1)S(1)}, bf16[6,2,128,128]{3,2,1,0:T(8,128)(2,1)S(1)}, u32[]{:S(2)}, u32[]{:S(2)}) collective-permute-start(bf16[6,2,128,128]{3,2,1,0:T(8,128)(2,1)S(1)} %collective-permute-done.11.refs_4_), channel_id=1, source_target_pairs={{0,56},{8,0},{16,8},{24,16},{32,24},{40,32},{48,40},{56,48},{1,57}... | collective-permute-start | bytes 1179656 | tf_op jit(solution)/shard_map/ppermute | solution.py:27
  79.1 1.9 %collective-permute-start.9 = (bf16[6,2,128,128]{3,2,1,0:T(8,128)(2,1)S(1)}, bf16[6,2,128,128]{3,2,1,0:T(8,128)(2,1)S(1)}, u32[]{:S(2)}, u32[]{:S(2)}) collective-permute-start(bf16[6,2,128,128]{3,2,1,0:T(8,128)(2,1)S(1)} %collective-permute-done.8.refs_3_.refs_5_), channel_id=1, source_target_pairs={{0,8},{8,16},{16,24},{24,32},{32,40},{40,48},{48,56},{56,0},{1,9},... | collective-permute-start | bytes 1179656 | tf_op jit(solution)/shard_map/ppermute | solution.py:27
  81.1 2.2 %collective-permute-start.18 = (bf16[10,2,128,128]{3,2,1,0:T(8,128)(2,1)S(1)}, bf16[10,2,128,128]{3,2,1,0:T(8,128)(2,1)S(1)}, u32[]{:S(2)}, u32[]{:S(2)}) collective-permute-start(bf16[10,2,128,128]{3,2,1,0:T(8,128)(2,1)S(1)} %slice_dynamic-update-slice_fusion), channel_id=1, source_target_pairs={{0,64},{64,0},{1,65},{65,1},{2,66},{66,2},{3,67},{67,3},{4,68},{68... | collective-permute-start | bytes 1966088 | tf_op jit(solution)/shard_map/ppermute | solution.py:27
  83.3 3.6 %shard_map.75 = (f32[1,2048]{1,0:T(1,128)S(1)}, f32[8,2048]{1,0:T(8,128)S(1)}, f32[128,2048]{1,0:T(8,128)S(1)}) custom-call(s32[8]{0:T(128)S(1)} %pad_add_fusion.2.refs_0_, bf16[144,1024]{1,0:T(8,128)(2,1)S(1)} %collective-permute-done.refs_1_, bf16[144,1024]{1,0:T(8,128)(2,1)S(1)} %collective-permute-done.1.refs_2_, ...), custom_call_target="tpu_custom_call" | custom-call | flops 1073741824 | bytes 3670016 | tf_op jit(solution)/shard_map/pallas_call | solution.py:163
  86.9 3.6 %shard_map.76 = (f32[1,2048]{1,0:T(1,128)S(1)}, f32[8,2048]{1,0:T(8,128)S(1)}, f32[128,2048]{1,0:T(8,128)S(1)}) custom-call(s32[8]{0:T(128)S(1)} %pad_add_fusion.1.refs_0_, bf16[144,1024]{1,0:T(8,128)(2,1)S(1)} %collective-permute-done.refs_1_, bf16[144,1024]{1,0:T(8,128)(2,1)S(1)} %collective-permute-done.1.refs_2_, ...), custom_call_target="tpu_custom_call" | custom-call | flops 1073741824 | bytes 3670016 | tf_op jit(solution)/shard_map/pallas_call | solution.py:163
  90.5 0.8 collective-permute-done.9.refs_3_.refs_7_
  91.4 1.6 shard_map.78
  93.0 1.9 %collective-permute-start.13 = (f32[144,1024]{1,0:T(8,128)S(1)}, f32[144,1024]{1,0:T(8,128)S(1)}, u32[]{:S(2)}, u32[]{:S(2)}) collective-permute-start(f32[144,1024]{1,0:T(8,128)S(1)} %shard_map.78), channel_id=1, source_target_pairs={{0,1},{1,0},{2,3},{3,2},{4,5},{5,4},{6,7},{7,6},{8,9},{9,8},{10,11... | collective-permute-start | bytes 1769480 | tf_op jit(solution)/shard_map/ppermute | solution.py:27
  95.8 6.9 %collective-permute-start.19 = (bf16[6,2,128,128]{3,2,1,0:T(8,128)(2,1)}, bf16[6,2,128,128]{3,2,1,0:T(8,128)(2,1)}, u32[]{:S(2)}, u32[]{:S(2)}) collective-permute-start(bf16[6,2,128,128]{3,2,1,0:T(8,128)(2,1)} %pad_maximum_fusion), channel_id=1, source_target_pairs={{0,64},{64,0},{1,65},{65,1},{2,66},{66,2},{3,67},{67,3},{4,68},{68... | collective-permute-start | bytes 1179656 | tf_op jit(solution)/shard_map/ppermute | solution.py:27
  102.7 1.6 shard_map.77.a_ref
  104.4 0.9 shard_map.79
  105.3 2.1 %collective-permute-start.14 = (bf16[128,1024]{1,0:T(8,128)(2,1)}, bf16[128,1024]{1,0:T(8,128)(2,1)S(1)}, u32[]{:S(2)}, u32[]{:S(2)}) collective-permute-start(bf16[128,1024]{1,0:T(8,128)(2,1)} %shard_map.79), channel_id=1, source_target_pairs={{0,0},{1,128},{128,129},{129,257},{256,256},{257,384},{384,385},{3... | collective-permute-start | bytes 786440 | tf_op jit(solution)/shard_map/ppermute | solution.py:342
  107.4 4.0 %collective-permute-start.15 = (bf16[128,1024]{1,0:T(8,128)(2,1)}, bf16[128,1024]{1,0:T(8,128)(2,1)S(1)}, u32[]{:S(2)}, u32[]{:S(2)}) collective-permute-start(bf16[128,1024]{1,0:T(8,128)(2,1)} %shard_map.79), channel_id=1, source_target_pairs={{0,128},{1,256},{128,257},{129,385},{256,384},{257,0},{384,1},{385... | collective-permute-start | bytes 786440 | tf_op jit(solution)/shard_map/ppermute | solution.py:342
  111.4 4.4 %collective-permute-start.16 = (bf16[128,1024]{1,0:T(8,128)(2,1)}, bf16[128,1024]{1,0:T(8,128)(2,1)S(1)}, u32[]{:S(2)}, u32[]{:S(2)}) collective-permute-start(bf16[128,1024]{1,0:T(8,128)(2,1)} %shard_map.79), channel_id=1, source_target_pairs={{0,256},{1,384},{128,385},{129,1},{256,0},{257,128},{384,129},{385... | collective-permute-start | bytes 786440 | tf_op jit(solution)/shard_map/ppermute | solution.py:342
  115.9 0.8 copy-done.2
  116.7 1.9 %collective-permute-start.17 = (bf16[128,1024]{1,0:T(8,128)(2,1)}, bf16[128,1024]{1,0:T(8,128)(2,1)S(1)}, u32[]{:S(2)}, u32[]{:S(2)}) collective-permute-start(bf16[128,1024]{1,0:T(8,128)(2,1)} %shard_map.79), channel_id=1, source_target_pairs={{0,384},{1,0},{128,1},{129,129},{256,128},{257,256},{384,257},{385... | collective-permute-start | bytes 786440 | tf_op jit(solution)/shard_map/ppermute | solution.py:342
  118.8 14.0 %collective-permute-done.19.refs_9_ = bf16[6,2,128,128]{3,2,1,0:T(8,128)(2,1)} collective-permute-done((bf16[6,2,128,128]{3,2,1,0:T(8,128)(2,1)}, bf16[6,2,128,128]{3,2,1,0:T(8,128)(2,1)}, u32[]{:S(2)}, u32[]{:S(2)}) %collective-permute-start.19) | collective-permute-done | bytes 393248 | tf_op jit(solution)/shard_map/ppermute | solution.py:27
  132.8 1.0 copy-done.1
  133.8 1.1 copy-done.3
  134.8 1.0 copy-done.5
  135.8 1.4 shard_map.80.w_ref
  138.0 1.9 %collective-permute-start.20 = (f32[4,128,512]{2,1,0:T(8,128)S(1)}, f32[4,128,512]{2,1,0:T(8,128)S(1)}, u32[]{:S(2)}, u32[]{:S(2)}) collective-permute-start(f32[4,128,512]{2,1,0:T(8,128)S(1)} %shard_map.82), channel_id=1, source_target_pairs={{0,1},{1,0},{2,3},{3,2},{4,5},{5,4},{6,7},{7,6},{8,9},{9,8},{10,11... | collective-permute-start | bytes 3145736 | tf_op jit(solution)/shard_map/ppermute | solution.py:27
  140.6 1.9 %collective-permute-done.20 = f32[4,128,512]{2,1,0:T(8,128)S(1)} collective-permute-done((f32[4,128,512]{2,1,0:T(8,128)S(1)}, f32[4,128,512]{2,1,0:T(8,128)S(1)}, u32[]{:S(2)}, u32[]{:S(2)}) %collective-permute-start.20) | collective-permute-done | bytes 1048608 | tf_op jit(solution)/shard_map/ppermute | solution.py:27
  142.8 2.8 %collective-permute-start.24 = (bf16[128,512]{1,0:T(8,128)(2,1)S(1)}, bf16[128,512]{1,0:T(8,128)(2,1)S(1)}, u32[]{:S(2)}, u32[]{:S(2)}) collective-permute-start(bf16[128,512]{1,0:T(8,128)(2,1)S(1)} %get-tuple-element.34), channel_id=1, source_target_pairs={{0,128},{2,0},{4,384},{6,256},{128,258},{130,130},{132,2},{134,386... | collective-permute-start | bytes 393224 | tf_op jit(solution)/shard_map/ppermute | solution.py:362
  145.5 6.4 %collective-permute-start.23 = (bf16[128,512]{1,0:T(8,128)(2,1)S(1)}, bf16[128,512]{1,0:T(8,128)(2,1)S(1)}, u32[]{:S(2)}, u32[]{:S(2)}) collective-permute-start(bf16[128,512]{1,0:T(8,128)(2,1)S(1)} %get-tuple-element.35), channel_id=1, source_target_pairs={{0,256},{2,128},{4,0},{6,384},{128,386},{130,258},{132,130},{134,2... | collective-permute-start | bytes 393224 | tf_op jit(solution)/shard_map/ppermute | solution.py:362
  151.9 1.9 %collective-permute-start.22 = (bf16[128,512]{1,0:T(8,128)(2,1)S(1)}, bf16[128,512]{1,0:T(8,128)(2,1)S(1)}, u32[]{:S(2)}, u32[]{:S(2)}) collective-permute-start(bf16[128,512]{1,0:T(8,128)(2,1)S(1)} %get-tuple-element.36), channel_id=1, source_target_pairs={{0,384},{2,256},{4,128},{6,0},{128,2},{130,386},{132,258},{134,130... | collective-permute-start | bytes 393224 | tf_op jit(solution)/shard_map/ppermute | solution.py:362
  153.9 1.9 %collective-permute-start.21 = (bf16[128,512]{1,0:T(8,128)(2,1)S(1)}, bf16[128,512]{1,0:T(8,128)(2,1)S(1)}, u32[]{:S(2)}, u32[]{:S(2)}) collective-permute-start(bf16[128,512]{1,0:T(8,128)(2,1)S(1)} %get-tuple-element.33), channel_id=1, source_target_pairs={{0,0},{2,384},{4,256},{6,128},{128,130},{130,2},{132,386},{134,258... | collective-permute-start | bytes 393224 | tf_op jit(solution)/shard_map/ppermute | solution.py:362
  156.5 8.4 %collective-permute-done.24 = bf16[128,512]{1,0:T(8,128)(2,1)S(1)} collective-permute-done((bf16[128,512]{1,0:T(8,128)(2,1)S(1)}, bf16[128,512]{1,0:T(8,128)(2,1)S(1)}, u32[]{:S(2)}, u32[]{:S(2)}) %collective-permute-start.24) | collective-permute-done | bytes 131104 | tf_op jit(solution)/shard_map/ppermute | solution.py:362
  164.9 17.7 %collective-permute-done.21 = bf16[128,512]{1,0:T(8,128)(2,1)S(1)} collective-permute-done((bf16[128,512]{1,0:T(8,128)(2,1)S(1)}, bf16[128,512]{1,0:T(8,128)(2,1)S(1)}, u32[]{:S(2)}, u32[]{:S(2)}) %collective-permute-start.21) | collective-permute-done | bytes 131104 | tf_op jit(solution)/shard_map/ppermute | solution.py:362
  (54 shorter events, 6.1 us)
Async XLA Ops:
  0.0 67.9 %copy-start.6 = (f32[128]{0:T(128)S(1)}, f32[128]{0:T(128)}, u32[]{:S(2)}) copy-start(f32[128]{0:T(128)} %param.10) | copy-start | bytes 1540
  0.8 26.5 %collective-permute-start.2 = (bf16[1,2,128,128]{3,2,1,0:T(8,128)(2,1)S(1)}, bf16[1,2,128,128]{3,2,1,0:T(8,128)(2,1)S(1)}, u32[]{:S(2)}, u32[]{:S(2)}) collective-permute-start(bf16[1,2,128,128]{3,2,1,0:T(8,128)(2,1)S(1)} %maximum_bitcast_fusion), channel_id=1, source_target_pairs={{0,0},{1,128},{128,1},{129,129},{64,64},{65,192},{192,65},{193,193... | collective-permute-start | bytes 196616 | tf_op jit(solution)/shard_map/ppermute | solution.py:285
  3.0 24.4 %collective-permute-start.3 = (bf16[1,2,128,128]{3,2,1,0:T(8,128)(2,1)S(1)}, bf16[1,2,128,128]{3,2,1,0:T(8,128)(2,1)S(1)}, u32[]{:S(2)}, u32[]{:S(2)}) collective-permute-start(bf16[1,2,128,128]{3,2,1,0:T(8,128)(2,1)S(1)} %maximum_bitcast_fusion), channel_id=1, source_target_pairs={{0,256},{1,384},{128,257},{129,385},{64,320},{65,448},{192,321},{1... | collective-permute-start | bytes 196616 | tf_op jit(solution)/shard_map/ppermute | solution.py:285
  6.3 21.1 %collective-permute-start.4 = (bf16[1,2,128,128]{3,2,1,0:T(8,128)(2,1)S(1)}, bf16[1,2,128,128]{3,2,1,0:T(8,128)(2,1)S(1)}, u32[]{:S(2)}, u32[]{:S(2)}) collective-permute-start(bf16[1,2,128,128]{3,2,1,0:T(8,128)(2,1)S(1)} %maximum_bitcast_fusion), channel_id=1, source_target_pairs={{0,64},{1,192},{128,65},{129,193},{64,0},{65,128},{192,1},{193,129... | collective-permute-start | bytes 196616 | tf_op jit(solution)/shard_map/ppermute | solution.py:285
  8.2 19.2 %collective-permute-start.5 = (bf16[1,2,128,128]{3,2,1,0:T(8,128)(2,1)S(1)}, bf16[1,2,128,128]{3,2,1,0:T(8,128)(2,1)S(1)}, u32[]{:S(2)}, u32[]{:S(2)}) collective-permute-start(bf16[1,2,128,128]{3,2,1,0:T(8,128)(2,1)S(1)} %maximum_bitcast_fusion), channel_id=1, source_target_pairs={{0,320},{1,448},{128,321},{129,449},{64,256},{65,384},{192,257},{1... | collective-permute-start | bytes 196616 | tf_op jit(solution)/shard_map/ppermute | solution.py:285
  19.0 35.3 %collective-permute-start = (bf16[144,1024]{1,0:T(8,128)(2,1)S(1)}, bf16[144,1024]{1,0:T(8,128)(2,1)S(1)}, u32[]{:S(2)}, u32[]{:S(2)}) collective-permute-start(bf16[144,1024]{1,0:T(8,128)(2,1)S(1)} %fusion.1), channel_id=1, source_target_pairs={{0,0},{1,128},{128,1},{129,129},{64,64},{65,192},{192,65},{193,193... | collective-permute-start | bytes 884744 | tf_op jit(solution)/shard_map/ppermute | solution.py:285
  22.8 9.1 %all-to-all-start = ((bf16[4,128,128]{2,1,0:T(8,128)(2,1)}), bf16[4,128,128]{2,1,0:T(8,128)(2,1)S(1)}, u32[]{:S(2)}, u32[]{:S(2)}) async-start(bf16[4,128,128]{2,1,0:T(8,128)(2,1)} %bitcast.11), calls=%async_computation | async-start | bytes 262144 | tf_op jit(solution)/shard_map/all_to_all | solution.py:288
  31.9 42.0 %copy-start.4 = (bf16[6,2,128,128]{3,2,1,0:T(8,128)(2,1)}, bf16[6,2,128,128]{3,2,1,0:T(8,128)(2,1)S(1)}, u32[]{:S(2)}) copy-start(bf16[6,2,128,128]{3,2,1,0:T(8,128)(2,1)S(1)} %get-tuple-element.38.refs_3_.refs_0_) | copy-start | bytes 1179652
  31.9 20.3 %collective-permute-start.6 = (bf16[6,2,128,128]{3,2,1,0:T(8,128)(2,1)S(1)}, bf16[6,2,128,128]{3,2,1,0:T(8,128)(2,1)S(1)}, u32[]{:S(2)}, u32[]{:S(2)}) collective-permute-start(bf16[6,2,128,128]{3,2,1,0:T(8,128)(2,1)S(1)} %get-tuple-element.38.refs_3_.refs_0_), channel_id=1, source_target_pairs={{0,8},{8,16},{16,24},{24,32},{32,40},{40,48},{48,56},{56,0},{1,9},... | collective-permute-start | bytes 1179656 | tf_op jit(solution)/shard_map/ppermute | solution.py:27
  36.3 20.0 %collective-permute-start.10 = (bf16[6,2,128,128]{3,2,1,0:T(8,128)(2,1)S(1)}, bf16[6,2,128,128]{3,2,1,0:T(8,128)(2,1)S(1)}, u32[]{:S(2)}, u32[]{:S(2)}) collective-permute-start(bf16[6,2,128,128]{3,2,1,0:T(8,128)(2,1)S(1)} %get-tuple-element.38.refs_3_.refs_0_), channel_id=1, source_target_pairs={{0,56},{8,0},{16,8},{24,16},{32,24},{40,32},{48,40},{56,48},{1,57}... | collective-permute-start | bytes 1179656 | tf_op jit(solution)/shard_map/ppermute | solution.py:27
  52.3 13.7 %collective-permute-start.7 = (bf16[6,2,128,128]{3,2,1,0:T(8,128)(2,1)S(1)}, bf16[6,2,128,128]{3,2,1,0:T(8,128)(2,1)S(1)}, u32[]{:S(2)}, u32[]{:S(2)}) collective-permute-start(bf16[6,2,128,128]{3,2,1,0:T(8,128)(2,1)S(1)} %collective-permute-done.6.refs_3_.refs_1_), channel_id=1, source_target_pairs={{0,8},{8,16},{16,24},{24,32},{32,40},{40,48},{48,56},{56,0},{1,9},... | collective-permute-start | bytes 1179656 | tf_op jit(solution)/shard_map/ppermute | solution.py:27
  54.4 13.5 %collective-permute-start.1 = (bf16[144,1024]{1,0:T(8,128)(2,1)S(1)}, bf16[144,1024]{1,0:T(8,128)(2,1)S(1)}, u32[]{:S(2)}, u32[]{:S(2)}) collective-permute-start(bf16[144,1024]{1,0:T(8,128)(2,1)S(1)} %collective-permute-done.refs_1_), channel_id=1, source_target_pairs={{0,1},{1,0},{2,3},{3,2},{4,5},{5,4},{6,7},{7,6},{8,9},{9,8},{10,11... | collective-permute-start | bytes 884744 | tf_op jit(solution)/shard_map/ppermute | solution.py:27
  56.3 17.7 %collective-permute-start.11 = (bf16[6,2,128,128]{3,2,1,0:T(8,128)(2,1)S(1)}, bf16[6,2,128,128]{3,2,1,0:T(8,128)(2,1)S(1)}, u32[]{:S(2)}, u32[]{:S(2)}) collective-permute-start(bf16[6,2,128,128]{3,2,1,0:T(8,128)(2,1)S(1)} %collective-permute-done.10.refs_4_.refs_2_), channel_id=1, source_target_pairs={{0,56},{8,0},{16,8},{24,16},{32,24},{40,32},{48,40},{56,48},{1,57}... | collective-permute-start | bytes 1179656 | tf_op jit(solution)/shard_map/ppermute | solution.py:27
  65.9 13.2 %collective-permute-start.8 = (bf16[6,2,128,128]{3,2,1,0:T(8,128)(2,1)S(1)}, bf16[6,2,128,128]{3,2,1,0:T(8,128)(2,1)S(1)}, u32[]{:S(2)}, u32[]{:S(2)}) collective-permute-start(bf16[6,2,128,128]{3,2,1,0:T(8,128)(2,1)S(1)} %collective-permute-done.7.refs_3_), channel_id=1, source_target_pairs={{0,8},{8,16},{16,24},{24,32},{32,40},{40,48},{48,56},{56,0},{1,9},... | collective-permute-start | bytes 1179656 | tf_op jit(solution)/shard_map/ppermute | solution.py:27
  73.9 12.9 %collective-permute-start.12 = (bf16[6,2,128,128]{3,2,1,0:T(8,128)(2,1)S(1)}, bf16[6,2,128,128]{3,2,1,0:T(8,128)(2,1)S(1)}, u32[]{:S(2)}, u32[]{:S(2)}) collective-permute-start(bf16[6,2,128,128]{3,2,1,0:T(8,128)(2,1)S(1)} %collective-permute-done.11.refs_4_), channel_id=1, source_target_pairs={{0,56},{8,0},{16,8},{24,16},{32,24},{40,32},{48,40},{56,48},{1,57}... | collective-permute-start | bytes 1179656 | tf_op jit(solution)/shard_map/ppermute | solution.py:27
  79.1 12.2 %collective-permute-start.9 = (bf16[6,2,128,128]{3,2,1,0:T(8,128)(2,1)S(1)}, bf16[6,2,128,128]{3,2,1,0:T(8,128)(2,1)S(1)}, u32[]{:S(2)}, u32[]{:S(2)}) collective-permute-start(bf16[6,2,128,128]{3,2,1,0:T(8,128)(2,1)S(1)} %collective-permute-done.8.refs_3_.refs_5_), channel_id=1, source_target_pairs={{0,8},{8,16},{16,24},{24,32},{32,40},{40,48},{48,56},{56,0},{1,9},... | collective-permute-start | bytes 1179656 | tf_op jit(solution)/shard_map/ppermute | solution.py:27
  81.1 34.8 %collective-permute-start.18 = (bf16[10,2,128,128]{3,2,1,0:T(8,128)(2,1)S(1)}, bf16[10,2,128,128]{3,2,1,0:T(8,128)(2,1)S(1)}, u32[]{:S(2)}, u32[]{:S(2)}) collective-permute-start(bf16[10,2,128,128]{3,2,1,0:T(8,128)(2,1)S(1)} %slice_dynamic-update-slice_fusion), channel_id=1, source_target_pairs={{0,64},{64,0},{1,65},{65,1},{2,66},{66,2},{3,67},{67,3},{4,68},{68... | collective-permute-start | bytes 1966088 | tf_op jit(solution)/shard_map/ppermute | solution.py:27
  86.9 8.1 %copy-start = (bf16[6,2,128,128]{3,2,1,0:T(8,128)(2,1)}, bf16[6,2,128,128]{3,2,1,0:T(8,128)(2,1)S(1)}, u32[]{:S(2)}) copy-start(bf16[6,2,128,128]{3,2,1,0:T(8,128)(2,1)S(1)} %collective-permute-done.12.refs_4_.refs_6_) | copy-start | bytes 1179652
  93.0 11.3 %collective-permute-start.13 = (f32[144,1024]{1,0:T(8,128)S(1)}, f32[144,1024]{1,0:T(8,128)S(1)}, u32[]{:S(2)}, u32[]{:S(2)}) collective-permute-start(f32[144,1024]{1,0:T(8,128)S(1)} %shard_map.78), channel_id=1, source_target_pairs={{0,1},{1,0},{2,3},{3,2},{4,5},{5,4},{6,7},{7,6},{8,9},{9,8},{10,11... | collective-permute-start | bytes 1769480 | tf_op jit(solution)/shard_map/ppermute | solution.py:27
  95.8 36.9 %collective-permute-start.19 = (bf16[6,2,128,128]{3,2,1,0:T(8,128)(2,1)}, bf16[6,2,128,128]{3,2,1,0:T(8,128)(2,1)}, u32[]{:S(2)}, u32[]{:S(2)}) collective-permute-start(bf16[6,2,128,128]{3,2,1,0:T(8,128)(2,1)} %pad_maximum_fusion), channel_id=1, source_target_pairs={{0,64},{64,0},{1,65},{65,1},{2,66},{66,2},{3,67},{67,3},{4,68},{68... | collective-permute-start | bytes 1179656 | tf_op jit(solution)/shard_map/ppermute | solution.py:27
  105.3 31.9 %collective-permute-start.14 = (bf16[128,1024]{1,0:T(8,128)(2,1)}, bf16[128,1024]{1,0:T(8,128)(2,1)S(1)}, u32[]{:S(2)}, u32[]{:S(2)}) collective-permute-start(bf16[128,1024]{1,0:T(8,128)(2,1)} %shard_map.79), channel_id=1, source_target_pairs={{0,0},{1,128},{128,129},{129,257},{256,256},{257,384},{384,385},{3... | collective-permute-start | bytes 786440 | tf_op jit(solution)/shard_map/ppermute | solution.py:342
  107.4 29.8 %collective-permute-start.15 = (bf16[128,1024]{1,0:T(8,128)(2,1)}, bf16[128,1024]{1,0:T(8,128)(2,1)S(1)}, u32[]{:S(2)}, u32[]{:S(2)}) collective-permute-start(bf16[128,1024]{1,0:T(8,128)(2,1)} %shard_map.79), channel_id=1, source_target_pairs={{0,128},{1,256},{128,257},{129,385},{256,384},{257,0},{384,1},{385... | collective-permute-start | bytes 786440 | tf_op jit(solution)/shard_map/ppermute | solution.py:342
  111.4 25.8 %collective-permute-start.16 = (bf16[128,1024]{1,0:T(8,128)(2,1)}, bf16[128,1024]{1,0:T(8,128)(2,1)S(1)}, u32[]{:S(2)}, u32[]{:S(2)}) collective-permute-start(bf16[128,1024]{1,0:T(8,128)(2,1)} %shard_map.79), channel_id=1, source_target_pairs={{0,256},{1,384},{128,385},{129,1},{256,0},{257,128},{384,129},{385... | collective-permute-start | bytes 786440 | tf_op jit(solution)/shard_map/ppermute | solution.py:342
  115.9 0.9 copy-start.2
  116.7 20.5 %collective-permute-start.17 = (bf16[128,1024]{1,0:T(8,128)(2,1)}, bf16[128,1024]{1,0:T(8,128)(2,1)S(1)}, u32[]{:S(2)}, u32[]{:S(2)}) collective-permute-start(bf16[128,1024]{1,0:T(8,128)(2,1)} %shard_map.79), channel_id=1, source_target_pairs={{0,384},{1,0},{128,1},{129,129},{256,128},{257,256},{384,257},{385... | collective-permute-start | bytes 786440 | tf_op jit(solution)/shard_map/ppermute | solution.py:342
  132.8 1.0 copy-start.1
  133.8 1.1 copy-start.3
  134.8 1.0 copy-start.5
  138.0 4.6 %collective-permute-start.20 = (f32[4,128,512]{2,1,0:T(8,128)S(1)}, f32[4,128,512]{2,1,0:T(8,128)S(1)}, u32[]{:S(2)}, u32[]{:S(2)}) collective-permute-start(f32[4,128,512]{2,1,0:T(8,128)S(1)} %shard_map.82), channel_id=1, source_target_pairs={{0,1},{1,0},{2,3},{3,2},{4,5},{5,4},{6,7},{7,6},{8,9},{9,8},{10,11... | collective-permute-start | bytes 3145736 | tf_op jit(solution)/shard_map/ppermute | solution.py:27
  142.8 22.1 %collective-permute-start.24 = (bf16[128,512]{1,0:T(8,128)(2,1)S(1)}, bf16[128,512]{1,0:T(8,128)(2,1)S(1)}, u32[]{:S(2)}, u32[]{:S(2)}) collective-permute-start(bf16[128,512]{1,0:T(8,128)(2,1)S(1)} %get-tuple-element.34), channel_id=1, source_target_pairs={{0,128},{2,0},{4,384},{6,256},{128,258},{130,130},{132,2},{134,386... | collective-permute-start | bytes 393224 | tf_op jit(solution)/shard_map/ppermute | solution.py:362
  145.5 19.3 %collective-permute-start.23 = (bf16[128,512]{1,0:T(8,128)(2,1)S(1)}, bf16[128,512]{1,0:T(8,128)(2,1)S(1)}, u32[]{:S(2)}, u32[]{:S(2)}) collective-permute-start(bf16[128,512]{1,0:T(8,128)(2,1)S(1)} %get-tuple-element.35), channel_id=1, source_target_pairs={{0,256},{2,128},{4,0},{6,384},{128,386},{130,258},{132,130},{134,2... | collective-permute-start | bytes 393224 | tf_op jit(solution)/shard_map/ppermute | solution.py:362
  151.9 12.9 %collective-permute-start.22 = (bf16[128,512]{1,0:T(8,128)(2,1)S(1)}, bf16[128,512]{1,0:T(8,128)(2,1)S(1)}, u32[]{:S(2)}, u32[]{:S(2)}) collective-permute-start(bf16[128,512]{1,0:T(8,128)(2,1)S(1)} %get-tuple-element.36), channel_id=1, source_target_pairs={{0,384},{2,256},{4,128},{6,0},{128,2},{130,386},{132,258},{134,130... | collective-permute-start | bytes 393224 | tf_op jit(solution)/shard_map/ppermute | solution.py:362
  153.9 28.7 %collective-permute-start.21 = (bf16[128,512]{1,0:T(8,128)(2,1)S(1)}, bf16[128,512]{1,0:T(8,128)(2,1)S(1)}, u32[]{:S(2)}, u32[]{:S(2)}) collective-permute-start(bf16[128,512]{1,0:T(8,128)(2,1)S(1)} %get-tuple-element.33), channel_id=1, source_target_pairs={{0,0},{2,384},{4,256},{6,128},{128,130},{130,2},{132,386},{134,258... | collective-permute-start | bytes 393224 | tf_op jit(solution)/shard_map/ppermute | solution.py:362

commit v3 on v2

--- a/solution.py
+++ b/solution.py
@@ -204,35 +204,29 @@
 
 
 def assemble_kernel(at_ref, *refs):
-    chunks, first_ref, second_ref, out_ref = refs[:8], refs[8], refs[9], refs[10]
+    chunks, out_ref = refs[:8], refs[8]
     for p in range(8):
         for y in range(2):
-            if y == 0:
-                source, base = chunks[p], BLOCKS
-            elif p < 5:
-                source, base = first_ref, 2 * p
-            else:
-                source, base = second_ref, 2 * (p - 5)
-            slot = at_ref[2 * p + y]
             for x in range(4):
-                block = source[base + x // 2, x % 2]
+                tile = x * 2 + y
+                block = chunks[p][BLOCKS + tile // 2, tile % 2]
                 for t in range(8):
-                    out_ref[x, slot, :, t * 128 : (t + 1) * 128] = block[
+                    out_ref[x, y * 8 + at_ref[p], :, t * 128 : (t + 1) * 128] = block[
                         t * 16 : (t + 1) * 16
                     ]
 
 
-def assemble(at, chunks, first, second):
+def assemble(at, chunks):
     return pl.pallas_call(
         assemble_kernel,
         out_shape=jax.ShapeDtypeStruct((4, 16, 16, 1024), jnp.bfloat16),
-        in_specs=[SMEM] + [VMEM] * 10,
+        in_specs=[SMEM] + [VMEM] * 8,
         out_specs=VMEM,
         cost_estimate=pl.CostEstimate(
             flops=0, bytes_accessed=4 << 20, transcendentals=0
         ),
         compiler_params=pltpu.CompilerParams(vmem_limit_bytes=16 << 20),
-    )(at, *chunks, first, second)
+    )(at, *chunks)
 
 
 def project_kernel(col_ref, turn_ref, a0, a1, a2, a3, w_ref, out_ref):
@@ -284,9 +278,10 @@
                         pairs.append((source, (x * 2 + (y + dy) % 2) * 2 + a))
         return lax.ppermute(value, ("x", "yh", "c"), pairs)
 
-    quarter = output_weight[0].reshape(16, 4, 8, 128).transpose(1, 2, 0, 3)
+    quarter = output_weight[0].reshape(16, 4, 1, 8, 128).transpose(1, 2, 3, 0, 4)
+    quarter = jnp.broadcast_to(quarter, (4, 2, 8, 16, 128)).reshape(1024, 128)
     quarter = lax.all_to_all(
-        quarter.reshape(512, 128), "x", split_axis=0, concat_axis=0, tiled=True
+        quarter, ("x", "yh"), split_axis=0, concat_axis=0, tiled=True
     )
     own = jnp.stack([keys, values])[None]
     chunk = jnp.concatenate(
@@ -295,7 +290,7 @@
             trade(own, di=1),
             trade(own, dy=1),
             trade(own, di=1, dy=1),
-            quarter.reshape(2, 2, 128, 128),
+            quarter.reshape(4, 2, 128, 128),
         ]
     )
     block_x = 2 * (ax // 2) + core
@@ -341,27 +336,21 @@
         ]
         slots.append(lax.ppermute(attended, ("x", "c"), pairs))
     parts = [chunk, right[1], left[1], right[2], left[2], right[3], left[3], right[4]]
-    first = shift(jnp.concatenate([c[BLOCKS:] for c in parts[:5]]), "yh", 1)
-    second = shift(jnp.concatenate([c[BLOCKS:] for c in parts[5:]]), "yh", 1)
-    at = jnp.stack(
-        [((ay + dy) % 2) * 8 + (az + h) % 8 for h in hops for dy in (0, 1)]
-    ).astype(jnp.int32)
-    weight = assemble(at, parts, first, second)
+    at = jnp.stack([(az + h) % 8 for h in hops]).astype(jnp.int32)
+    weight = assemble(at, parts)
 
     core = core.astype(jnp.int32)[None]
     turn = (core + 4 - lax.axis_index("yl")) % 4
     for_other = project(1 - core, turn, slots, weight)
     from_other = shift(for_other, "c", 1)
     for_own = project(core, turn, slots, weight)
-    combined = None
-    for s in range(4):
-        pairs = [
-            (x * 4 + y, ((x - y - s) % 4) * 4 + x) for x in range(4) for y in range(4)
-        ]
+    combined = for_own[0] + from_other[0]
+    for s in range(1, 4):
         part = (for_own[s] + from_other[s]).astype(jnp.bfloat16)
-        part = lax.ppermute(part, ("x", "yl"), pairs).astype(jnp.float32)
-        combined = part if combined is None else combined + part
-    return (jnp.tanh(attn_gate[0]) * combined).astype(jnp.bfloat16)
+        combined = combined + shift(part, "yl", s).astype(jnp.float32)
+    result = (jnp.tanh(attn_gate[0]) * combined).astype(jnp.bfloat16)
+    pairs = [(x * 4 + y, ((x - y) % 4) * 4 + x) for x in range(4) for y in range(4)]
+    return lax.ppermute(result, ("x", "yl"), pairs)
 
 
 def solution(mesh):

time: 185 us -> 177 us (0.957)
  the two profiles are of different devices: /device:TPU:38 before, /device:TPU:7 now
where the time goes in v3:
time: 177 us; the launch traced here: 176 us
  starting transfers between devices  93.3 us (53%)
  waiting for transfers between devices  54 us (31%)
  Pallas kernels  20.9 us (12%)
  local copies, waits for them, and re-layouts  4.65 us (3%)
    ppermute x13, starting transfers between devices, shift(): lax.ppermute(value, axis, [(s, (s + steps) % count) for s in range(count)])  55.8 us
    ppermute x13, waiting for transfers between devices, shift(): lax.ppermute(value, axis, [(s, (s + steps) % count) for s in range(count)])  28 us
    pallas_call x6, Pallas kernels, attend(): pl.pallas_call(body, out_shape=out_shape, in_specs=[SMEM] + [VMEM] * (2 +...  17.7 us
    ppermute x5, starting transfers between devices, trade(): return lax.ppermute(value, ('x', 'yh', 'c'), pairs)  15.1 us
    ppermute x1, waiting for transfers between devices, work(): return lax.ppermute(result, ('x', 'yl'), pairs)  13 us
    all_to_all x1, starting transfers between devices, work(): lax.all_to_all(quarter, ('x', 'yh'), split_axis=0, concat_axis=0, tiled=T...  12.2 us
    ppermute x5, waiting for transfers between devices, trade(): return lax.ppermute(value, ('x', 'yh', 'c'), pairs)  8.26 us
    ppermute x4, starting transfers between devices, work(): slots.append(lax.ppermute(attended, ('x', 'c'), pairs))  8.23 us
  transfers between devices with their start and end apart: 24, of which 7 were waited for; matrix products, arithmetic and copies ran while one was open for 1% of the time, Pallas kernels for 10%

profile of v3, /device:TPU:7, one launch (start us, length us, event | category | flops | bytes accessed | tf_op | source)
XLA Modules:
  0.0 175.5 jit_solution(9401644629386338814)
XLA Ops:
  0.0 0.8 maximum_bitcast_fusion
  0.8 0.7 collective-permute-start.2
  1.5 0.9 copy.9
  2.5 0.7 broadcast_in_dim.19
  3.2 12.2 %all-to-all-start = ((bf16[8,128,128]{2,1,0:T(8,128)(2,1)}), bf16[8,128,128]{2,1,0:T(8,128)(2,1)S(1)}, u32[]{:S(2)}, u32[]{:S(2)}) async-start(bf16[8,128,128]{2,1,0:T(8,128)(2,1)} %bitcast.12), calls=%async_computation | async-start | bytes 524288 | tf_op jit(solution)/shard_map/all_to_all | solution.py:283
  15.4 3.1 %collective-permute-start.3 = (bf16[1,2,128,128]{3,2,1,0:T(8,128)(2,1)S(1)}, bf16[1,2,128,128]{3,2,1,0:T(8,128)(2,1)S(1)}, u32[]{:S(2)}, u32[]{:S(2)}) collective-permute-start(bf16[1,2,128,128]{3,2,1,0:T(8,128)(2,1)S(1)} %maximum_bitcast_fusion), channel_id=1, source_target_pairs={{0,256},{1,384},{128,257},{129,385},{64,320},{65,448},{192,321},{1... | collective-permute-start | bytes 196616 | tf_op jit(solution)/shard_map/ppermute | solution.py:279
  18.5 7.0 %collective-permute-start.4 = (bf16[1,2,128,128]{3,2,1,0:T(8,128)(2,1)S(1)}, bf16[1,2,128,128]{3,2,1,0:T(8,128)(2,1)S(1)}, u32[]{:S(2)}, u32[]{:S(2)}) collective-permute-start(bf16[1,2,128,128]{3,2,1,0:T(8,128)(2,1)S(1)} %maximum_bitcast_fusion), channel_id=1, source_target_pairs={{0,64},{1,192},{128,65},{129,193},{64,0},{65,128},{192,1},{193,129... | collective-permute-start | bytes 196616 | tf_op jit(solution)/shard_map/ppermute | solution.py:279
  25.5 3.7 %collective-permute-start.5 = (bf16[1,2,128,128]{3,2,1,0:T(8,128)(2,1)S(1)}, bf16[1,2,128,128]{3,2,1,0:T(8,128)(2,1)S(1)}, u32[]{:S(2)}, u32[]{:S(2)}) collective-permute-start(bf16[1,2,128,128]{3,2,1,0:T(8,128)(2,1)S(1)} %maximum_bitcast_fusion), channel_id=1, source_target_pairs={{0,320},{1,448},{128,321},{129,449},{64,256},{65,384},{192,257},{1... | collective-permute-start | bytes 196616 | tf_op jit(solution)/shard_map/ppermute | solution.py:279
  29.3 8.2 %collective-permute-done.5 = bf16[1,2,128,128]{3,2,1,0:T(8,128)(2,1)S(1)} collective-permute-done((bf16[1,2,128,128]{3,2,1,0:T(8,128)(2,1)S(1)}, bf16[1,2,128,128]{3,2,1,0:T(8,128)(2,1)S(1)}, u32[]{:S(2)}, u32[]{:S(2)}) %collective-permute-start.5) | collective-permute-done | bytes 65568 | tf_op jit(solution)/shard_map/ppermute | solution.py:279
  37.6 4.0 %collective-permute-start.6 = (bf16[8,2,128,128]{3,2,1,0:T(8,128)(2,1)S(1)}, bf16[8,2,128,128]{3,2,1,0:T(8,128)(2,1)S(1)}, u32[]{:S(2)}, u32[]{:S(2)}) collective-permute-start(bf16[8,2,128,128]{3,2,1,0:T(8,128)(2,1)S(1)} %constant_dynamic-update-slice_fusion.refs_3_.refs_0_), channel_id=1, source_target_pairs={{0,8},{8,16},{16,24},{24,32},{32,40},{40,48},{48,56},{56,0},{1,9},... | collective-permute-start | bytes 1572872 | tf_op jit(solution)/shard_map/ppermute | solution.py:27
  41.6 8.6 %collective-permute-start.10 = (bf16[8,2,128,128]{3,2,1,0:T(8,128)(2,1)S(1)}, bf16[8,2,128,128]{3,2,1,0:T(8,128)(2,1)S(1)}, u32[]{:S(2)}, u32[]{:S(2)}) collective-permute-start(bf16[8,2,128,128]{3,2,1,0:T(8,128)(2,1)S(1)} %constant_dynamic-update-slice_fusion.refs_3_.refs_0_), channel_id=1, source_target_pairs={{0,56},{8,0},{16,8},{24,16},{32,24},{40,32},{48,40},{56,48},{1,57}... | collective-permute-start | bytes 1572872 | tf_op jit(solution)/shard_map/ppermute | solution.py:27
  50.2 9.6 %collective-permute-done.6.refs_3_.refs_1_ = bf16[8,2,128,128]{3,2,1,0:T(8,128)(2,1)S(1)} collective-permute-done((bf16[8,2,128,128]{3,2,1,0:T(8,128)(2,1)S(1)}, bf16[8,2,128,128]{3,2,1,0:T(8,128)(2,1)S(1)}, u32[]{:S(2)}, u32[]{:S(2)}) %collective-permute-start.6) | collective-permute-done | bytes 524320 | tf_op jit(solution)/shard_map/ppermute | solution.py:27
  59.9 1.9 %collective-permute-start.7 = (bf16[8,2,128,128]{3,2,1,0:T(8,128)(2,1)S(1)}, bf16[8,2,128,128]{3,2,1,0:T(8,128)(2,1)S(1)}, u32[]{:S(2)}, u32[]{:S(2)}) collective-permute-start(bf16[8,2,128,128]{3,2,1,0:T(8,128)(2,1)S(1)} %collective-permute-done.6.refs_3_.refs_1_), channel_id=1, source_target_pairs={{0,8},{8,16},{16,24},{24,32},{32,40},{40,48},{48,56},{56,0},{1,9},... | collective-permute-start | bytes 1572872 | tf_op jit(solution)/shard_map/ppermute | solution.py:27
  61.8 4.8 %collective-permute-start.11 = (bf16[8,2,128,128]{3,2,1,0:T(8,128)(2,1)S(1)}, bf16[8,2,128,128]{3,2,1,0:T(8,128)(2,1)}, u32[]{:S(2)}, u32[]{:S(2)}) collective-permute-start(bf16[8,2,128,128]{3,2,1,0:T(8,128)(2,1)S(1)} %collective-permute-done.10.refs_4_.refs_2_), channel_id=1, source_target_pairs={{0,56},{8,0},{16,8},{24,16},{32,24},{40,32},{48,40},{56,48},{1,57}... | collective-permute-start | bytes 1572872 | tf_op jit(solution)/shard_map/ppermute | solution.py:27
  66.7 9.7 %collective-permute-done.7.refs_3_ = bf16[8,2,128,128]{3,2,1,0:T(8,128)(2,1)S(1)} collective-permute-done((bf16[8,2,128,128]{3,2,1,0:T(8,128)(2,1)S(1)}, bf16[8,2,128,128]{3,2,1,0:T(8,128)(2,1)S(1)}, u32[]{:S(2)}, u32[]{:S(2)}) %collective-permute-start.7) | collective-permute-done | bytes 524320 | tf_op jit(solution)/shard_map/ppermute | solution.py:27
  76.4 1.9 %collective-permute-start.8 = (bf16[8,2,128,128]{3,2,1,0:T(8,128)(2,1)S(1)}, bf16[8,2,128,128]{3,2,1,0:T(8,128)(2,1)}, u32[]{:S(2)}, u32[]{:S(2)}) collective-permute-start(bf16[8,2,128,128]{3,2,1,0:T(8,128)(2,1)S(1)} %collective-permute-done.7.refs_3_), channel_id=1, source_target_pairs={{0,8},{8,16},{16,24},{24,32},{32,40},{40,48},{48,56},{56,0},{1,9},... | collective-permute-start | bytes 1572872 | tf_op jit(solution)/shard_map/ppermute | solution.py:27
  78.3 0.7 collective-permute-start
  79.3 9.9 %collective-permute-start.1 = (bf16[144,1024]{1,0:T(8,128)(2,1)S(1)}, bf16[144,1024]{1,0:T(8,128)(2,1)S(1)}, u32[]{:S(2)}, u32[]{:S(2)}) collective-permute-start(bf16[144,1024]{1,0:T(8,128)(2,1)S(1)} %collective-permute-done.refs_1_), channel_id=1, source_target_pairs={{0,1},{1,0},{2,3},{3,2},{4,5},{5,4},{6,7},{7,6},{8,9},{9,8},{10,11... | collective-permute-start | bytes 884744 | tf_op jit(solution)/shard_map/ppermute | solution.py:27
  89.2 4.9 %collective-permute-start.12 = (bf16[8,2,128,128]{3,2,1,0:T(8,128)(2,1)}, bf16[8,2,128,128]{3,2,1,0:T(8,128)(2,1)S(1)}, u32[]{:S(2)}, u32[]{:S(2)}) collective-permute-start(bf16[8,2,128,128]{3,2,1,0:T(8,128)(2,1)} %collective-permute-done.11.refs_4_), channel_id=1, source_target_pairs={{0,56},{8,0},{16,8},{24,16},{32,24},{40,32},{48,40},{56,48},{1,57}... | collective-permute-start | bytes 1572872 | tf_op jit(solution)/shard_map/ppermute | solution.py:27
  94.2 1.9 %collective-permute-start.9 = (bf16[8,2,128,128]{3,2,1,0:T(8,128)(2,1)}, bf16[8,2,128,128]{3,2,1,0:T(8,128)(2,1)S(1)}, u32[]{:S(2)}, u32[]{:S(2)}) collective-permute-start(bf16[8,2,128,128]{3,2,1,0:T(8,128)(2,1)} %collective-permute-done.8.refs_3_.refs_5_), channel_id=1, source_target_pairs={{0,8},{8,16},{16,24},{24,32},{32,40},{40,48},{48,56},{56,0},{1,9},... | collective-permute-start | bytes 1572872 | tf_op jit(solution)/shard_map/ppermute | solution.py:27
  96.2 2.4 %shard_map.73 = (bf16[2048,128]{1,0:T(8,128)(2,1)S(1)}, f32[1,2048]{1,0:T(1,128)S(1)}, f32[8,2048]{1,0:T(8,128)S(1)}, f32[128,2048]{1,0:T(8,128)S(1)}) custom-call(s32[4]{0:T(128)S(1)} %get-tuple-element.41.refs_0_, bf16[144,1024]{1,0:T(8,128)(2,1)S(1)} %collective-permute-done.refs_1_, bf16[144,1024]{1,0:T(8,128)(2,1)S(1)} %collective-permute-done.1.refs_2_, ...), custom_call_target="tpu_custom_call" | custom-call | flops 536870912 | bytes 3407872 | tf_op jit(solution)/shard_map/pallas_call | solution.py:163
  98.7 3.6 %shard_map.74 = (f32[1,2048]{1,0:T(1,128)S(1)}, f32[8,2048]{1,0:T(8,128)S(1)}, f32[128,2048]{1,0:T(8,128)S(1)}) custom-call(s32[8]{0:T(128)S(1)} %pad_add_fusion.3.refs_0_, bf16[144,1024]{1,0:T(8,128)(2,1)S(1)} %collective-permute-done.refs_1_, bf16[144,1024]{1,0:T(8,128)(2,1)S(1)} %collective-permute-done.1.refs_2_, ...), custom_call_target="tpu_custom_call" | custom-call | flops 1073741824 | bytes 3670016 | tf_op jit(solution)/shard_map/pallas_call | solution.py:163
  102.3 4.1 %shard_map.75 = (f32[1,2048]{1,0:T(1,128)S(1)}, f32[8,2048]{1,0:T(8,128)S(1)}, f32[128,2048]{1,0:T(8,128)S(1)}) custom-call(s32[8]{0:T(128)S(1)} %pad_add_fusion.2.refs_0_, bf16[144,1024]{1,0:T(8,128)(2,1)S(1)} %collective-permute-done.refs_1_, bf16[144,1024]{1,0:T(8,128)(2,1)S(1)} %collective-permute-done.1.refs_2_, ...), custom_call_target="tpu_custom_call" | custom-call | flops 1073741824 | bytes 3670016 | tf_op jit(solution)/shard_map/pallas_call | solution.py:163
  106.4 4.3 %shard_map.76 = (f32[1,2048]{1,0:T(1,128)S(1)}, f32[8,2048]{1,0:T(8,128)S(1)}, f32[128,2048]{1,0:T(8,128)S(1)}) custom-call(s32[8]{0:T(128)S(1)} %pad_add_fusion.1.refs_0_, bf16[144,1024]{1,0:T(8,128)(2,1)S(1)} %collective-permute-done.refs_1_, bf16[144,1024]{1,0:T(8,128)(2,1)S(1)} %collective-permute-done.1.refs_2_, ...), custom_call_target="tpu_custom_call" | custom-call | flops 1073741824 | bytes 3670016 | tf_op jit(solution)/shard_map/pallas_call | solution.py:163
  110.7 1.6 shard_map.78
  112.4 3.2 %collective-permute-start.13 = (f32[144,1024]{1,0:T(8,128)S(1)}, f32[144,1024]{1,0:T(8,128)S(1)}, u32[]{:S(2)}, u32[]{:S(2)}) collective-permute-start(f32[144,1024]{1,0:T(8,128)S(1)} %shard_map.78), channel_id=1, source_target_pairs={{0,1},{1,0},{2,3},{3,2},{4,5},{5,4},{6,7},{7,6},{8,9},{9,8},{10,11... | collective-permute-start | bytes 1769480 | tf_op jit(solution)/shard_map/ppermute | solution.py:27
  115.5 1.6 shard_map.77.a_ref
  117.2 0.2 shard_map.79
  117.4 2.4 %collective-permute-start.14 = (bf16[128,1024]{1,0:T(8,128)(2,1)S(1)}, bf16[128,1024]{1,0:T(8,128)(2,1)S(1)}, u32[]{:S(2)}, u32[]{:S(2)}) collective-permute-start(bf16[128,1024]{1,0:T(8,128)(2,1)S(1)} %shard_map.79), channel_id=1, source_target_pairs={{0,0},{1,128},{128,129},{129,257},{256,256},{257,384},{384,385},{3... | collective-permute-start | bytes 786440 | tf_op jit(solution)/shard_map/ppermute | solution.py:337
  119.8 3.2 %collective-permute-start.15 = (bf16[128,1024]{1,0:T(8,128)(2,1)S(1)}, bf16[128,1024]{1,0:T(8,128)(2,1)S(1)}, u32[]{:S(2)}, u32[]{:S(2)}) collective-permute-start(bf16[128,1024]{1,0:T(8,128)(2,1)S(1)} %shard_map.79), channel_id=1, source_target_pairs={{0,128},{1,256},{128,257},{129,385},{256,384},{257,0},{384,1},{385... | collective-permute-start | bytes 786440 | tf_op jit(solution)/shard_map/ppermute | solution.py:337
  123.0 1.9 %collective-permute-start.16 = (bf16[128,1024]{1,0:T(8,128)(2,1)S(1)}, bf16[128,1024]{1,0:T(8,128)(2,1)S(1)}, u32[]{:S(2)}, u32[]{:S(2)}) collective-permute-start(bf16[128,1024]{1,0:T(8,128)(2,1)S(1)} %shard_map.79), channel_id=1, source_target_pairs={{0,256},{1,384},{128,385},{129,1},{256,0},{257,128},{384,129},{385... | collective-permute-start | bytes 786440 | tf_op jit(solution)/shard_map/ppermute | solution.py:337
  125.0 0.7 collective-permute-start.17
  125.8 1.0 copy-done.1
  126.8 1.0 copy-done.3
  127.8 1.6 shard_map.80.w_ref
  129.4 4.7 %collective-permute-done.16.a2 = bf16[128,1024]{1,0:T(8,128)(2,1)S(1)} collective-permute-done((bf16[128,1024]{1,0:T(8,128)(2,1)S(1)}, bf16[128,1024]{1,0:T(8,128)(2,1)S(1)}, u32[]{:S(2)}, u32[]{:S(2)}) %collective-permute-start.16) | collective-permute-done | bytes 262176 | tf_op jit(solution)/shard_map/ppermute | solution.py:337
  134.2 0.7 shard_map.82
  134.9 5.9 %collective-permute-start.18 = (f32[4,128,512]{2,1,0:T(8,128)S(1)}, f32[4,128,512]{2,1,0:T(8,128)S(1)}, u32[]{:S(2)}, u32[]{:S(2)}) collective-permute-start(f32[4,128,512]{2,1,0:T(8,128)S(1)} %shard_map.82), channel_id=1, source_target_pairs={{0,1},{1,0},{2,3},{3,2},{4,5},{5,4},{6,7},{7,6},{8,9},{9,8},{10,11... | collective-permute-start | bytes 3145736 | tf_op jit(solution)/shard_map/ppermute | solution.py:27
  140.7 0.7 shard_map.81
  141.5 1.6 collective-permute-done.18
  143.0 0.2 fusion.11
  143.2 2.5 %collective-permute-start.21 = (bf16[128,512]{1,0:T(8,128)(2,1)S(1)}, bf16[128,512]{1,0:T(8,128)(2,1)S(1)}, u32[]{:S(2)}, u32[]{:S(2)}) collective-permute-start(bf16[128,512]{1,0:T(8,128)(2,1)S(1)} %get-tuple-element.34), channel_id=1, source_target_pairs={{0,6},{2,0},{4,2},{6,4},{1,7},{3,1},{5,3},{7,5},{8,14},{10,8},{12,... | collective-permute-start | bytes 393224 | tf_op jit(solution)/shard_map/ppermute | solution.py:27
  145.7 4.4 %collective-permute-start.20 = (bf16[128,512]{1,0:T(8,128)(2,1)S(1)}, bf16[128,512]{1,0:T(8,128)(2,1)S(1)}, u32[]{:S(2)}, u32[]{:S(2)}) collective-permute-start(bf16[128,512]{1,0:T(8,128)(2,1)S(1)} %get-tuple-element.35), channel_id=1, source_target_pairs={{0,4},{2,6},{4,0},{6,2},{1,5},{3,7},{5,1},{7,3},{8,12},{10,14},{12... | collective-permute-start | bytes 393224 | tf_op jit(solution)/shard_map/ppermute | solution.py:27
  150.2 1.9 %collective-permute-start.19 = (bf16[128,512]{1,0:T(8,128)(2,1)S(1)}, bf16[128,512]{1,0:T(8,128)(2,1)S(1)}, u32[]{:S(2)}, u32[]{:S(2)}) collective-permute-start(bf16[128,512]{1,0:T(8,128)(2,1)S(1)} %get-tuple-element.33), channel_id=1, source_target_pairs={{0,2},{2,4},{4,6},{6,0},{1,3},{3,5},{5,7},{7,1},{8,10},{10,12},{12... | collective-permute-start | bytes 393224 | tf_op jit(solution)/shard_map/ppermute | solution.py:27
  152.8 7.1 %collective-permute-done.20 = bf16[128,512]{1,0:T(8,128)(2,1)S(1)} collective-permute-done((bf16[128,512]{1,0:T(8,128)(2,1)S(1)}, bf16[128,512]{1,0:T(8,128)(2,1)S(1)}, u32[]{:S(2)}, u32[]{:S(2)}) %collective-permute-start.20) | collective-permute-done | bytes 131104 | tf_op jit(solution)/shard_map/ppermute | solution.py:27
  160.0 1.9 %collective-permute-start.22 = (bf16[128,512]{1,0:T(8,128)(2,1)S(1)}, bf16[128,512]{1,0:T(8,128)(2,1)S(1)}, u32[]{:S(2)}, u32[]{:S(2)}) collective-permute-start(bf16[128,512]{1,0:T(8,128)(2,1)S(1)} %fusion.10), channel_id=1, source_target_pairs={{0,0},{2,384},{4,256},{6,128},{128,130},{130,2},{132,386},{134,258... | collective-permute-start | bytes 393224 | tf_op jit(solution)/shard_map/ppermute | solution.py:353
  161.9 13.0 %collective-permute-done.22 = bf16[128,512]{1,0:T(8,128)(2,1)S(1)} collective-permute-done((bf16[128,512]{1,0:T(8,128)(2,1)S(1)}, bf16[128,512]{1,0:T(8,128)(2,1)S(1)}, u32[]{:S(2)}, u32[]{:S(2)}) %collective-permute-start.22) | collective-permute-done | bytes 131104 | tf_op jit(solution)/shard_map/ppermute | solution.py:353
  174.9 0.7 copy.16
  (44 shorter events, 0.7 us)
Async XLA Ops:
  0.0 66.6 %copy-start.6 = (s32[2,128]{1,0:T(2,128)S(1)}, s32[2,128]{1,0:T(2,128)}, u32[]{:S(2)}) copy-start(s32[2,128]{1,0:T(2,128)} %param.11) | copy-start | bytes 3076
  0.0 78.3 %copy-start.5 = (bf16[128,1024]{1,0:T(8,128)(2,1)S(1)}, bf16[128,1024]{1,0:T(8,128)(2,1)}, u32[]{:S(2)}) copy-start(bf16[128,1024]{1,0:T(8,128)(2,1)} %param.7) | copy-start | bytes 786436
  0.0 96.2 %copy-start.4 = (f32[128]{0:T(128)S(1)}, f32[128]{0:T(128)}, u32[]{:S(2)}) copy-start(f32[128]{0:T(128)} %param.10) | copy-start | bytes 1540
  0.8 28.4 %collective-permute-start.2 = (bf16[1,2,128,128]{3,2,1,0:T(8,128)(2,1)S(1)}, bf16[1,2,128,128]{3,2,1,0:T(8,128)(2,1)S(1)}, u32[]{:S(2)}, u32[]{:S(2)}) collective-permute-start(bf16[1,2,128,128]{3,2,1,0:T(8,128)(2,1)S(1)} %maximum_bitcast_fusion), channel_id=1, source_target_pairs={{0,0},{1,128},{128,1},{129,129},{64,64},{65,192},{192,65},{193,193... | collective-permute-start | bytes 196616 | tf_op jit(solution)/shard_map/ppermute | solution.py:279
  3.2 34.3 %all-to-all-start = ((bf16[8,128,128]{2,1,0:T(8,128)(2,1)}), bf16[8,128,128]{2,1,0:T(8,128)(2,1)S(1)}, u32[]{:S(2)}, u32[]{:S(2)}) async-start(bf16[8,128,128]{2,1,0:T(8,128)(2,1)} %bitcast.12), calls=%async_computation | async-start | bytes 524288 | tf_op jit(solution)/shard_map/all_to_all | solution.py:283
  15.4 13.8 %collective-permute-start.3 = (bf16[1,2,128,128]{3,2,1,0:T(8,128)(2,1)S(1)}, bf16[1,2,128,128]{3,2,1,0:T(8,128)(2,1)S(1)}, u32[]{:S(2)}, u32[]{:S(2)}) collective-permute-start(bf16[1,2,128,128]{3,2,1,0:T(8,128)(2,1)S(1)} %maximum_bitcast_fusion), channel_id=1, source_target_pairs={{0,256},{1,384},{128,257},{129,385},{64,320},{65,448},{192,321},{1... | collective-permute-start | bytes 196616 | tf_op jit(solution)/shard_map/ppermute | solution.py:279
  18.5 10.8 %collective-permute-start.4 = (bf16[1,2,128,128]{3,2,1,0:T(8,128)(2,1)S(1)}, bf16[1,2,128,128]{3,2,1,0:T(8,128)(2,1)S(1)}, u32[]{:S(2)}, u32[]{:S(2)}) collective-permute-start(bf16[1,2,128,128]{3,2,1,0:T(8,128)(2,1)S(1)} %maximum_bitcast_fusion), channel_id=1, source_target_pairs={{0,64},{1,192},{128,65},{129,193},{64,0},{65,128},{192,1},{193,129... | collective-permute-start | bytes 196616 | tf_op jit(solution)/shard_map/ppermute | solution.py:279
  25.5 12.0 %collective-permute-start.5 = (bf16[1,2,128,128]{3,2,1,0:T(8,128)(2,1)S(1)}, bf16[1,2,128,128]{3,2,1,0:T(8,128)(2,1)S(1)}, u32[]{:S(2)}, u32[]{:S(2)}) collective-permute-start(bf16[1,2,128,128]{3,2,1,0:T(8,128)(2,1)S(1)} %maximum_bitcast_fusion), channel_id=1, source_target_pairs={{0,320},{1,448},{128,321},{129,449},{64,256},{65,384},{192,257},{1... | collective-permute-start | bytes 196616 | tf_op jit(solution)/shard_map/ppermute | solution.py:279
  37.6 22.2 %collective-permute-start.6 = (bf16[8,2,128,128]{3,2,1,0:T(8,128)(2,1)S(1)}, bf16[8,2,128,128]{3,2,1,0:T(8,128)(2,1)S(1)}, u32[]{:S(2)}, u32[]{:S(2)}) collective-permute-start(bf16[8,2,128,128]{3,2,1,0:T(8,128)(2,1)S(1)} %constant_dynamic-update-slice_fusion.refs_3_.refs_0_), channel_id=1, source_target_pairs={{0,8},{8,16},{16,24},{24,32},{32,40},{40,48},{48,56},{56,0},{1,9},... | collective-permute-start | bytes 1572872 | tf_op jit(solution)/shard_map/ppermute | solution.py:27
  41.6 20.2 %collective-permute-start.10 = (bf16[8,2,128,128]{3,2,1,0:T(8,128)(2,1)S(1)}, bf16[8,2,128,128]{3,2,1,0:T(8,128)(2,1)S(1)}, u32[]{:S(2)}, u32[]{:S(2)}) collective-permute-start(bf16[8,2,128,128]{3,2,1,0:T(8,128)(2,1)S(1)} %constant_dynamic-update-slice_fusion.refs_3_.refs_0_), channel_id=1, source_target_pairs={{0,56},{8,0},{16,8},{24,16},{32,24},{40,32},{48,40},{56,48},{1,57}... | collective-permute-start | bytes 1572872 | tf_op jit(solution)/shard_map/ppermute | solution.py:27
  59.9 16.5 %collective-permute-start.7 = (bf16[8,2,128,128]{3,2,1,0:T(8,128)(2,1)S(1)}, bf16[8,2,128,128]{3,2,1,0:T(8,128)(2,1)S(1)}, u32[]{:S(2)}, u32[]{:S(2)}) collective-permute-start(bf16[8,2,128,128]{3,2,1,0:T(8,128)(2,1)S(1)} %collective-permute-done.6.refs_3_.refs_1_), channel_id=1, source_target_pairs={{0,8},{8,16},{16,24},{24,32},{32,40},{40,48},{48,56},{56,0},{1,9},... | collective-permute-start | bytes 1572872 | tf_op jit(solution)/shard_map/ppermute | solution.py:27
  61.8 27.4 %collective-permute-start.11 = (bf16[8,2,128,128]{3,2,1,0:T(8,128)(2,1)S(1)}, bf16[8,2,128,128]{3,2,1,0:T(8,128)(2,1)}, u32[]{:S(2)}, u32[]{:S(2)}) collective-permute-start(bf16[8,2,128,128]{3,2,1,0:T(8,128)(2,1)S(1)} %collective-permute-done.10.refs_4_.refs_2_), channel_id=1, source_target_pairs={{0,56},{8,0},{16,8},{24,16},{32,24},{40,32},{48,40},{56,48},{1,57}... | collective-permute-start | bytes 1572872 | tf_op jit(solution)/shard_map/ppermute | solution.py:27
  76.4 25.9 %copy-start = (bf16[8,2,128,128]{3,2,1,0:T(8,128)(2,1)}, bf16[8,2,128,128]{3,2,1,0:T(8,128)(2,1)S(1)}, u32[]{:S(2)}) copy-start(bf16[8,2,128,128]{3,2,1,0:T(8,128)(2,1)S(1)} %collective-permute-done.7.refs_3_) | copy-start | bytes 1572868
  76.4 17.8 %collective-permute-start.8 = (bf16[8,2,128,128]{3,2,1,0:T(8,128)(2,1)S(1)}, bf16[8,2,128,128]{3,2,1,0:T(8,128)(2,1)}, u32[]{:S(2)}, u32[]{:S(2)}) collective-permute-start(bf16[8,2,128,128]{3,2,1,0:T(8,128)(2,1)S(1)} %collective-permute-done.7.refs_3_), channel_id=1, source_target_pairs={{0,8},{8,16},{16,24},{24,32},{32,40},{40,48},{48,56},{56,0},{1,9},... | collective-permute-start | bytes 1572872 | tf_op jit(solution)/shard_map/ppermute | solution.py:27
  78.3 0.9 collective-permute-start
  79.3 17.0 %collective-permute-start.1 = (bf16[144,1024]{1,0:T(8,128)(2,1)S(1)}, bf16[144,1024]{1,0:T(8,128)(2,1)S(1)}, u32[]{:S(2)}, u32[]{:S(2)}) collective-permute-start(bf16[144,1024]{1,0:T(8,128)(2,1)S(1)} %collective-permute-done.refs_1_), channel_id=1, source_target_pairs={{0,1},{1,0},{2,3},{3,2},{4,5},{5,4},{6,7},{7,6},{8,9},{9,8},{10,11... | collective-permute-start | bytes 884744 | tf_op jit(solution)/shard_map/ppermute | solution.py:27
  89.2 17.1 %collective-permute-start.12 = (bf16[8,2,128,128]{3,2,1,0:T(8,128)(2,1)}, bf16[8,2,128,128]{3,2,1,0:T(8,128)(2,1)S(1)}, u32[]{:S(2)}, u32[]{:S(2)}) collective-permute-start(bf16[8,2,128,128]{3,2,1,0:T(8,128)(2,1)} %collective-permute-done.11.refs_4_), channel_id=1, source_target_pairs={{0,56},{8,0},{16,8},{24,16},{32,24},{40,32},{48,40},{56,48},{1,57}... | collective-permute-start | bytes 1572872 | tf_op jit(solution)/shard_map/ppermute | solution.py:27
  94.2 16.6 %collective-permute-start.9 = (bf16[8,2,128,128]{3,2,1,0:T(8,128)(2,1)}, bf16[8,2,128,128]{3,2,1,0:T(8,128)(2,1)S(1)}, u32[]{:S(2)}, u32[]{:S(2)}) collective-permute-start(bf16[8,2,128,128]{3,2,1,0:T(8,128)(2,1)} %collective-permute-done.8.refs_3_.refs_5_), channel_id=1, source_target_pairs={{0,8},{8,16},{16,24},{24,32},{32,40},{40,48},{48,56},{56,0},{1,9},... | collective-permute-start | bytes 1572872 | tf_op jit(solution)/shard_map/ppermute | solution.py:27
  106.4 4.3 %copy-start.2 = (bf16[8,2,128,128]{3,2,1,0:T(8,128)(2,1)}, bf16[8,2,128,128]{3,2,1,0:T(8,128)(2,1)S(1)}, u32[]{:S(2)}) copy-start(bf16[8,2,128,128]{3,2,1,0:T(8,128)(2,1)S(1)} %collective-permute-done.12.refs_4_.refs_6_) | copy-start | bytes 1572868
  112.4 4.8 %collective-permute-start.13 = (f32[144,1024]{1,0:T(8,128)S(1)}, f32[144,1024]{1,0:T(8,128)S(1)}, u32[]{:S(2)}, u32[]{:S(2)}) collective-permute-start(f32[144,1024]{1,0:T(8,128)S(1)} %shard_map.78), channel_id=1, source_target_pairs={{0,1},{1,0},{2,3},{3,2},{4,5},{5,4},{6,7},{7,6},{8,9},{9,8},{10,11... | collective-permute-start | bytes 1769480 | tf_op jit(solution)/shard_map/ppermute | solution.py:27
  117.4 12.0 %collective-permute-start.14 = (bf16[128,1024]{1,0:T(8,128)(2,1)S(1)}, bf16[128,1024]{1,0:T(8,128)(2,1)S(1)}, u32[]{:S(2)}, u32[]{:S(2)}) collective-permute-start(bf16[128,1024]{1,0:T(8,128)(2,1)S(1)} %shard_map.79), channel_id=1, source_target_pairs={{0,0},{1,128},{128,129},{129,257},{256,256},{257,384},{384,385},{3... | collective-permute-start | bytes 786440 | tf_op jit(solution)/shard_map/ppermute | solution.py:337
  119.8 9.6 %collective-permute-start.15 = (bf16[128,1024]{1,0:T(8,128)(2,1)S(1)}, bf16[128,1024]{1,0:T(8,128)(2,1)S(1)}, u32[]{:S(2)}, u32[]{:S(2)}) collective-permute-start(bf16[128,1024]{1,0:T(8,128)(2,1)S(1)} %shard_map.79), channel_id=1, source_target_pairs={{0,128},{1,256},{128,257},{129,385},{256,384},{257,0},{384,1},{385... | collective-permute-start | bytes 786440 | tf_op jit(solution)/shard_map/ppermute | solution.py:337
  123.0 11.1 %collective-permute-start.16 = (bf16[128,1024]{1,0:T(8,128)(2,1)S(1)}, bf16[128,1024]{1,0:T(8,128)(2,1)S(1)}, u32[]{:S(2)}, u32[]{:S(2)}) collective-permute-start(bf16[128,1024]{1,0:T(8,128)(2,1)S(1)} %shard_map.79), channel_id=1, source_target_pairs={{0,256},{1,384},{128,385},{129,1},{256,0},{257,128},{384,129},{385... | collective-permute-start | bytes 786440 | tf_op jit(solution)/shard_map/ppermute | solution.py:337
  125.0 9.2 %collective-permute-start.17 = (bf16[128,1024]{1,0:T(8,128)(2,1)S(1)}, bf16[128,1024]{1,0:T(8,128)(2,1)S(1)}, u32[]{:S(2)}, u32[]{:S(2)}) collective-permute-start(bf16[128,1024]{1,0:T(8,128)(2,1)S(1)} %shard_map.79), channel_id=1, source_target_pairs={{0,384},{1,0},{128,1},{129,129},{256,128},{257,256},{384,257},{385... | collective-permute-start | bytes 786440 | tf_op jit(solution)/shard_map/ppermute | solution.py:337
  125.8 1.0 copy-start.1
  126.8 1.0 copy-start.3
  134.9 8.1 %collective-permute-start.18 = (f32[4,128,512]{2,1,0:T(8,128)S(1)}, f32[4,128,512]{2,1,0:T(8,128)S(1)}, u32[]{:S(2)}, u32[]{:S(2)}) collective-permute-start(f32[4,128,512]{2,1,0:T(8,128)S(1)} %shard_map.82), channel_id=1, source_target_pairs={{0,1},{1,0},{2,3},{3,2},{4,5},{5,4},{6,7},{7,6},{8,9},{9,8},{10,11... | collective-permute-start | bytes 3145736 | tf_op jit(solution)/shard_map/ppermute | solution.py:27
  143.2 9.6 %collective-permute-start.21 = (bf16[128,512]{1,0:T(8,128)(2,1)S(1)}, bf16[128,512]{1,0:T(8,128)(2,1)S(1)}, u32[]{:S(2)}, u32[]{:S(2)}) collective-permute-start(bf16[128,512]{1,0:T(8,128)(2,1)S(1)} %get-tuple-element.34), channel_id=1, source_target_pairs={{0,6},{2,0},{4,2},{6,4},{1,7},{3,1},{5,3},{7,5},{8,14},{10,8},{12,... | collective-permute-start | bytes 393224 | tf_op jit(solution)/shard_map/ppermute | solution.py:27
  145.7 14.1 %collective-permute-start.20 = (bf16[128,512]{1,0:T(8,128)(2,1)S(1)}, bf16[128,512]{1,0:T(8,128)(2,1)S(1)}, u32[]{:S(2)}, u32[]{:S(2)}) collective-permute-start(bf16[128,512]{1,0:T(8,128)(2,1)S(1)} %get-tuple-element.35), channel_id=1, source_target_pairs={{0,4},{2,6},{4,0},{6,2},{1,5},{3,7},{5,1},{7,3},{8,12},{10,14},{12... | collective-permute-start | bytes 393224 | tf_op jit(solution)/shard_map/ppermute | solution.py:27
  150.2 9.7 %collective-permute-start.19 = (bf16[128,512]{1,0:T(8,128)(2,1)S(1)}, bf16[128,512]{1,0:T(8,128)(2,1)S(1)}, u32[]{:S(2)}, u32[]{:S(2)}) collective-permute-start(bf16[128,512]{1,0:T(8,128)(2,1)S(1)} %get-tuple-element.33), channel_id=1, source_target_pairs={{0,2},{2,4},{4,6},{6,0},{1,3},{3,5},{5,7},{7,1},{8,10},{10,12},{12... | collective-permute-start | bytes 393224 | tf_op jit(solution)/shard_map/ppermute | solution.py:27
  160.0 14.9 %collective-permute-start.22 = (bf16[128,512]{1,0:T(8,128)(2,1)S(1)}, bf16[128,512]{1,0:T(8,128)(2,1)S(1)}, u32[]{:S(2)}, u32[]{:S(2)}) collective-permute-start(bf16[128,512]{1,0:T(8,128)(2,1)S(1)} %fusion.10), channel_id=1, source_target_pairs={{0,0},{2,384},{4,256},{6,128},{128,130},{130,2},{132,386},{134,258... | collective-permute-start | bytes 393224 | tf_op jit(solution)/shard_map/ppermute | solution.py:353

commit v4 on v3

--- a/solution.py
+++ b/solution.py
@@ -203,64 +203,50 @@
     )(a, b)
 
 
-def assemble_kernel(at_ref, *refs):
-    chunks, out_ref = refs[:8], refs[8]
-    for p in range(8):
-        for y in range(2):
-            for x in range(4):
+def project_kernel(info_ref, *refs):
+    slots, chunks, out_ref, held, done = refs[:4], refs[4:12], *refs[12:]
+    rows = pl.ds(pl.multiple_of(info_ref[0] * 64, 64), 64)
+    for p, chunk in enumerate(chunks):
+        base = BLOCKS if p < 7 else 0
+        for x in range(4):
+            for y in range(2):
                 tile = x * 2 + y
-                block = chunks[p][BLOCKS + tile // 2, tile % 2]
-                for t in range(8):
-                    out_ref[x, y * 8 + at_ref[p], :, t * 128 : (t + 1) * 128] = block[
-                        t * 16 : (t + 1) * 16
-                    ]
-
-
-def assemble(at, chunks):
-    return pl.pallas_call(
-        assemble_kernel,
-        out_shape=jax.ShapeDtypeStruct((4, 16, 16, 1024), jnp.bfloat16),
-        in_specs=[SMEM] + [VMEM] * 8,
-        out_specs=VMEM,
-        cost_estimate=pl.CostEstimate(
-            flops=0, bytes_accessed=4 << 20, transcendentals=0
-        ),
-        compiler_params=pltpu.CompilerParams(vmem_limit_bytes=16 << 20),
-    )(at, *chunks)
-
-
-def project_kernel(col_ref, turn_ref, a0, a1, a2, a3, w_ref, out_ref):
+                pltpu.make_async_copy(
+                    chunk.at[base + tile // 2, tile % 2, rows],
+                    held.at[x, y * 8 + info_ref[2 + p]],
+                    done,
+                ).start()
+    pltpu.make_async_copy(held, held, done).wait()
     total = None
-    a = jnp.concatenate([a0[...], a1[...], a2[...], a3[...]], axis=0)
+    a = jnp.concatenate([slot[...] for slot in slots], axis=0)
     for x in range(4):
+        w = jnp.concatenate(
+            [held[x, :, t * 16 : (t + 1) * 16].reshape(256, 128) for t in range(4)],
+            axis=1,
+        )
         part = jnp.dot(
-            a[:, x * 256 : (x + 1) * 256],
-            w_ref[x].reshape(256, 512),
-            preferred_element_type=jnp.float32,
+            a[:, x * 256 : (x + 1) * 256], w, preferred_element_type=jnp.float32
         )
         total = part if total is None else total + part
     for k in range(4):
-        out_ref[(turn_ref[0] + k) % 4] = total[k * TOK : (k + 1) * TOK]
-
-
-def project(column, turn, slots, weight):
+        out_ref[(info_ref[1] + k) % 4] = total[k * TOK : (k + 1) * TOK]
+
+
+def project(info, slots, chunks):
     return pl.pallas_call(
         project_kernel,
-        grid_spec=pltpu.PrefetchScalarGridSpec(
-            num_scalar_prefetch=2,
-            grid=(1,),
-            in_specs=[pl.BlockSpec((TOK, ROWS), lambda i, col, turn: (0, 0))] * 4
-            + [
-                pl.BlockSpec((4, 16, 16, 512), lambda i, col, turn: (0, 0, 0, col[0])),
-            ],
-            out_specs=pl.BlockSpec((4, TOK, 512), lambda i, col, turn: (0, 0, 0)),
-        ),
         out_shape=jax.ShapeDtypeStruct((4, TOK, 512), jnp.float32),
+        in_specs=[SMEM] + [VMEM] * 4 + [pl.BlockSpec(memory_space=pl.ANY)] * 8,
+        out_specs=VMEM,
+        scratch_shapes=[
+            pltpu.VMEM((4, 16, 64, 128), jnp.bfloat16),
+            pltpu.SemaphoreType.DMA,
+        ],
         cost_estimate=pl.CostEstimate(
             flops=512 * 1024 * 1024, bytes_accessed=3 << 20, transcendentals=0
         ),
         compiler_params=pltpu.CompilerParams(vmem_limit_bytes=16 << 20),
-    )(column, turn, *slots, weight)
+    )(info, *slots, *chunks)
 
 
 def work(queries, keys, values, q_gain, frame_bounds, output_weight, attn_gate):
@@ -310,10 +296,11 @@
     packs = (near, far)
 
     right, left = [chunk], [chunk]
-    for s in range(1, 5):
+    for _ in range(1, 4):
         right.append(shift(right[-1], "z", 1))
-        if s < 4:
-            left.append(shift(left[-1], "z", -1))
+        left.append(shift(left[-1], "z", -1))
+    right.append(shift(right[3][:BLOCKS], "z", 1))
+    left.append(shift(left[3][BLOCKS:], "z", -1))
     gain = q_gain[None, :]
     state = attend(ids[0], packs, [chunk], gain, None)
     for s in range(1, 4):
@@ -335,15 +322,13 @@
             (x * 2 + c, ((x + k + c) % 4) * 2 + x % 2) for x in range(4) for c in range(2)
         ]
         slots.append(lax.ppermute(attended, ("x", "c"), pairs))
-    parts = [chunk, right[1], left[1], right[2], left[2], right[3], left[3], right[4]]
-    at = jnp.stack([(az + h) % 8 for h in hops]).astype(jnp.int32)
-    weight = assemble(at, parts)
-
-    core = core.astype(jnp.int32)[None]
+    parts = [chunk, right[1], left[1], right[2], left[2], right[3], left[3]]
+    parts.append(left[4])
     turn = (core + 4 - lax.axis_index("yl")) % 4
-    for_other = project(1 - core, turn, slots, weight)
+    info = [turn] + [(az + h) % 8 for h in hops]
+    for_other = project(jnp.stack([1 - core] + info).astype(jnp.int32), slots, parts)
     from_other = shift(for_other, "c", 1)
-    for_own = project(core, turn, slots, weight)
+    for_own = project(jnp.stack([core] + info).astype(jnp.int32), slots, parts)
     combined = for_own[0] + from_other[0]
     for s in range(1, 4):
         part = (for_own[s] + from_other[s]).astype(jnp.bfloat16)

time: 177 us -> 185 us (1.045)
  Pallas kernels: 20.9 us -> 26.7 us
  other arithmetic: 1.44 us -> 3.44 us
    pallas_call x3 -> x2, Pallas kernels: 2.99 us -> 8.78 us  [project(): pl.pallas_call(project_kernel, out_shape=jax.ShapeDtypeStruct((4, TOK, 51...]
    ppermute x4, starting transfers between devices: 8.23 us -> 11 us  [work(): slots.append(lax.ppermute(attended, ('x', 'c'), pairs))]
    unnamed x20 -> x14, local copies, waits for them, and re-layouts: 3.73 us -> 1.4 us
    ppermute x13 -> x14, starting transfers between devices: 55.8 us -> 54.8 us  [shift(): lax.ppermute(value, axis, [(s, (s + steps) % count) for s in range(count)])]
    ppermute x13 -> x14, waiting for transfers between devices: 28 us -> 28.5 us  [shift(): lax.ppermute(value, axis, [(s, (s + steps) % count) for s in range(count)])]
  transfers between devices with their start and end apart: 24 -> 25, of which waited for: 7 -> 7; matrix products, arithmetic and copies ran while one was open for 1% -> 1% of each run, Pallas kernels for 10% -> 11%
where the time goes in v4:
time: 185 us; the launch traced here: 184 us
  starting transfers between devices  95 us (51%)
  waiting for transfers between devices  54.6 us (30%)
  Pallas kernels  26.7 us (14%)
  other arithmetic  3.44 us (2%)
  local copies, waits for them, and re-layouts  3.12 us (2%)
    ppermute x14, starting transfers between devices, shift(): lax.ppermute(value, axis, [(s, (s + steps) % count) for s in range(count)])  54.8 us
    ppermute x14, waiting for transfers between devices, shift(): lax.ppermute(value, axis, [(s, (s + steps) % count) for s in range(count)])  28.5 us
    pallas_call x6, Pallas kernels, attend(): pl.pallas_call(body, out_shape=out_shape, in_specs=[SMEM] + [VMEM] * (2 +...  17 us
    ppermute x5, starting transfers between devices, trade(): return lax.ppermute(value, ('x', 'yh', 'c'), pairs)  15.1 us
    ppermute x1, waiting for transfers between devices, work(): return lax.ppermute(result, ('x', 'yl'), pairs)  12.4 us
    all_to_all x1, starting transfers between devices, work(): lax.all_to_all(quarter, ('x', 'yh'), split_axis=0, concat_axis=0, tiled=T...  12.2 us
    ppermute x4, starting transfers between devices, work(): slots.append(lax.ppermute(attended, ('x', 'c'), pairs))  11 us
    pallas_call x2, Pallas kernels, project(): pl.pallas_call(project_kernel, out_shape=jax.ShapeDtypeStruct((4, TOK, 51...  8.78 us
  transfers between devices with their start and end apart: 25, of which 7 were waited for; matrix products, arithmetic and copies ran while one was open for 1% of the time, Pallas kernels for 11%

profile of v4, /device:TPU:7, one launch (start us, length us, event | category | flops | bytes accessed | tf_op | source)
XLA Modules:
  0.0 184.2 jit_solution(15719727045533518346)
XLA Ops:
  0.0 0.8 maximum_bitcast_fusion
  0.8 0.7 collective-permute-start.2
  1.6 0.7 broadcast_in_dim.15
  2.3 12.2 %all-to-all-start = ((bf16[8,128,128]{2,1,0:T(8,128)(2,1)}), bf16[8,128,128]{2,1,0:T(8,128)(2,1)S(1)}, u32[]{:S(2)}, u32[]{:S(2)}) async-start(bf16[8,128,128]{2,1,0:T(8,128)(2,1)} %bitcast.20), calls=%async_computation | async-start | bytes 524288 | tf_op jit(solution)/shard_map/all_to_all | solution.py:269
  14.5 3.1 %collective-permute-start.3 = (bf16[1,2,128,128]{3,2,1,0:T(8,128)(2,1)S(1)}, bf16[1,2,128,128]{3,2,1,0:T(8,128)(2,1)S(1)}, u32[]{:S(2)}, u32[]{:S(2)}) collective-permute-start(bf16[1,2,128,128]{3,2,1,0:T(8,128)(2,1)S(1)} %maximum_bitcast_fusion), channel_id=1, source_target_pairs={{0,256},{1,384},{128,257},{129,385},{64,320},{65,448},{192,321},{1... | collective-permute-start | bytes 196616 | tf_op jit(solution)/shard_map/ppermute | solution.py:265
  17.6 7.0 %collective-permute-start.4 = (bf16[1,2,128,128]{3,2,1,0:T(8,128)(2,1)S(1)}, bf16[1,2,128,128]{3,2,1,0:T(8,128)(2,1)S(1)}, u32[]{:S(2)}, u32[]{:S(2)}) collective-permute-start(bf16[1,2,128,128]{3,2,1,0:T(8,128)(2,1)S(1)} %maximum_bitcast_fusion), channel_id=1, source_target_pairs={{0,64},{1,192},{128,65},{129,193},{64,0},{65,128},{192,1},{193,129... | collective-permute-start | bytes 196616 | tf_op jit(solution)/shard_map/ppermute | solution.py:265
  24.6 3.7 %collective-permute-start.5 = (bf16[1,2,128,128]{3,2,1,0:T(8,128)(2,1)S(1)}, bf16[1,2,128,128]{3,2,1,0:T(8,128)(2,1)S(1)}, u32[]{:S(2)}, u32[]{:S(2)}) collective-permute-start(bf16[1,2,128,128]{3,2,1,0:T(8,128)(2,1)S(1)} %maximum_bitcast_fusion), channel_id=1, source_target_pairs={{0,320},{1,448},{128,321},{129,449},{64,256},{65,384},{192,257},{1... | collective-permute-start | bytes 196616 | tf_op jit(solution)/shard_map/ppermute | solution.py:265
  28.4 8.2 %collective-permute-done.5 = bf16[1,2,128,128]{3,2,1,0:T(8,128)(2,1)S(1)} collective-permute-done((bf16[1,2,128,128]{3,2,1,0:T(8,128)(2,1)S(1)}, bf16[1,2,128,128]{3,2,1,0:T(8,128)(2,1)S(1)}, u32[]{:S(2)}, u32[]{:S(2)}) %collective-permute-start.5) | collective-permute-done | bytes 65568 | tf_op jit(solution)/shard_map/ppermute | solution.py:265
  36.7 4.1 %collective-permute-start.6 = (bf16[8,2,128,128]{3,2,1,0:T(8,128)(2,1)S(1)}, bf16[8,2,128,128]{3,2,1,0:T(8,128)(2,1)S(1)}, u32[]{:S(2)}, u32[]{:S(2)}) collective-permute-start(bf16[8,2,128,128]{3,2,1,0:T(8,128)(2,1)S(1)} %constant_dynamic-update-slice_fusion.refs_3_.refs_4_), channel_id=1, source_target_pairs={{0,8},{8,16},{16,24},{24,32},{32,40},{40,48},{48,56},{56,0},{1,9},... | collective-permute-start | bytes 1572872 | tf_op jit(solution)/shard_map/ppermute | solution.py:27
  40.9 8.6 %collective-permute-start.10 = (bf16[8,2,128,128]{3,2,1,0:T(8,128)(2,1)S(1)}, bf16[8,2,128,128]{3,2,1,0:T(8,128)(2,1)S(1)}, u32[]{:S(2)}, u32[]{:S(2)}) collective-permute-start(bf16[8,2,128,128]{3,2,1,0:T(8,128)(2,1)S(1)} %constant_dynamic-update-slice_fusion.refs_3_.refs_4_), channel_id=1, source_target_pairs={{0,56},{8,0},{16,8},{24,16},{32,24},{40,32},{48,40},{56,48},{1,57}... | collective-permute-start | bytes 1572872 | tf_op jit(solution)/shard_map/ppermute | solution.py:27
  49.5 9.6 %collective-permute-done.6.refs_3_.refs_5_ = bf16[8,2,128,128]{3,2,1,0:T(8,128)(2,1)S(1)} collective-permute-done((bf16[8,2,128,128]{3,2,1,0:T(8,128)(2,1)S(1)}, bf16[8,2,128,128]{3,2,1,0:T(8,128)(2,1)S(1)}, u32[]{:S(2)}, u32[]{:S(2)}) %collective-permute-start.6) | collective-permute-done | bytes 524320 | tf_op jit(solution)/shard_map/ppermute | solution.py:27
  59.1 1.9 %collective-permute-start.7 = (bf16[8,2,128,128]{3,2,1,0:T(8,128)(2,1)S(1)}, bf16[8,2,128,128]{3,2,1,0:T(8,128)(2,1)S(1)}, u32[]{:S(2)}, u32[]{:S(2)}) collective-permute-start(bf16[8,2,128,128]{3,2,1,0:T(8,128)(2,1)S(1)} %collective-permute-done.6.refs_3_.refs_5_), channel_id=1, source_target_pairs={{0,8},{8,16},{16,24},{24,32},{32,40},{40,48},{48,56},{56,0},{1,9},... | collective-permute-start | bytes 1572872 | tf_op jit(solution)/shard_map/ppermute | solution.py:27
  61.0 4.8 %collective-permute-start.11 = (bf16[8,2,128,128]{3,2,1,0:T(8,128)(2,1)S(1)}, bf16[8,2,128,128]{3,2,1,0:T(8,128)(2,1)}, u32[]{:S(2)}, u32[]{:S(2)}) collective-permute-start(bf16[8,2,128,128]{3,2,1,0:T(8,128)(2,1)S(1)} %collective-permute-done.10.refs_4_.refs_6_), channel_id=1, source_target_pairs={{0,56},{8,0},{16,8},{24,16},{32,24},{40,32},{48,40},{56,48},{1,57}... | collective-permute-start | bytes 1572872 | tf_op jit(solution)/shard_map/ppermute | solution.py:27
  65.9 0.7 collective-permute-start
  66.9 8.7 %collective-permute-done.7.refs_3_.refs_7_ = bf16[8,2,128,128]{3,2,1,0:T(8,128)(2,1)S(1)} collective-permute-done((bf16[8,2,128,128]{3,2,1,0:T(8,128)(2,1)S(1)}, bf16[8,2,128,128]{3,2,1,0:T(8,128)(2,1)S(1)}, u32[]{:S(2)}, u32[]{:S(2)}) %collective-permute-start.7) | collective-permute-done | bytes 524320 | tf_op jit(solution)/shard_map/ppermute | solution.py:27
  75.6 1.9 %collective-permute-start.8 = (bf16[8,2,128,128]{3,2,1,0:T(8,128)(2,1)S(1)}, bf16[8,2,128,128]{3,2,1,0:T(8,128)(2,1)S(1)}, u32[]{:S(2)}, u32[]{:S(2)}) collective-permute-start(bf16[8,2,128,128]{3,2,1,0:T(8,128)(2,1)S(1)} %collective-permute-done.7.refs_3_.refs_7_), channel_id=1, source_target_pairs={{0,8},{8,16},{16,24},{24,32},{32,40},{40,48},{48,56},{56,0},{1,9},... | collective-permute-start | bytes 1572872 | tf_op jit(solution)/shard_map/ppermute | solution.py:27
  77.5 2.9 %collective-permute-start.1 = (bf16[144,1024]{1,0:T(8,128)(2,1)S(1)}, bf16[144,1024]{1,0:T(8,128)(2,1)S(1)}, u32[]{:S(2)}, u32[]{:S(2)}) collective-permute-start(bf16[144,1024]{1,0:T(8,128)(2,1)S(1)} %collective-permute-done.refs_1_), channel_id=1, source_target_pairs={{0,1},{1,0},{2,3},{3,2},{4,5},{5,4},{6,7},{7,6},{8,9},{9,8},{10,11... | collective-permute-start | bytes 884744 | tf_op jit(solution)/shard_map/ppermute | solution.py:27
  80.4 4.9 %collective-permute-start.12 = (bf16[8,2,128,128]{3,2,1,0:T(8,128)(2,1)}, bf16[8,2,128,128]{3,2,1,0:T(8,128)(2,1)S(1)}, u32[]{:S(2)}, u32[]{:S(2)}) collective-permute-start(bf16[8,2,128,128]{3,2,1,0:T(8,128)(2,1)} %collective-permute-done.11.refs_4_.refs_8_), channel_id=1, source_target_pairs={{0,56},{8,0},{16,8},{24,16},{32,24},{40,32},{48,40},{56,48},{1,57}... | collective-permute-start | bytes 1572872 | tf_op jit(solution)/shard_map/ppermute | solution.py:27
  85.5 0.7 copy-done
  86.2 2.4 %shard_map.73 = (bf16[2048,128]{1,0:T(8,128)(2,1)S(1)}, f32[1,2048]{1,0:T(1,128)S(1)}, f32[8,2048]{1,0:T(8,128)S(1)}, f32[128,2048]{1,0:T(8,128)S(1)}) custom-call(s32[4]{0:T(128)S(1)} %get-tuple-element.41.refs_0_, bf16[144,1024]{1,0:T(8,128)(2,1)S(1)} %collective-permute-done.refs_1_, bf16[144,1024]{1,0:T(8,128)(2,1)S(1)} %collective-permute-done.1.refs_2_, ...), custom_call_target="tpu_custom_call" | custom-call | flops 536870912 | bytes 3407872 | tf_op jit(solution)/shard_map/pallas_call | solution.py:163
  88.6 2.6 %collective-permute-done.8.refs_3_.refs_9_ = bf16[8,2,128,128]{3,2,1,0:T(8,128)(2,1)S(1)} collective-permute-done((bf16[8,2,128,128]{3,2,1,0:T(8,128)(2,1)S(1)}, bf16[8,2,128,128]{3,2,1,0:T(8,128)(2,1)S(1)}, u32[]{:S(2)}, u32[]{:S(2)}) %collective-permute-start.8) | collective-permute-done | bytes 524320 | tf_op jit(solution)/shard_map/ppermute | solution.py:27
  91.3 2.1 %collective-permute-start.9 = (bf16[4,2,128,128]{3,2,1,0:T(8,128)(2,1)S(1)}, bf16[4,2,128,128]{3,2,1,0:T(8,128)(2,1)S(1)}, u32[]{:S(2)}, u32[]{:S(2)}) collective-permute-start(bf16[4,2,128,128]{3,2,1,0:T(8,128)(2,1)S(1)} %slice.40), channel_id=1, source_target_pairs={{0,8},{8,16},{16,24},{24,32},{32,40},{40,48},{48,56},{56,0},{1,9},... | collective-permute-start | bytes 786440 | tf_op jit(solution)/shard_map/ppermute | solution.py:27
  93.4 3.6 %shard_map.74 = (f32[1,2048]{1,0:T(1,128)S(1)}, f32[8,2048]{1,0:T(8,128)S(1)}, f32[128,2048]{1,0:T(8,128)S(1)}) custom-call(s32[8]{0:T(128)S(1)} %pad_add_fusion.3.refs_0_, bf16[144,1024]{1,0:T(8,128)(2,1)S(1)} %collective-permute-done.refs_1_, bf16[144,1024]{1,0:T(8,128)(2,1)S(1)} %collective-permute-done.1.refs_2_, ...), custom_call_target="tpu_custom_call" | custom-call | flops 1073741824 | bytes 3670016 | tf_op jit(solution)/shard_map/pallas_call | solution.py:163
  96.9 4.1 %shard_map.75 = (f32[1,2048]{1,0:T(1,128)S(1)}, f32[8,2048]{1,0:T(8,128)S(1)}, f32[128,2048]{1,0:T(8,128)S(1)}) custom-call(s32[8]{0:T(128)S(1)} %pad_add_fusion.2.refs_0_, bf16[144,1024]{1,0:T(8,128)(2,1)S(1)} %collective-permute-done.refs_1_, bf16[144,1024]{1,0:T(8,128)(2,1)S(1)} %collective-permute-done.1.refs_2_, ...), custom_call_target="tpu_custom_call" | custom-call | flops 1073741824 | bytes 3670016 | tf_op jit(solution)/shard_map/pallas_call | solution.py:163
  101.1 3.6 %shard_map.76 = (f32[1,2048]{1,0:T(1,128)S(1)}, f32[8,2048]{1,0:T(8,128)S(1)}, f32[128,2048]{1,0:T(8,128)S(1)}) custom-call(s32[8]{0:T(128)S(1)} %pad_add_fusion.1.refs_0_, bf16[144,1024]{1,0:T(8,128)(2,1)S(1)} %collective-permute-done.refs_1_, bf16[144,1024]{1,0:T(8,128)(2,1)S(1)} %collective-permute-done.1.refs_2_, ...), custom_call_target="tpu_custom_call" | custom-call | flops 1073741824 | bytes 3670016 | tf_op jit(solution)/shard_map/pallas_call | solution.py:163
  104.7 1.6 shard_map.78
  106.3 3.7 %collective-permute-start.13 = (f32[144,1024]{1,0:T(8,128)S(1)}, f32[144,1024]{1,0:T(8,128)S(1)}, u32[]{:S(2)}, u32[]{:S(2)}) collective-permute-start(f32[144,1024]{1,0:T(8,128)S(1)} %shard_map.78), channel_id=1, source_target_pairs={{0,1},{1,0},{2,3},{3,2},{4,5},{5,4},{6,7},{7,6},{8,9},{9,8},{10,11... | collective-permute-start | bytes 1769480 | tf_op jit(solution)/shard_map/ppermute | solution.py:27
  110.0 0.7 slice.41
  110.8 4.8 %collective-permute-start.18 = (bf16[4,2,128,128]{3,2,1,0:T(8,128)(2,1)}, bf16[4,2,128,128]{3,2,1,0:T(8,128)(2,1)}, u32[]{:S(2)}, u32[]{:S(2)}) collective-permute-start(bf16[4,2,128,128]{3,2,1,0:T(8,128)(2,1)} %slice.41), channel_id=1, source_target_pairs={{0,56},{8,0},{16,8},{24,16},{32,24},{40,32},{48,40},{56,48},{1,57}... | collective-permute-start | bytes 786440 | tf_op jit(solution)/shard_map/ppermute | solution.py:27
  115.6 1.6 shard_map.77.a_ref
  117.3 0.9 shard_map.79
  118.2 1.9 %collective-permute-start.14 = (bf16[128,1024]{1,0:T(8,128)(2,1)}, bf16[128,1024]{1,0:T(8,128)(2,1)S(1)}, u32[]{:S(2)}, u32[]{:S(2)}) collective-permute-start(bf16[128,1024]{1,0:T(8,128)(2,1)} %shard_map.79), channel_id=1, source_target_pairs={{0,0},{1,128},{128,129},{129,257},{256,256},{257,384},{384,385},{3... | collective-permute-start | bytes 786440 | tf_op jit(solution)/shard_map/ppermute | solution.py:324
  120.1 3.4 %collective-permute-start.15 = (bf16[128,1024]{1,0:T(8,128)(2,1)}, bf16[128,1024]{1,0:T(8,128)(2,1)}, u32[]{:S(2)}, u32[]{:S(2)}) collective-permute-start(bf16[128,1024]{1,0:T(8,128)(2,1)} %shard_map.79), channel_id=1, source_target_pairs={{0,128},{1,256},{128,257},{129,385},{256,384},{257,0},{384,1},{385... | collective-permute-start | bytes 786440 | tf_op jit(solution)/shard_map/ppermute | solution.py:324
  123.5 2.0 %collective-permute-start.16 = (bf16[128,1024]{1,0:T(8,128)(2,1)}, bf16[128,1024]{1,0:T(8,128)(2,1)}, u32[]{:S(2)}, u32[]{:S(2)}) collective-permute-start(bf16[128,1024]{1,0:T(8,128)(2,1)} %shard_map.79), channel_id=1, source_target_pairs={{0,256},{1,384},{128,385},{129,1},{256,0},{257,128},{384,129},{385... | collective-permute-start | bytes 786440 | tf_op jit(solution)/shard_map/ppermute | solution.py:324
  125.6 3.6 %collective-permute-start.17 = (bf16[128,1024]{1,0:T(8,128)(2,1)}, bf16[128,1024]{1,0:T(8,128)(2,1)}, u32[]{:S(2)}, u32[]{:S(2)}) collective-permute-start(bf16[128,1024]{1,0:T(8,128)(2,1)} %shard_map.79), channel_id=1, source_target_pairs={{0,384},{1,0},{128,1},{129,129},{256,128},{257,256},{384,257},{385... | collective-permute-start | bytes 786440 | tf_op jit(solution)/shard_map/ppermute | solution.py:324
  129.3 5.5 %collective-permute-done.16.refs_2_ = bf16[128,1024]{1,0:T(8,128)(2,1)} collective-permute-done((bf16[128,1024]{1,0:T(8,128)(2,1)}, bf16[128,1024]{1,0:T(8,128)(2,1)}, u32[]{:S(2)}, u32[]{:S(2)}) %collective-permute-start.16) | collective-permute-done | bytes 262176 | tf_op jit(solution)/shard_map/ppermute | solution.py:324
  134.8 4.9 %shard_map.81 = f32[4,128,512]{2,1,0:T(8,128)} custom-call(s32[10]{0:T(128)S(1)} %stack.92.info_ref, bf16[128,1024]{1,0:T(8,128)(2,1)S(1)} %collective-permute-done.14.refs_0_, bf16[128,1024]{1,0:T(8,128)(2,1)} %collective-permute-done.15.refs_1_, bf16[128,1024]{1,0:T(8,128)(2,1)} %collective-permute-done.16.refs_2_, ...), custom_call_target="tpu_custom_call" | custom-call | flops 536870912 | bytes 3145728 | tf_op jit(solution)/shard_map/pallas_call | solution.py:236
  139.7 6.4 %collective-permute-start.19 = (f32[4,128,512]{2,1,0:T(8,128)}, f32[4,128,512]{2,1,0:T(8,128)}, u32[]{:S(2)}, u32[]{:S(2)}) collective-permute-start(f32[4,128,512]{2,1,0:T(8,128)} %shard_map.81), channel_id=1, source_target_pairs={{0,1},{1,0},{2,3},{3,2},{4,5},{5,4},{6,7},{7,6},{8,9},{9,8},{10,11... | collective-permute-start | bytes 3145736 | tf_op jit(solution)/shard_map/ppermute | solution.py:27
  146.1 3.9 %shard_map.80 = f32[4,128,512]{2,1,0:T(8,128)S(1)} custom-call(s32[10]{0:T(128)S(1)} %stack.82.info_ref, bf16[128,1024]{1,0:T(8,128)(2,1)S(1)} %collective-permute-done.14.refs_0_, bf16[128,1024]{1,0:T(8,128)(2,1)} %collective-permute-done.15.refs_1_, bf16[128,1024]{1,0:T(8,128)(2,1)} %collective-permute-done.16.refs_2_, ...), custom_call_target="tpu_custom_call" | custom-call | flops 536870912 | bytes 3145728 | tf_op jit(solution)/shard_map/pallas_call | solution.py:236
  150.0 1.2 fusion.11
  151.3 2.7 %collective-permute-start.22 = (bf16[128,512]{1,0:T(8,128)(2,1)S(1)}, bf16[128,512]{1,0:T(8,128)(2,1)S(1)}, u32[]{:S(2)}, u32[]{:S(2)}) collective-permute-start(bf16[128,512]{1,0:T(8,128)(2,1)S(1)} %get-tuple-element.34), channel_id=1, source_target_pairs={{0,6},{2,0},{4,2},{6,4},{1,7},{3,1},{5,3},{7,5},{8,14},{10,8},{12,... | collective-permute-start | bytes 393224 | tf_op jit(solution)/shard_map/ppermute | solution.py:27
  154.0 4.1 %collective-permute-start.21 = (bf16[128,512]{1,0:T(8,128)(2,1)S(1)}, bf16[128,512]{1,0:T(8,128)(2,1)S(1)}, u32[]{:S(2)}, u32[]{:S(2)}) collective-permute-start(bf16[128,512]{1,0:T(8,128)(2,1)S(1)} %get-tuple-element.35), channel_id=1, source_target_pairs={{0,4},{2,6},{4,0},{6,2},{1,5},{3,7},{5,1},{7,3},{8,12},{10,14},{12... | collective-permute-start | bytes 393224 | tf_op jit(solution)/shard_map/ppermute | solution.py:27
  158.1 1.9 %collective-permute-start.20 = (bf16[128,512]{1,0:T(8,128)(2,1)S(1)}, bf16[128,512]{1,0:T(8,128)(2,1)S(1)}, u32[]{:S(2)}, u32[]{:S(2)}) collective-permute-start(bf16[128,512]{1,0:T(8,128)(2,1)S(1)} %get-tuple-element.33), channel_id=1, source_target_pairs={{0,2},{2,4},{4,6},{6,0},{1,3},{3,5},{5,7},{7,1},{8,10},{10,12},{12... | collective-permute-start | bytes 393224 | tf_op jit(solution)/shard_map/ppermute | solution.py:27
  160.7 7.4 %collective-permute-done.21 = bf16[128,512]{1,0:T(8,128)(2,1)S(1)} collective-permute-done((bf16[128,512]{1,0:T(8,128)(2,1)S(1)}, bf16[128,512]{1,0:T(8,128)(2,1)S(1)}, u32[]{:S(2)}, u32[]{:S(2)}) %collective-permute-start.21) | collective-permute-done | bytes 131104 | tf_op jit(solution)/shard_map/ppermute | solution.py:27
  168.2 1.0 fusion.10
  169.2 1.9 %collective-permute-start.23 = (bf16[128,512]{1,0:T(8,128)(2,1)S(1)}, bf16[128,512]{1,0:T(8,128)(2,1)S(1)}, u32[]{:S(2)}, u32[]{:S(2)}) collective-permute-start(bf16[128,512]{1,0:T(8,128)(2,1)S(1)} %fusion.10), channel_id=1, source_target_pairs={{0,0},{2,384},{4,256},{6,128},{128,130},{130,2},{132,386},{134,258... | collective-permute-start | bytes 393224 | tf_op jit(solution)/shard_map/ppermute | solution.py:338
  171.1 12.4 %collective-permute-done.23 = bf16[128,512]{1,0:T(8,128)(2,1)S(1)} collective-permute-done((bf16[128,512]{1,0:T(8,128)(2,1)S(1)}, bf16[128,512]{1,0:T(8,128)(2,1)S(1)}, u32[]{:S(2)}, u32[]{:S(2)}) %collective-permute-start.23) | collective-permute-done | bytes 131104 | tf_op jit(solution)/shard_map/ppermute | solution.py:338
  183.6 0.7 copy.16
  (42 shorter events, 0.8 us)
Async XLA Ops:
  0.0 1.5 copy-start.2
  0.8 27.5 %collective-permute-start.2 = (bf16[1,2,128,128]{3,2,1,0:T(8,128)(2,1)S(1)}, bf16[1,2,128,128]{3,2,1,0:T(8,128)(2,1)S(1)}, u32[]{:S(2)}, u32[]{:S(2)}) collective-permute-start(bf16[1,2,128,128]{3,2,1,0:T(8,128)(2,1)S(1)} %maximum_bitcast_fusion), channel_id=1, source_target_pairs={{0,0},{1,128},{128,1},{129,129},{64,64},{65,192},{192,65},{193,193... | collective-permute-start | bytes 196616 | tf_op jit(solution)/shard_map/ppermute | solution.py:265
  2.3 34.3 %all-to-all-start = ((bf16[8,128,128]{2,1,0:T(8,128)(2,1)}), bf16[8,128,128]{2,1,0:T(8,128)(2,1)S(1)}, u32[]{:S(2)}, u32[]{:S(2)}) async-start(bf16[8,128,128]{2,1,0:T(8,128)(2,1)} %bitcast.20), calls=%async_computation | async-start | bytes 524288 | tf_op jit(solution)/shard_map/all_to_all | solution.py:269
  14.5 13.8 %collective-permute-start.3 = (bf16[1,2,128,128]{3,2,1,0:T(8,128)(2,1)S(1)}, bf16[1,2,128,128]{3,2,1,0:T(8,128)(2,1)S(1)}, u32[]{:S(2)}, u32[]{:S(2)}) collective-permute-start(bf16[1,2,128,128]{3,2,1,0:T(8,128)(2,1)S(1)} %maximum_bitcast_fusion), channel_id=1, source_target_pairs={{0,256},{1,384},{128,257},{129,385},{64,320},{65,448},{192,321},{1... | collective-permute-start | bytes 196616 | tf_op jit(solution)/shard_map/ppermute | solution.py:265
  17.6 10.8 %collective-permute-start.4 = (bf16[1,2,128,128]{3,2,1,0:T(8,128)(2,1)S(1)}, bf16[1,2,128,128]{3,2,1,0:T(8,128)(2,1)S(1)}, u32[]{:S(2)}, u32[]{:S(2)}) collective-permute-start(bf16[1,2,128,128]{3,2,1,0:T(8,128)(2,1)S(1)} %maximum_bitcast_fusion), channel_id=1, source_target_pairs={{0,64},{1,192},{128,65},{129,193},{64,0},{65,128},{192,1},{193,129... | collective-permute-start | bytes 196616 | tf_op jit(solution)/shard_map/ppermute | solution.py:265
  24.6 12.0 %collective-permute-start.5 = (bf16[1,2,128,128]{3,2,1,0:T(8,128)(2,1)S(1)}, bf16[1,2,128,128]{3,2,1,0:T(8,128)(2,1)S(1)}, u32[]{:S(2)}, u32[]{:S(2)}) collective-permute-start(bf16[1,2,128,128]{3,2,1,0:T(8,128)(2,1)S(1)} %maximum_bitcast_fusion), channel_id=1, source_target_pairs={{0,320},{1,448},{128,321},{129,449},{64,256},{65,384},{192,257},{1... | collective-permute-start | bytes 196616 | tf_op jit(solution)/shard_map/ppermute | solution.py:265
  36.7 29.2 %copy-start.3 = (s32[2,128]{1,0:T(2,128)S(1)}, s32[2,128]{1,0:T(2,128)}, u32[]{:S(2)}) copy-start(s32[2,128]{1,0:T(2,128)} %param.11) | copy-start | bytes 3076
  36.7 29.2 %copy-start.1 = (bf16[128,1024]{1,0:T(8,128)(2,1)S(1)}, bf16[128,1024]{1,0:T(8,128)(2,1)}, u32[]{:S(2)}) copy-start(bf16[128,1024]{1,0:T(8,128)(2,1)} %param.7) | copy-start | bytes 786436
  36.7 22.4 %collective-permute-start.6 = (bf16[8,2,128,128]{3,2,1,0:T(8,128)(2,1)S(1)}, bf16[8,2,128,128]{3,2,1,0:T(8,128)(2,1)S(1)}, u32[]{:S(2)}, u32[]{:S(2)}) collective-permute-start(bf16[8,2,128,128]{3,2,1,0:T(8,128)(2,1)S(1)} %constant_dynamic-update-slice_fusion.refs_3_.refs_4_), channel_id=1, source_target_pairs={{0,8},{8,16},{16,24},{24,32},{32,40},{40,48},{48,56},{56,0},{1,9},... | collective-permute-start | bytes 1572872 | tf_op jit(solution)/shard_map/ppermute | solution.py:27
  40.9 20.2 %collective-permute-start.10 = (bf16[8,2,128,128]{3,2,1,0:T(8,128)(2,1)S(1)}, bf16[8,2,128,128]{3,2,1,0:T(8,128)(2,1)S(1)}, u32[]{:S(2)}, u32[]{:S(2)}) collective-permute-start(bf16[8,2,128,128]{3,2,1,0:T(8,128)(2,1)S(1)} %constant_dynamic-update-slice_fusion.refs_3_.refs_4_), channel_id=1, source_target_pairs={{0,56},{8,0},{16,8},{24,16},{32,24},{40,32},{48,40},{56,48},{1,57}... | collective-permute-start | bytes 1572872 | tf_op jit(solution)/shard_map/ppermute | solution.py:27
  59.1 16.5 %collective-permute-start.7 = (bf16[8,2,128,128]{3,2,1,0:T(8,128)(2,1)S(1)}, bf16[8,2,128,128]{3,2,1,0:T(8,128)(2,1)S(1)}, u32[]{:S(2)}, u32[]{:S(2)}) collective-permute-start(bf16[8,2,128,128]{3,2,1,0:T(8,128)(2,1)S(1)} %collective-permute-done.6.refs_3_.refs_5_), channel_id=1, source_target_pairs={{0,8},{8,16},{16,24},{24,32},{32,40},{40,48},{48,56},{56,0},{1,9},... | collective-permute-start | bytes 1572872 | tf_op jit(solution)/shard_map/ppermute | solution.py:27
  61.0 19.4 %collective-permute-start.11 = (bf16[8,2,128,128]{3,2,1,0:T(8,128)(2,1)S(1)}, bf16[8,2,128,128]{3,2,1,0:T(8,128)(2,1)}, u32[]{:S(2)}, u32[]{:S(2)}) collective-permute-start(bf16[8,2,128,128]{3,2,1,0:T(8,128)(2,1)S(1)} %collective-permute-done.10.refs_4_.refs_6_), channel_id=1, source_target_pairs={{0,56},{8,0},{16,8},{24,16},{32,24},{40,32},{48,40},{56,48},{1,57}... | collective-permute-start | bytes 1572872 | tf_op jit(solution)/shard_map/ppermute | solution.py:27
  65.9 11.6 %collective-permute-start = (bf16[144,1024]{1,0:T(8,128)(2,1)S(1)}, bf16[144,1024]{1,0:T(8,128)(2,1)S(1)}, u32[]{:S(2)}, u32[]{:S(2)}) collective-permute-start(bf16[144,1024]{1,0:T(8,128)(2,1)S(1)} %fusion.1), channel_id=1, source_target_pairs={{0,0},{1,128},{128,1},{129,129},{64,64},{65,192},{192,65},{193,193... | collective-permute-start | bytes 884744 | tf_op jit(solution)/shard_map/ppermute | solution.py:265
  75.6 15.6 %collective-permute-start.8 = (bf16[8,2,128,128]{3,2,1,0:T(8,128)(2,1)S(1)}, bf16[8,2,128,128]{3,2,1,0:T(8,128)(2,1)S(1)}, u32[]{:S(2)}, u32[]{:S(2)}) collective-permute-start(bf16[8,2,128,128]{3,2,1,0:T(8,128)(2,1)S(1)} %collective-permute-done.7.refs_3_.refs_7_), channel_id=1, source_target_pairs={{0,8},{8,16},{16,24},{24,32},{32,40},{40,48},{48,56},{56,0},{1,9},... | collective-permute-start | bytes 1572872 | tf_op jit(solution)/shard_map/ppermute | solution.py:27
  77.5 8.0 %collective-permute-start.1 = (bf16[144,1024]{1,0:T(8,128)(2,1)S(1)}, bf16[144,1024]{1,0:T(8,128)(2,1)S(1)}, u32[]{:S(2)}, u32[]{:S(2)}) collective-permute-start(bf16[144,1024]{1,0:T(8,128)(2,1)S(1)} %collective-permute-done.refs_1_), channel_id=1, source_target_pairs={{0,1},{1,0},{2,3},{3,2},{4,5},{5,4},{6,7},{7,6},{8,9},{9,8},{10,11... | collective-permute-start | bytes 884744 | tf_op jit(solution)/shard_map/ppermute | solution.py:27
  80.4 20.6 %collective-permute-start.12 = (bf16[8,2,128,128]{3,2,1,0:T(8,128)(2,1)}, bf16[8,2,128,128]{3,2,1,0:T(8,128)(2,1)S(1)}, u32[]{:S(2)}, u32[]{:S(2)}) collective-permute-start(bf16[8,2,128,128]{3,2,1,0:T(8,128)(2,1)} %collective-permute-done.11.refs_4_.refs_8_), channel_id=1, source_target_pairs={{0,56},{8,0},{16,8},{24,16},{32,24},{40,32},{48,40},{56,48},{1,57}... | collective-permute-start | bytes 1572872 | tf_op jit(solution)/shard_map/ppermute | solution.py:27
  85.5 0.7 copy-start
  91.3 13.4 %collective-permute-start.9 = (bf16[4,2,128,128]{3,2,1,0:T(8,128)(2,1)S(1)}, bf16[4,2,128,128]{3,2,1,0:T(8,128)(2,1)S(1)}, u32[]{:S(2)}, u32[]{:S(2)}) collective-permute-start(bf16[4,2,128,128]{3,2,1,0:T(8,128)(2,1)S(1)} %slice.40), channel_id=1, source_target_pairs={{0,8},{8,16},{16,24},{24,32},{32,40},{40,48},{48,56},{56,0},{1,9},... | collective-permute-start | bytes 786440 | tf_op jit(solution)/shard_map/ppermute | solution.py:27
  106.3 10.9 %collective-permute-start.13 = (f32[144,1024]{1,0:T(8,128)S(1)}, f32[144,1024]{1,0:T(8,128)S(1)}, u32[]{:S(2)}, u32[]{:S(2)}) collective-permute-start(f32[144,1024]{1,0:T(8,128)S(1)} %shard_map.78), channel_id=1, source_target_pairs={{0,1},{1,0},{2,3},{3,2},{4,5},{5,4},{6,7},{7,6},{8,9},{9,8},{10,11... | collective-permute-start | bytes 1769480 | tf_op jit(solution)/shard_map/ppermute | solution.py:27
  110.8 18.5 %collective-permute-start.18 = (bf16[4,2,128,128]{3,2,1,0:T(8,128)(2,1)}, bf16[4,2,128,128]{3,2,1,0:T(8,128)(2,1)}, u32[]{:S(2)}, u32[]{:S(2)}) collective-permute-start(bf16[4,2,128,128]{3,2,1,0:T(8,128)(2,1)} %slice.41), channel_id=1, source_target_pairs={{0,56},{8,0},{16,8},{24,16},{32,24},{40,32},{48,40},{56,48},{1,57}... | collective-permute-start | bytes 786440 | tf_op jit(solution)/shard_map/ppermute | solution.py:27
  118.2 11.1 %collective-permute-start.14 = (bf16[128,1024]{1,0:T(8,128)(2,1)}, bf16[128,1024]{1,0:T(8,128)(2,1)S(1)}, u32[]{:S(2)}, u32[]{:S(2)}) collective-permute-start(bf16[128,1024]{1,0:T(8,128)(2,1)} %shard_map.79), channel_id=1, source_target_pairs={{0,0},{1,128},{128,129},{129,257},{256,256},{257,384},{384,385},{3... | collective-permute-start | bytes 786440 | tf_op jit(solution)/shard_map/ppermute | solution.py:324
  120.1 9.2 %collective-permute-start.15 = (bf16[128,1024]{1,0:T(8,128)(2,1)}, bf16[128,1024]{1,0:T(8,128)(2,1)}, u32[]{:S(2)}, u32[]{:S(2)}) collective-permute-start(bf16[128,1024]{1,0:T(8,128)(2,1)} %shard_map.79), channel_id=1, source_target_pairs={{0,128},{1,256},{128,257},{129,385},{256,384},{257,0},{384,1},{385... | collective-permute-start | bytes 786440 | tf_op jit(solution)/shard_map/ppermute | solution.py:324
  123.5 11.2 %collective-permute-start.16 = (bf16[128,1024]{1,0:T(8,128)(2,1)}, bf16[128,1024]{1,0:T(8,128)(2,1)}, u32[]{:S(2)}, u32[]{:S(2)}) collective-permute-start(bf16[128,1024]{1,0:T(8,128)(2,1)} %shard_map.79), channel_id=1, source_target_pairs={{0,256},{1,384},{128,385},{129,1},{256,0},{257,128},{384,129},{385... | collective-permute-start | bytes 786440 | tf_op jit(solution)/shard_map/ppermute | solution.py:324
  125.6 9.2 %collective-permute-start.17 = (bf16[128,1024]{1,0:T(8,128)(2,1)}, bf16[128,1024]{1,0:T(8,128)(2,1)}, u32[]{:S(2)}, u32[]{:S(2)}) collective-permute-start(bf16[128,1024]{1,0:T(8,128)(2,1)} %shard_map.79), channel_id=1, source_target_pairs={{0,384},{1,0},{128,1},{129,129},{256,128},{257,256},{384,257},{385... | collective-permute-start | bytes 786440 | tf_op jit(solution)/shard_map/ppermute | solution.py:324
  139.7 10.4 %collective-permute-start.19 = (f32[4,128,512]{2,1,0:T(8,128)}, f32[4,128,512]{2,1,0:T(8,128)}, u32[]{:S(2)}, u32[]{:S(2)}) collective-permute-start(f32[4,128,512]{2,1,0:T(8,128)} %shard_map.81), channel_id=1, source_target_pairs={{0,1},{1,0},{2,3},{3,2},{4,5},{5,4},{6,7},{7,6},{8,9},{9,8},{10,11... | collective-permute-start | bytes 3145736 | tf_op jit(solution)/shard_map/ppermute | solution.py:27
  151.3 9.4 %collective-permute-start.22 = (bf16[128,512]{1,0:T(8,128)(2,1)S(1)}, bf16[128,512]{1,0:T(8,128)(2,1)S(1)}, u32[]{:S(2)}, u32[]{:S(2)}) collective-permute-start(bf16[128,512]{1,0:T(8,128)(2,1)S(1)} %get-tuple-element.34), channel_id=1, source_target_pairs={{0,6},{2,0},{4,2},{6,4},{1,7},{3,1},{5,3},{7,5},{8,14},{10,8},{12,... | collective-permute-start | bytes 393224 | tf_op jit(solution)/shard_map/ppermute | solution.py:27
  154.0 14.1 %collective-permute-start.21 = (bf16[128,512]{1,0:T(8,128)(2,1)S(1)}, bf16[128,512]{1,0:T(8,128)(2,1)S(1)}, u32[]{:S(2)}, u32[]{:S(2)}) collective-permute-start(bf16[128,512]{1,0:T(8,128)(2,1)S(1)} %get-tuple-element.35), channel_id=1, source_target_pairs={{0,4},{2,6},{4,0},{6,2},{1,5},{3,7},{5,1},{7,3},{8,12},{10,14},{12... | collective-permute-start | bytes 393224 | tf_op jit(solution)/shard_map/ppermute | solution.py:27
  158.1 10.1 %collective-permute-start.20 = (bf16[128,512]{1,0:T(8,128)(2,1)S(1)}, bf16[128,512]{1,0:T(8,128)(2,1)S(1)}, u32[]{:S(2)}, u32[]{:S(2)}) collective-permute-start(bf16[128,512]{1,0:T(8,128)(2,1)S(1)} %get-tuple-element.33), channel_id=1, source_target_pairs={{0,2},{2,4},{4,6},{6,0},{1,3},{3,5},{5,7},{7,1},{8,10},{10,12},{12... | collective-permute-start | bytes 393224 | tf_op jit(solution)/shard_map/ppermute | solution.py:27
  169.2 14.4 %collective-permute-start.23 = (bf16[128,512]{1,0:T(8,128)(2,1)S(1)}, bf16[128,512]{1,0:T(8,128)(2,1)S(1)}, u32[]{:S(2)}, u32[]{:S(2)}) collective-permute-start(bf16[128,512]{1,0:T(8,128)(2,1)S(1)} %fusion.10), channel_id=1, source_target_pairs={{0,0},{2,384},{4,256},{6,128},{128,130},{130,2},{132,386},{134,258... | collective-permute-start | bytes 393224 | tf_op jit(solution)/shard_map/ppermute | solution.py:338

commit v5 on v3

--- a/solution.py
+++ b/solution.py
@@ -27,7 +27,7 @@
     return lax.ppermute(value, axis, [(s, (s + steps) % count) for s in range(count)])
 
 
-def attention_kernel(n_chunks, first, half, ids_ref, *refs):
+def attention_kernel(offset, n_chunks, first, half, ids_ref, *refs):
     refs = list(refs)
     packs = [refs.pop(0) for _ in range(2)]
     chunks = [refs.pop(0) for _ in range(n_chunks)]
@@ -86,7 +86,7 @@
         allowed = []
         new = m
         for j in range(BLOCKS):
-            block = ids_ref[c * BLOCKS + j].astype(jnp.float32)
+            block = ids_ref[(offset + c) * BLOCKS + j].astype(jnp.float32)
             ok = (lower <= block) & (block < upper)
             top = jnp.max(s[j * D : (j + 1) * D], axis=0, keepdims=True)
             new = jnp.maximum(new, jnp.where(ok, top, LOW))
@@ -140,7 +140,7 @@
             acc_out[:, cols[w]] = acc
 
 
-def attend(ids, packs, chunks, gain, state, half=None):
+def attend(ids, offset, packs, chunks, gain, state, half=None):
     first = state is None
     sums = (
         jax.ShapeDtypeStruct((1, 2 * ROWS), jnp.float32),
@@ -158,7 +158,7 @@
     rows = 2 * ROWS if half is None else ROWS
 
     def body(*refs):
-        attention_kernel(len(chunks), first, half, *refs)
+        attention_kernel(offset, len(chunks), first, half, *refs)
 
     out = pl.pallas_call(
         body,
@@ -284,25 +284,20 @@
         quarter, ("x", "yh"), split_axis=0, concat_axis=0, tiled=True
     )
     own = jnp.stack([keys, values])[None]
-    chunk = jnp.concatenate(
-        [
-            trade(own),
-            trade(own, di=1),
-            trade(own, dy=1),
-            trade(own, di=1, dy=1),
-            quarter.reshape(4, 2, 128, 128),
-        ]
-    )
+    pair = jnp.concatenate([trade(own), trade(own, dy=1)])
+    across = shift(pair, "x", 2)
+    chunk = jnp.concatenate([pair, across, quarter.reshape(4, 2, 128, 128)])
     block_x = 2 * (ax // 2) + core
     in_chunk = jnp.stack(
         [
             ((block_x + 2 * di) % 4) * 16 + ((ay + dy) % 2) * 8
+            for di in (0, 1)
             for dy in (0, 1)
-            for di in (0, 1)
         ]
     ).astype(jnp.int32)
     hops = [0, -1, 1, -2, 2, -3, 3, -4]
-    ids = [in_chunk + (az + h) % 8 for h in hops]
+    at = (az + jnp.array(hops, jnp.int32)) % 8
+    ids = (at[:, None] + in_chunk[None, :]).reshape(-1)
 
     bounds = jnp.pad(frame_bounds.astype(jnp.bfloat16), ((0, 14), (0, ROWS - TOK)))
     near = trade(jnp.concatenate([queries, bounds]))
@@ -315,18 +310,19 @@
         if s < 4:
             left.append(shift(left[-1], "z", -1))
     gain = q_gain[None, :]
-    state = attend(ids[0], packs, [chunk], gain, None)
+    state = attend(ids, 0, packs, [chunk], gain, None)
     for s in range(1, 4):
         state = attend(
-            jnp.concatenate(ids[2 * s - 1 : 2 * s + 1]),
+            ids,
+            2 * s - 1,
             packs,
             [right[s], left[s]],
             gain,
             state,
         )
-    send = attend(ids[7], packs, [right[4]], gain, state, half=1)
+    send = attend(ids, 7, packs, [right[4]], gain, state, half=1)
     received = shift(send, "c", 1)
-    keep = attend(ids[7], packs, [right[4]], gain, state, half=0)
+    keep = attend(ids, 7, packs, [right[4]], gain, state, half=0)
     attended = merge(keep, received)
 
     slots = []
@@ -336,7 +332,6 @@
         ]
         slots.append(lax.ppermute(attended, ("x", "c"), pairs))
     parts = [chunk, right[1], left[1], right[2], left[2], right[3], left[3], right[4]]
-    at = jnp.stack([(az + h) % 8 for h in hops]).astype(jnp.int32)
     weight = assemble(at, parts)
 
     core = core.astype(jnp.int32)[None]

time: 177 us -> 171 us (0.966)
  the two profiles are of different devices: /device:TPU:7 before, /device:TPU:6 now
where the time goes in v5:
time: 171 us; the launch traced here: 170 us
  starting transfers between devices  91.4 us (53%)
  waiting for transfers between devices  51.9 us (30%)
  Pallas kernels  21 us (12%)
  local copies, waits for them, and re-layouts  3.54 us (2%)
    ppermute x14, starting transfers between devices, shift(): lax.ppermute(value, axis, [(s, (s + steps) % count) for s in range(count)])  49.3 us
    ppermute x14, waiting for transfers between devices, shift(): lax.ppermute(value, axis, [(s, (s + steps) % count) for s in range(count)])  27.5 us
    ppermute x3, starting transfers between devices, trade(): return lax.ppermute(value, ('x', 'yh', 'c'), pairs)  18.5 us
    pallas_call x6, Pallas kernels, attend(): pl.pallas_call(body, out_shape=out_shape, in_specs=[SMEM] + [VMEM] * (2 +...  17.6 us
    ppermute x1, waiting for transfers between devices, work(): return lax.ppermute(result, ('x', 'yl'), pairs)  12.4 us
    ppermute x4, starting transfers between devices, work(): slots.append(lax.ppermute(attended, ('x', 'c'), pairs))  11.5 us
    all_to_all x1, starting transfers between devices, work(): lax.all_to_all(quarter, ('x', 'yh'), split_axis=0, concat_axis=0, tiled=T...  10 us
    ppermute x3, waiting for transfers between devices, trade(): return lax.ppermute(value, ('x', 'yh', 'c'), pairs)  6.23 us
  transfers between devices with their start and end apart: 23, of which 13 were waited for; matrix products, arithmetic and copies ran while one was open for 1% of the time, Pallas kernels for 11%

profile of v5, /device:TPU:6, one launch (start us, length us, event | category | flops | bytes accessed | tf_op | source)
XLA Modules:
  0.0 170.3 jit_solution(14757640803852295430)
XLA Ops:
  0.0 1.0 copy.11
  1.1 0.7 broadcast_in_dim.21
  1.8 10.0 %all-to-all-start = ((bf16[8,128,128]{2,1,0:T(8,128)(2,1)}), bf16[8,128,128]{2,1,0:T(8,128)(2,1)S(1)}, u32[]{:S(2)}, u32[]{:S(2)}) async-start(bf16[8,128,128]{2,1,0:T(8,128)(2,1)} %bitcast.12), calls=%async_computation | async-start | bytes 524288 | tf_op jit(solution)/shard_map/all_to_all | solution.py:283
  11.8 0.8 maximum_bitcast_fusion
  12.6 6.4 %collective-permute-start.3 = (bf16[1,2,128,128]{3,2,1,0:T(8,128)(2,1)S(1)}, bf16[1,2,128,128]{3,2,1,0:T(8,128)(2,1)S(1)}, u32[]{:S(2)}, u32[]{:S(2)}) collective-permute-start(bf16[1,2,128,128]{3,2,1,0:T(8,128)(2,1)S(1)} %maximum_bitcast_fusion), channel_id=1, source_target_pairs={{0,64},{1,192},{128,65},{129,193},{64,0},{65,128},{192,1},{193,129... | collective-permute-start | bytes 196616 | tf_op jit(solution)/shard_map/ppermute | solution.py:279
  19.0 3.9 %collective-permute-start.2 = (bf16[1,2,128,128]{3,2,1,0:T(8,128)(2,1)S(1)}, bf16[1,2,128,128]{3,2,1,0:T(8,128)(2,1)S(1)}, u32[]{:S(2)}, u32[]{:S(2)}) collective-permute-start(bf16[1,2,128,128]{3,2,1,0:T(8,128)(2,1)S(1)} %maximum_bitcast_fusion), channel_id=1, source_target_pairs={{0,0},{1,128},{128,1},{129,129},{64,64},{65,192},{192,65},{193,193... | collective-permute-start | bytes 196616 | tf_op jit(solution)/shard_map/ppermute | solution.py:279
  23.0 0.8 collective-permute-done.3
  23.7 1.2 collective-permute-done.2
  24.9 3.4 %collective-permute-start.4 = (bf16[2,2,128,128]{3,2,1,0:T(8,128)(2,1)S(1)}, bf16[2,2,128,128]{3,2,1,0:T(8,128)(2,1)S(1)}, u32[]{:S(2)}, u32[]{:S(2)}) collective-permute-start(bf16[2,2,128,128]{3,2,1,0:T(8,128)(2,1)S(1)} %pad_maximum_fusion.1), channel_id=1, source_target_pairs={{0,256},{128,384},{256,0},{384,128},{1,257},{129,385},{257,1},{385... | collective-permute-start | bytes 393224 | tf_op jit(solution)/shard_map/ppermute | solution.py:27
  28.3 5.0 %collective-permute-done.4 = bf16[2,2,128,128]{3,2,1,0:T(8,128)(2,1)S(1)} collective-permute-done((bf16[2,2,128,128]{3,2,1,0:T(8,128)(2,1)S(1)}, bf16[2,2,128,128]{3,2,1,0:T(8,128)(2,1)S(1)}, u32[]{:S(2)}, u32[]{:S(2)}) %collective-permute-start.4) | collective-permute-done | bytes 131104 | tf_op jit(solution)/shard_map/ppermute | solution.py:27
  33.4 4.3 %collective-permute-start.5 = (bf16[8,2,128,128]{3,2,1,0:T(8,128)(2,1)S(1)}, bf16[8,2,128,128]{3,2,1,0:T(8,128)(2,1)S(1)}, u32[]{:S(2)}, u32[]{:S(2)}) collective-permute-start(bf16[8,2,128,128]{3,2,1,0:T(8,128)(2,1)S(1)} %pad_maximum_fusion.refs_3_.refs_0_), channel_id=1, source_target_pairs={{0,8},{8,16},{16,24},{24,32},{32,40},{40,48},{48,56},{56,0},{1,9},... | collective-permute-start | bytes 1572872 | tf_op jit(solution)/shard_map/ppermute | solution.py:27
  37.6 8.6 %collective-permute-start.9 = (bf16[8,2,128,128]{3,2,1,0:T(8,128)(2,1)S(1)}, bf16[8,2,128,128]{3,2,1,0:T(8,128)(2,1)S(1)}, u32[]{:S(2)}, u32[]{:S(2)}) collective-permute-start(bf16[8,2,128,128]{3,2,1,0:T(8,128)(2,1)S(1)} %pad_maximum_fusion.refs_3_.refs_0_), channel_id=1, source_target_pairs={{0,56},{8,0},{16,8},{24,16},{32,24},{40,32},{48,40},{56,48},{1,57}... | collective-permute-start | bytes 1572872 | tf_op jit(solution)/shard_map/ppermute | solution.py:27
  46.2 7.0 %collective-permute-done.5.refs_3_.refs_1_ = bf16[8,2,128,128]{3,2,1,0:T(8,128)(2,1)S(1)} collective-permute-done((bf16[8,2,128,128]{3,2,1,0:T(8,128)(2,1)S(1)}, bf16[8,2,128,128]{3,2,1,0:T(8,128)(2,1)S(1)}, u32[]{:S(2)}, u32[]{:S(2)}) %collective-permute-start.5) | collective-permute-done | bytes 524320 | tf_op jit(solution)/shard_map/ppermute | solution.py:27
  53.2 1.9 %collective-permute-start.6 = (bf16[8,2,128,128]{3,2,1,0:T(8,128)(2,1)S(1)}, bf16[8,2,128,128]{3,2,1,0:T(8,128)(2,1)S(1)}, u32[]{:S(2)}, u32[]{:S(2)}) collective-permute-start(bf16[8,2,128,128]{3,2,1,0:T(8,128)(2,1)S(1)} %collective-permute-done.5.refs_3_.refs_1_), channel_id=1, source_target_pairs={{0,8},{8,16},{16,24},{24,32},{32,40},{40,48},{48,56},{56,0},{1,9},... | collective-permute-start | bytes 1572872 | tf_op jit(solution)/shard_map/ppermute | solution.py:27
  55.2 5.1 %collective-permute-start.10 = (bf16[8,2,128,128]{3,2,1,0:T(8,128)(2,1)S(1)}, bf16[8,2,128,128]{3,2,1,0:T(8,128)(2,1)}, u32[]{:S(2)}, u32[]{:S(2)}) collective-permute-start(bf16[8,2,128,128]{3,2,1,0:T(8,128)(2,1)S(1)} %collective-permute-done.9.refs_4_.refs_2_), channel_id=1, source_target_pairs={{0,56},{8,0},{16,8},{24,16},{32,24},{40,32},{48,40},{56,48},{1,57}... | collective-permute-start | bytes 1572872 | tf_op jit(solution)/shard_map/ppermute | solution.py:27
  60.3 6.1 %collective-permute-done.6.refs_3_ = bf16[8,2,128,128]{3,2,1,0:T(8,128)(2,1)S(1)} collective-permute-done((bf16[8,2,128,128]{3,2,1,0:T(8,128)(2,1)S(1)}, bf16[8,2,128,128]{3,2,1,0:T(8,128)(2,1)S(1)}, u32[]{:S(2)}, u32[]{:S(2)}) %collective-permute-start.6) | collective-permute-done | bytes 524320 | tf_op jit(solution)/shard_map/ppermute | solution.py:27
  66.5 1.9 %collective-permute-start.7 = (bf16[8,2,128,128]{3,2,1,0:T(8,128)(2,1)S(1)}, bf16[8,2,128,128]{3,2,1,0:T(8,128)(2,1)}, u32[]{:S(2)}, u32[]{:S(2)}) collective-permute-start(bf16[8,2,128,128]{3,2,1,0:T(8,128)(2,1)S(1)} %collective-permute-done.6.refs_3_), channel_id=1, source_target_pairs={{0,8},{8,16},{16,24},{24,32},{32,40},{40,48},{48,56},{56,0},{1,9},... | collective-permute-start | bytes 1572872 | tf_op jit(solution)/shard_map/ppermute | solution.py:27
  68.4 8.1 %collective-permute-start = (bf16[144,1024]{1,0:T(8,128)(2,1)S(1)}, bf16[144,1024]{1,0:T(8,128)(2,1)S(1)}, u32[]{:S(2)}, u32[]{:S(2)}) collective-permute-start(bf16[144,1024]{1,0:T(8,128)(2,1)S(1)} %fusion.1), channel_id=1, source_target_pairs={{0,0},{1,128},{128,1},{129,129},{64,64},{65,192},{192,65},{193,193... | collective-permute-start | bytes 884744 | tf_op jit(solution)/shard_map/ppermute | solution.py:279
  76.6 4.3 %collective-permute-done.refs_1_ = bf16[144,1024]{1,0:T(8,128)(2,1)S(1)} collective-permute-done((bf16[144,1024]{1,0:T(8,128)(2,1)S(1)}, bf16[144,1024]{1,0:T(8,128)(2,1)S(1)}, u32[]{:S(2)}, u32[]{:S(2)}) %collective-permute-start) | collective-permute-done | bytes 294944 | tf_op jit(solution)/shard_map/ppermute | solution.py:279
  80.9 1.9 %collective-permute-start.1 = (bf16[144,1024]{1,0:T(8,128)(2,1)S(1)}, bf16[144,1024]{1,0:T(8,128)(2,1)S(1)}, u32[]{:S(2)}, u32[]{:S(2)}) collective-permute-start(bf16[144,1024]{1,0:T(8,128)(2,1)S(1)} %collective-permute-done.refs_1_), channel_id=1, source_target_pairs={{0,1},{1,0},{2,3},{3,2},{4,5},{5,4},{6,7},{7,6},{8,9},{9,8},{10,11... | collective-permute-start | bytes 884744 | tf_op jit(solution)/shard_map/ppermute | solution.py:27
  82.9 4.9 %collective-permute-start.11 = (bf16[8,2,128,128]{3,2,1,0:T(8,128)(2,1)}, bf16[8,2,128,128]{3,2,1,0:T(8,128)(2,1)}, u32[]{:S(2)}, u32[]{:S(2)}) collective-permute-start(bf16[8,2,128,128]{3,2,1,0:T(8,128)(2,1)} %collective-permute-done.10.refs_4_), channel_id=1, source_target_pairs={{0,56},{8,0},{16,8},{24,16},{32,24},{40,32},{48,40},{56,48},{1,57}... | collective-permute-start | bytes 1572872 | tf_op jit(solution)/shard_map/ppermute | solution.py:27
  87.8 1.9 %collective-permute-start.8 = (bf16[8,2,128,128]{3,2,1,0:T(8,128)(2,1)}, bf16[8,2,128,128]{3,2,1,0:T(8,128)(2,1)S(1)}, u32[]{:S(2)}, u32[]{:S(2)}) collective-permute-start(bf16[8,2,128,128]{3,2,1,0:T(8,128)(2,1)} %collective-permute-done.7.refs_3_.refs_5_), channel_id=1, source_target_pairs={{0,8},{8,16},{16,24},{24,32},{32,40},{40,48},{48,56},{56,0},{1,9},... | collective-permute-start | bytes 1572872 | tf_op jit(solution)/shard_map/ppermute | solution.py:27
  89.9 2.4 %shard_map.82 = (bf16[2048,128]{1,0:T(8,128)(2,1)S(1)}, f32[1,2048]{1,0:T(1,128)S(1)}, f32[8,2048]{1,0:T(8,128)S(1)}, f32[128,2048]{1,0:T(8,128)S(1)}) custom-call(s32[32]{0:T(128)S(1)} %add.127.refs_0_, bf16[144,1024]{1,0:T(8,128)(2,1)S(1)} %collective-permute-done.refs_1_, bf16[144,1024]{1,0:T(8,128)(2,1)S(1)} %collective-permute-done.1.refs_2_, ...), custom_call_target="tpu_custom_call" | custom-call | flops 536870912 | bytes 3407872 | tf_op jit(solution)/shard_map/pallas_call | solution.py:163
  92.3 3.6 %shard_map.83 = (f32[1,2048]{1,0:T(1,128)S(1)}, f32[8,2048]{1,0:T(8,128)S(1)}, f32[128,2048]{1,0:T(8,128)S(1)}) custom-call(s32[32]{0:T(128)S(1)} %add.127.refs_0_, bf16[144,1024]{1,0:T(8,128)(2,1)S(1)} %collective-permute-done.refs_1_, bf16[144,1024]{1,0:T(8,128)(2,1)S(1)} %collective-permute-done.1.refs_2_, ...), custom_call_target="tpu_custom_call" | custom-call | flops 1073741824 | bytes 3670016 | tf_op jit(solution)/shard_map/pallas_call | solution.py:163
  95.9 4.1 %shard_map.84 = (f32[1,2048]{1,0:T(1,128)S(1)}, f32[8,2048]{1,0:T(8,128)S(1)}, f32[128,2048]{1,0:T(8,128)S(1)}) custom-call(s32[32]{0:T(128)S(1)} %add.127.refs_0_, bf16[144,1024]{1,0:T(8,128)(2,1)S(1)} %collective-permute-done.refs_1_, bf16[144,1024]{1,0:T(8,128)(2,1)S(1)} %collective-permute-done.1.refs_2_, bf16[8,2,128,128]{3,2,1,0:T(8,128)(2,1)S(1)} %copy-done.1, ...), custom_call_target="tpu_custom_call" | custom-call | flops 1073741824 | bytes 3670016 | tf_op jit(solution)/shard_map/pallas_call | solution.py:163
  100.1 4.2 %shard_map.85 = (f32[1,2048]{1,0:T(1,128)S(1)}, f32[8,2048]{1,0:T(8,128)S(1)}, f32[128,2048]{1,0:T(8,128)S(1)}) custom-call(s32[32]{0:T(128)S(1)} %add.127.refs_0_, bf16[144,1024]{1,0:T(8,128)(2,1)S(1)} %collective-permute-done.refs_1_, bf16[144,1024]{1,0:T(8,128)(2,1)S(1)} %collective-permute-done.1.refs_2_, ...), custom_call_target="tpu_custom_call" | custom-call | flops 1073741824 | bytes 3670016 | tf_op jit(solution)/shard_map/pallas_call | solution.py:163
  104.3 0.9 collective-permute-done.8.refs_3_.refs_7_
  105.2 1.6 shard_map.87
  106.8 2.1 %collective-permute-start.12 = (f32[144,1024]{1,0:T(8,128)S(1)}, f32[144,1024]{1,0:T(8,128)S(1)}, u32[]{:S(2)}, u32[]{:S(2)}) collective-permute-start(f32[144,1024]{1,0:T(8,128)S(1)} %shard_map.87), channel_id=1, source_target_pairs={{0,1},{1,0},{2,3},{3,2},{4,5},{5,4},{6,7},{7,6},{8,9},{9,8},{10,11... | collective-permute-start | bytes 1769480 | tf_op jit(solution)/shard_map/ppermute | solution.py:27
  108.9 1.6 shard_map.86.a_ref
  110.9 2.3 %collective-permute-start.13 = (bf16[128,1024]{1,0:T(8,128)(2,1)S(1)}, bf16[128,1024]{1,0:T(8,128)(2,1)S(1)}, u32[]{:S(2)}, u32[]{:S(2)}) collective-permute-start(bf16[128,1024]{1,0:T(8,128)(2,1)S(1)} %shard_map.88), channel_id=1, source_target_pairs={{0,0},{1,128},{128,129},{129,257},{256,256},{257,384},{384,385},{3... | collective-permute-start | bytes 786440 | tf_op jit(solution)/shard_map/ppermute | solution.py:333
  113.2 2.0 %collective-permute-start.14 = (bf16[128,1024]{1,0:T(8,128)(2,1)S(1)}, bf16[128,1024]{1,0:T(8,128)(2,1)S(1)}, u32[]{:S(2)}, u32[]{:S(2)}) collective-permute-start(bf16[128,1024]{1,0:T(8,128)(2,1)S(1)} %shard_map.88), channel_id=1, source_target_pairs={{0,128},{1,256},{128,257},{129,385},{256,384},{257,0},{384,1},{385... | collective-permute-start | bytes 786440 | tf_op jit(solution)/shard_map/ppermute | solution.py:333
  115.2 5.2 %collective-permute-start.15 = (bf16[128,1024]{1,0:T(8,128)(2,1)S(1)}, bf16[128,1024]{1,0:T(8,128)(2,1)S(1)}, u32[]{:S(2)}, u32[]{:S(2)}) collective-permute-start(bf16[128,1024]{1,0:T(8,128)(2,1)S(1)} %shard_map.88), channel_id=1, source_target_pairs={{0,256},{1,384},{128,385},{129,1},{256,0},{257,128},{384,129},{385... | collective-permute-start | bytes 786440 | tf_op jit(solution)/shard_map/ppermute | solution.py:333
  120.5 1.9 %collective-permute-start.16 = (bf16[128,1024]{1,0:T(8,128)(2,1)S(1)}, bf16[128,1024]{1,0:T(8,128)(2,1)S(1)}, u32[]{:S(2)}, u32[]{:S(2)}) collective-permute-start(bf16[128,1024]{1,0:T(8,128)(2,1)S(1)} %shard_map.88), channel_id=1, source_target_pairs={{0,384},{1,0},{128,1},{129,129},{256,128},{257,256},{384,257},{385... | collective-permute-start | bytes 786440 | tf_op jit(solution)/shard_map/ppermute | solution.py:333
  122.4 1.0 copy-done.2
  123.4 1.7 %shard_map.89.w_ref = bf16[4,16,16,1024]{3,2,1,0:T(8,128)(2,1)S(1)} custom-call(s32[8]{0:T(128)S(1)} %and_select_fusion.at_ref, bf16[8,2,128,128]{3,2,1,0:T(8,128)(2,1)S(1)} %pad_maximum_fusion.refs_3_.refs_0_, bf16[8,2,128,128]{3,2,1,0:T(8,128)(2,1)S(1)} %collective-permute-done.5.refs_3_.refs_1_, ...), custom_call_target="tpu_custom_call" | custom-call | bytes 4194304 | tf_op jit(solution)/shard_map/pallas_call | solution.py:220
  125.2 1.9 %collective-permute-done.15.a2 = bf16[128,1024]{1,0:T(8,128)(2,1)S(1)} collective-permute-done((bf16[128,1024]{1,0:T(8,128)(2,1)S(1)}, bf16[128,1024]{1,0:T(8,128)(2,1)S(1)}, u32[]{:S(2)}, u32[]{:S(2)}) %collective-permute-start.15) | collective-permute-done | bytes 262176 | tf_op jit(solution)/shard_map/ppermute | solution.py:333
  127.1 3.9 %collective-permute-done.16.a3 = bf16[128,1024]{1,0:T(8,128)(2,1)S(1)} collective-permute-done((bf16[128,1024]{1,0:T(8,128)(2,1)S(1)}, bf16[128,1024]{1,0:T(8,128)(2,1)S(1)}, u32[]{:S(2)}, u32[]{:S(2)}) %collective-permute-start.16) | collective-permute-done | bytes 262176 | tf_op jit(solution)/shard_map/ppermute | solution.py:333
  131.0 0.7 shard_map.91
  131.7 1.9 %collective-permute-start.17 = (f32[4,128,512]{2,1,0:T(8,128)S(1)}, f32[4,128,512]{2,1,0:T(8,128)S(1)}, u32[]{:S(2)}, u32[]{:S(2)}) collective-permute-start(f32[4,128,512]{2,1,0:T(8,128)S(1)} %shard_map.91), channel_id=1, source_target_pairs={{0,1},{1,0},{2,3},{3,2},{4,5},{5,4},{6,7},{7,6},{8,9},{9,8},{10,11... | collective-permute-start | bytes 3145736 | tf_op jit(solution)/shard_map/ppermute | solution.py:27
  133.6 0.7 shard_map.90
  134.4 1.9 %collective-permute-done.17 = f32[4,128,512]{2,1,0:T(8,128)S(1)} collective-permute-done((f32[4,128,512]{2,1,0:T(8,128)S(1)}, f32[4,128,512]{2,1,0:T(8,128)S(1)}, u32[]{:S(2)}, u32[]{:S(2)}) %collective-permute-start.17) | collective-permute-done | bytes 1048608 | tf_op jit(solution)/shard_map/ppermute | solution.py:27
  136.4 4.3 %collective-permute-start.20 = (bf16[128,512]{1,0:T(8,128)(2,1)S(1)}, bf16[128,512]{1,0:T(8,128)(2,1)S(1)}, u32[]{:S(2)}, u32[]{:S(2)}) collective-permute-start(bf16[128,512]{1,0:T(8,128)(2,1)S(1)} %get-tuple-element.32), channel_id=1, source_target_pairs={{0,6},{2,0},{4,2},{6,4},{1,7},{3,1},{5,3},{7,5},{8,14},{10,8},{12,... | collective-permute-start | bytes 393224 | tf_op jit(solution)/shard_map/ppermute | solution.py:27
  140.7 4.3 %collective-permute-start.19 = (bf16[128,512]{1,0:T(8,128)(2,1)S(1)}, bf16[128,512]{1,0:T(8,128)(2,1)S(1)}, u32[]{:S(2)}, u32[]{:S(2)}) collective-permute-start(bf16[128,512]{1,0:T(8,128)(2,1)S(1)} %get-tuple-element.33), channel_id=1, source_target_pairs={{0,4},{2,6},{4,0},{6,2},{1,5},{3,7},{5,1},{7,3},{8,12},{10,14},{12... | collective-permute-start | bytes 393224 | tf_op jit(solution)/shard_map/ppermute | solution.py:27
  145.0 2.9 %collective-permute-start.18 = (bf16[128,512]{1,0:T(8,128)(2,1)S(1)}, bf16[128,512]{1,0:T(8,128)(2,1)S(1)}, u32[]{:S(2)}, u32[]{:S(2)}) collective-permute-start(bf16[128,512]{1,0:T(8,128)(2,1)S(1)} %get-tuple-element.31), channel_id=1, source_target_pairs={{0,2},{2,4},{4,6},{6,0},{1,3},{3,5},{5,7},{7,1},{8,10},{10,12},{12... | collective-permute-start | bytes 393224 | tf_op jit(solution)/shard_map/ppermute | solution.py:27
  148.6 6.4 %collective-permute-done.19 = bf16[128,512]{1,0:T(8,128)(2,1)S(1)} collective-permute-done((bf16[128,512]{1,0:T(8,128)(2,1)S(1)}, bf16[128,512]{1,0:T(8,128)(2,1)S(1)}, u32[]{:S(2)}, u32[]{:S(2)}) %collective-permute-start.19) | collective-permute-done | bytes 131104 | tf_op jit(solution)/shard_map/ppermute | solution.py:27
  155.1 2.2 %collective-permute-start.21 = (bf16[128,512]{1,0:T(8,128)(2,1)S(1)}, bf16[128,512]{1,0:T(8,128)(2,1)S(1)}, u32[]{:S(2)}, u32[]{:S(2)}) collective-permute-start(bf16[128,512]{1,0:T(8,128)(2,1)S(1)} %fusion.10), channel_id=1, source_target_pairs={{0,0},{2,384},{4,256},{6,128},{128,130},{130,2},{132,386},{134,258... | collective-permute-start | bytes 393224 | tf_op jit(solution)/shard_map/ppermute | solution.py:348
  157.3 12.4 %collective-permute-done.21 = bf16[128,512]{1,0:T(8,128)(2,1)S(1)} collective-permute-done((bf16[128,512]{1,0:T(8,128)(2,1)S(1)}, bf16[128,512]{1,0:T(8,128)(2,1)S(1)}, u32[]{:S(2)}, u32[]{:S(2)}) %collective-permute-start.21) | collective-permute-done | bytes 131104 | tf_op jit(solution)/shard_map/ppermute | solution.py:348
  (37 shorter events, 1.7 us)
Async XLA Ops:
  0.0 76.6 %copy-start.6 = (s32[8]{0:T(128)S(1)}, s32[8]{0:T(128)}, u32[]{:S(2)}) copy-start(s32[8]{0:T(128)} %constant.109.clone) | copy-start | bytes 100
  0.0 60.3 %copy-start.5 = (s32[2,128]{1,0:T(2,128)S(1)}, s32[2,128]{1,0:T(2,128)}, u32[]{:S(2)}) copy-start(s32[2,128]{1,0:T(2,128)} %param.12) | copy-start | bytes 3076
  0.0 68.4 %copy-start.4 = (bf16[128,1024]{1,0:T(8,128)(2,1)S(1)}, bf16[128,1024]{1,0:T(8,128)(2,1)}, u32[]{:S(2)}) copy-start(bf16[128,1024]{1,0:T(8,128)(2,1)} %param.8) | copy-start | bytes 786436
  0.0 89.9 %copy-start.3 = (f32[128]{0:T(128)S(1)}, f32[128]{0:T(128)}, u32[]{:S(2)}) copy-start(f32[128]{0:T(128)} %param.11) | copy-start | bytes 1540
  1.8 31.5 %all-to-all-start = ((bf16[8,128,128]{2,1,0:T(8,128)(2,1)}), bf16[8,128,128]{2,1,0:T(8,128)(2,1)S(1)}, u32[]{:S(2)}, u32[]{:S(2)}) async-start(bf16[8,128,128]{2,1,0:T(8,128)(2,1)} %bitcast.12), calls=%async_computation | async-start | bytes 524288 | tf_op jit(solution)/shard_map/all_to_all | solution.py:283
  12.6 11.2 %collective-permute-start.3 = (bf16[1,2,128,128]{3,2,1,0:T(8,128)(2,1)S(1)}, bf16[1,2,128,128]{3,2,1,0:T(8,128)(2,1)S(1)}, u32[]{:S(2)}, u32[]{:S(2)}) collective-permute-start(bf16[1,2,128,128]{3,2,1,0:T(8,128)(2,1)S(1)} %maximum_bitcast_fusion), channel_id=1, source_target_pairs={{0,64},{1,192},{128,65},{129,193},{64,0},{65,128},{192,1},{193,129... | collective-permute-start | bytes 196616 | tf_op jit(solution)/shard_map/ppermute | solution.py:279
  19.0 5.9 %collective-permute-start.2 = (bf16[1,2,128,128]{3,2,1,0:T(8,128)(2,1)S(1)}, bf16[1,2,128,128]{3,2,1,0:T(8,128)(2,1)S(1)}, u32[]{:S(2)}, u32[]{:S(2)}) collective-permute-start(bf16[1,2,128,128]{3,2,1,0:T(8,128)(2,1)S(1)} %maximum_bitcast_fusion), channel_id=1, source_target_pairs={{0,0},{1,128},{128,1},{129,129},{64,64},{65,192},{192,65},{193,193... | collective-permute-start | bytes 196616 | tf_op jit(solution)/shard_map/ppermute | solution.py:279
  24.9 8.4 %collective-permute-start.4 = (bf16[2,2,128,128]{3,2,1,0:T(8,128)(2,1)S(1)}, bf16[2,2,128,128]{3,2,1,0:T(8,128)(2,1)S(1)}, u32[]{:S(2)}, u32[]{:S(2)}) collective-permute-start(bf16[2,2,128,128]{3,2,1,0:T(8,128)(2,1)S(1)} %pad_maximum_fusion.1), channel_id=1, source_target_pairs={{0,256},{128,384},{256,0},{384,128},{1,257},{129,385},{257,1},{385... | collective-permute-start | bytes 393224 | tf_op jit(solution)/shard_map/ppermute | solution.py:27
  33.4 19.9 %collective-permute-start.5 = (bf16[8,2,128,128]{3,2,1,0:T(8,128)(2,1)S(1)}, bf16[8,2,128,128]{3,2,1,0:T(8,128)(2,1)S(1)}, u32[]{:S(2)}, u32[]{:S(2)}) collective-permute-start(bf16[8,2,128,128]{3,2,1,0:T(8,128)(2,1)S(1)} %pad_maximum_fusion.refs_3_.refs_0_), channel_id=1, source_target_pairs={{0,8},{8,16},{16,24},{24,32},{32,40},{40,48},{48,56},{56,0},{1,9},... | collective-permute-start | bytes 1572872 | tf_op jit(solution)/shard_map/ppermute | solution.py:27
  37.6 17.5 %collective-permute-start.9 = (bf16[8,2,128,128]{3,2,1,0:T(8,128)(2,1)S(1)}, bf16[8,2,128,128]{3,2,1,0:T(8,128)(2,1)S(1)}, u32[]{:S(2)}, u32[]{:S(2)}) collective-permute-start(bf16[8,2,128,128]{3,2,1,0:T(8,128)(2,1)S(1)} %pad_maximum_fusion.refs_3_.refs_0_), channel_id=1, source_target_pairs={{0,56},{8,0},{16,8},{24,16},{32,24},{40,32},{48,40},{56,48},{1,57}... | collective-permute-start | bytes 1572872 | tf_op jit(solution)/shard_map/ppermute | solution.py:27
  53.2 13.2 %collective-permute-start.6 = (bf16[8,2,128,128]{3,2,1,0:T(8,128)(2,1)S(1)}, bf16[8,2,128,128]{3,2,1,0:T(8,128)(2,1)S(1)}, u32[]{:S(2)}, u32[]{:S(2)}) collective-permute-start(bf16[8,2,128,128]{3,2,1,0:T(8,128)(2,1)S(1)} %collective-permute-done.5.refs_3_.refs_1_), channel_id=1, source_target_pairs={{0,8},{8,16},{16,24},{24,32},{32,40},{40,48},{48,56},{56,0},{1,9},... | collective-permute-start | bytes 1572872 | tf_op jit(solution)/shard_map/ppermute | solution.py:27
  55.2 27.7 %collective-permute-start.10 = (bf16[8,2,128,128]{3,2,1,0:T(8,128)(2,1)S(1)}, bf16[8,2,128,128]{3,2,1,0:T(8,128)(2,1)}, u32[]{:S(2)}, u32[]{:S(2)}) collective-permute-start(bf16[8,2,128,128]{3,2,1,0:T(8,128)(2,1)S(1)} %collective-permute-done.9.refs_4_.refs_2_), channel_id=1, source_target_pairs={{0,56},{8,0},{16,8},{24,16},{32,24},{40,32},{48,40},{56,48},{1,57}... | collective-permute-start | bytes 1572872 | tf_op jit(solution)/shard_map/ppermute | solution.py:27
  66.5 21.4 %copy-start = (bf16[8,2,128,128]{3,2,1,0:T(8,128)(2,1)}, bf16[8,2,128,128]{3,2,1,0:T(8,128)(2,1)S(1)}, u32[]{:S(2)}) copy-start(bf16[8,2,128,128]{3,2,1,0:T(8,128)(2,1)S(1)} %collective-permute-done.6.refs_3_) | copy-start | bytes 1572868
  66.5 21.4 %collective-permute-start.7 = (bf16[8,2,128,128]{3,2,1,0:T(8,128)(2,1)S(1)}, bf16[8,2,128,128]{3,2,1,0:T(8,128)(2,1)}, u32[]{:S(2)}, u32[]{:S(2)}) collective-permute-start(bf16[8,2,128,128]{3,2,1,0:T(8,128)(2,1)S(1)} %collective-permute-done.6.refs_3_), channel_id=1, source_target_pairs={{0,8},{8,16},{16,24},{24,32},{32,40},{40,48},{48,56},{56,0},{1,9},... | collective-permute-start | bytes 1572872 | tf_op jit(solution)/shard_map/ppermute | solution.py:27
  68.4 12.5 %collective-permute-start = (bf16[144,1024]{1,0:T(8,128)(2,1)S(1)}, bf16[144,1024]{1,0:T(8,128)(2,1)S(1)}, u32[]{:S(2)}, u32[]{:S(2)}) collective-permute-start(bf16[144,1024]{1,0:T(8,128)(2,1)S(1)} %fusion.1), channel_id=1, source_target_pairs={{0,0},{1,128},{128,1},{129,129},{64,64},{65,192},{192,65},{193,193... | collective-permute-start | bytes 884744 | tf_op jit(solution)/shard_map/ppermute | solution.py:279
  80.9 9.0 %collective-permute-start.1 = (bf16[144,1024]{1,0:T(8,128)(2,1)S(1)}, bf16[144,1024]{1,0:T(8,128)(2,1)S(1)}, u32[]{:S(2)}, u32[]{:S(2)}) collective-permute-start(bf16[144,1024]{1,0:T(8,128)(2,1)S(1)} %collective-permute-done.refs_1_), channel_id=1, source_target_pairs={{0,1},{1,0},{2,3},{3,2},{4,5},{5,4},{6,7},{7,6},{8,9},{9,8},{10,11... | collective-permute-start | bytes 884744 | tf_op jit(solution)/shard_map/ppermute | solution.py:27
  82.9 17.2 %collective-permute-start.11 = (bf16[8,2,128,128]{3,2,1,0:T(8,128)(2,1)}, bf16[8,2,128,128]{3,2,1,0:T(8,128)(2,1)}, u32[]{:S(2)}, u32[]{:S(2)}) collective-permute-start(bf16[8,2,128,128]{3,2,1,0:T(8,128)(2,1)} %collective-permute-done.10.refs_4_), channel_id=1, source_target_pairs={{0,56},{8,0},{16,8},{24,16},{32,24},{40,32},{48,40},{56,48},{1,57}... | collective-permute-start | bytes 1572872 | tf_op jit(solution)/shard_map/ppermute | solution.py:27
  87.8 17.4 %collective-permute-start.8 = (bf16[8,2,128,128]{3,2,1,0:T(8,128)(2,1)}, bf16[8,2,128,128]{3,2,1,0:T(8,128)(2,1)S(1)}, u32[]{:S(2)}, u32[]{:S(2)}) collective-permute-start(bf16[8,2,128,128]{3,2,1,0:T(8,128)(2,1)} %collective-permute-done.7.refs_3_.refs_5_), channel_id=1, source_target_pairs={{0,8},{8,16},{16,24},{24,32},{32,40},{40,48},{48,56},{56,0},{1,9},... | collective-permute-start | bytes 1572872 | tf_op jit(solution)/shard_map/ppermute | solution.py:27
  92.3 3.6 %copy-start.1 = (bf16[8,2,128,128]{3,2,1,0:T(8,128)(2,1)S(1)}, bf16[8,2,128,128]{3,2,1,0:T(8,128)(2,1)}, u32[]{:S(2)}) copy-start(bf16[8,2,128,128]{3,2,1,0:T(8,128)(2,1)} %copy-done) | copy-start | bytes 1572868
  106.8 3.9 %collective-permute-start.12 = (f32[144,1024]{1,0:T(8,128)S(1)}, f32[144,1024]{1,0:T(8,128)S(1)}, u32[]{:S(2)}, u32[]{:S(2)}) collective-permute-start(f32[144,1024]{1,0:T(8,128)S(1)} %shard_map.87), channel_id=1, source_target_pairs={{0,1},{1,0},{2,3},{3,2},{4,5},{5,4},{6,7},{7,6},{8,9},{9,8},{10,11... | collective-permute-start | bytes 1769480 | tf_op jit(solution)/shard_map/ppermute | solution.py:27
  110.9 14.3 %collective-permute-start.13 = (bf16[128,1024]{1,0:T(8,128)(2,1)S(1)}, bf16[128,1024]{1,0:T(8,128)(2,1)S(1)}, u32[]{:S(2)}, u32[]{:S(2)}) collective-permute-start(bf16[128,1024]{1,0:T(8,128)(2,1)S(1)} %shard_map.88), channel_id=1, source_target_pairs={{0,0},{1,128},{128,129},{129,257},{256,256},{257,384},{384,385},{3... | collective-permute-start | bytes 786440 | tf_op jit(solution)/shard_map/ppermute | solution.py:333
  113.2 12.0 %collective-permute-start.14 = (bf16[128,1024]{1,0:T(8,128)(2,1)S(1)}, bf16[128,1024]{1,0:T(8,128)(2,1)S(1)}, u32[]{:S(2)}, u32[]{:S(2)}) collective-permute-start(bf16[128,1024]{1,0:T(8,128)(2,1)S(1)} %shard_map.88), channel_id=1, source_target_pairs={{0,128},{1,256},{128,257},{129,385},{256,384},{257,0},{384,1},{385... | collective-permute-start | bytes 786440 | tf_op jit(solution)/shard_map/ppermute | solution.py:333
  115.2 11.9 %collective-permute-start.15 = (bf16[128,1024]{1,0:T(8,128)(2,1)S(1)}, bf16[128,1024]{1,0:T(8,128)(2,1)S(1)}, u32[]{:S(2)}, u32[]{:S(2)}) collective-permute-start(bf16[128,1024]{1,0:T(8,128)(2,1)S(1)} %shard_map.88), channel_id=1, source_target_pairs={{0,256},{1,384},{128,385},{129,1},{256,0},{257,128},{384,129},{385... | collective-permute-start | bytes 786440 | tf_op jit(solution)/shard_map/ppermute | solution.py:333
  120.5 10.5 %collective-permute-start.16 = (bf16[128,1024]{1,0:T(8,128)(2,1)S(1)}, bf16[128,1024]{1,0:T(8,128)(2,1)S(1)}, u32[]{:S(2)}, u32[]{:S(2)}) collective-permute-start(bf16[128,1024]{1,0:T(8,128)(2,1)S(1)} %shard_map.88), channel_id=1, source_target_pairs={{0,384},{1,0},{128,1},{129,129},{256,128},{257,256},{384,257},{385... | collective-permute-start | bytes 786440 | tf_op jit(solution)/shard_map/ppermute | solution.py:333
  122.4 1.0 copy-start.2
  131.7 4.6 %collective-permute-start.17 = (f32[4,128,512]{2,1,0:T(8,128)S(1)}, f32[4,128,512]{2,1,0:T(8,128)S(1)}, u32[]{:S(2)}, u32[]{:S(2)}) collective-permute-start(f32[4,128,512]{2,1,0:T(8,128)S(1)} %shard_map.91), channel_id=1, source_target_pairs={{0,1},{1,0},{2,3},{3,2},{4,5},{5,4},{6,7},{7,6},{8,9},{9,8},{10,11... | collective-permute-start | bytes 3145736 | tf_op jit(solution)/shard_map/ppermute | solution.py:27
  136.4 12.1 %collective-permute-start.20 = (bf16[128,512]{1,0:T(8,128)(2,1)S(1)}, bf16[128,512]{1,0:T(8,128)(2,1)S(1)}, u32[]{:S(2)}, u32[]{:S(2)}) collective-permute-start(bf16[128,512]{1,0:T(8,128)(2,1)S(1)} %get-tuple-element.32), channel_id=1, source_target_pairs={{0,6},{2,0},{4,2},{6,4},{1,7},{3,1},{5,3},{7,5},{8,14},{10,8},{12,... | collective-permute-start | bytes 393224 | tf_op jit(solution)/shard_map/ppermute | solution.py:27
  140.7 14.3 %collective-permute-start.19 = (bf16[128,512]{1,0:T(8,128)(2,1)S(1)}, bf16[128,512]{1,0:T(8,128)(2,1)S(1)}, u32[]{:S(2)}, u32[]{:S(2)}) collective-permute-start(bf16[128,512]{1,0:T(8,128)(2,1)S(1)} %get-tuple-element.33), channel_id=1, source_target_pairs={{0,4},{2,6},{4,0},{6,2},{1,5},{3,7},{5,1},{7,3},{8,12},{10,14},{12... | collective-permute-start | bytes 393224 | tf_op jit(solution)/shard_map/ppermute | solution.py:27
  145.0 10.0 %collective-permute-start.18 = (bf16[128,512]{1,0:T(8,128)(2,1)S(1)}, bf16[128,512]{1,0:T(8,128)(2,1)S(1)}, u32[]{:S(2)}, u32[]{:S(2)}) collective-permute-start(bf16[128,512]{1,0:T(8,128)(2,1)S(1)} %get-tuple-element.31), channel_id=1, source_target_pairs={{0,2},{2,4},{4,6},{6,0},{1,3},{3,5},{5,7},{7,1},{8,10},{10,12},{12... | collective-permute-start | bytes 393224 | tf_op jit(solution)/shard_map/ppermute | solution.py:27
  155.1 14.5 %collective-permute-start.21 = (bf16[128,512]{1,0:T(8,128)(2,1)S(1)}, bf16[128,512]{1,0:T(8,128)(2,1)S(1)}, u32[]{:S(2)}, u32[]{:S(2)}) collective-permute-start(bf16[128,512]{1,0:T(8,128)(2,1)S(1)} %fusion.10), channel_id=1, source_target_pairs={{0,0},{2,384},{4,256},{6,128},{128,130},{130,2},{132,386},{134,258... | collective-permute-start | bytes 393224 | tf_op jit(solution)/shard_map/ppermute | solution.py:348

commit v6 on v5

--- a/solution.py
+++ b/solution.py
@@ -209,7 +209,7 @@
         for y in range(2):
             for x in range(4):
                 tile = x * 2 + y
-                block = chunks[p][BLOCKS + tile // 2, tile % 2]
+                block = chunks[p][tile // 2, tile % 2]
                 for t in range(8):
                     out_ref[x, y * 8 + at_ref[p], :, t * 128 : (t + 1) * 128] = block[
                         t * 16 : (t + 1) * 16
@@ -305,10 +305,11 @@
     packs = (near, far)
 
     right, left = [chunk], [chunk]
-    for s in range(1, 5):
+    for _ in range(1, 4):
         right.append(shift(right[-1], "z", 1))
-        if s < 4:
-            left.append(shift(left[-1], "z", -1))
+        left.append(shift(left[-1], "z", -1))
+    right.append(shift(right[3][:BLOCKS], "z", 1))
+    left.append(shift(left[3][BLOCKS:], "z", -1))
     gain = q_gain[None, :]
     state = attend(ids, 0, packs, [chunk], gain, None)
     for s in range(1, 4):
@@ -331,7 +332,10 @@
             (x * 2 + c, ((x + k + c) % 4) * 2 + x % 2) for x in range(4) for c in range(2)
         ]
         slots.append(lax.ppermute(attended, ("x", "c"), pairs))
-    parts = [chunk, right[1], left[1], right[2], left[2], right[3], left[3], right[4]]
+    parts = []
+    for s in range(4):
+        parts += [c[BLOCKS:] for c in ([chunk] if s == 0 else [right[s], left[s]])]
+    parts.append(left[4])
     weight = assemble(at, parts)
 
     core = core.astype(jnp.int32)[None]

time: 171 us -> 175 us (1.023)
  the two profiles are of different devices: /device:TPU:6 before, /device:TPU:59 now
where the time goes in v6:
time: 175 us; the launch traced here: 174 us
  starting transfers between devices  94.5 us (54%)
  waiting for transfers between devices  51.3 us (29%)
  Pallas kernels  20.1 us (11%)
  local copies, waits for them, and re-layouts  5.48 us (3%)
    ppermute x15, starting transfers between devices, shift(): lax.ppermute(value, axis, [(s, (s + steps) % count) for s in range(count)])  61.2 us
    ppermute x15, waiting for transfers between devices, shift(): lax.ppermute(value, axis, [(s, (s + steps) % count) for s in range(count)])  25.3 us
    pallas_call x6, Pallas kernels, attend(): pl.pallas_call(body, out_shape=out_shape, in_specs=[SMEM] + [VMEM] * (2 +...  17.6 us
    ppermute x4, starting transfers between devices, work(): slots.append(lax.ppermute(attended, ('x', 'c'), pairs))  17.5 us
    ppermute x1, waiting for transfers between devices, work(): return lax.ppermute(result, ('x', 'yl'), pairs)  11.3 us
    all_to_all x1, starting transfers between devices, work(): lax.all_to_all(quarter, ('x', 'yh'), split_axis=0, concat_axis=0, tiled=T...  9.08 us
    ppermute x3, waiting for transfers between devices, trade(): return lax.ppermute(value, ('x', 'yh', 'c'), pairs)  8.79 us
    ppermute x4, waiting for transfers between devices, work(): slots.append(lax.ppermute(attended, ('x', 'c'), pairs))  6.02 us
  transfers between devices with their start and end apart: 24, of which 9 were waited for; matrix products, arithmetic and copies ran while one was open for 2% of the time, Pallas kernels for 10%

profile of v6, /device:TPU:59, one launch (start us, length us, event | category | flops | bytes accessed | tf_op | source)
XLA Modules:
  0.0 174.0 jit_solution(12016775084131478708)
XLA Ops:
  0.0 1.0 copy.11
  1.1 0.7 broadcast_in_dim.21
  1.8 9.1 %all-to-all-start = ((bf16[8,128,128]{2,1,0:T(8,128)(2,1)}), bf16[8,128,128]{2,1,0:T(8,128)(2,1)S(1)}, u32[]{:S(2)}, u32[]{:S(2)}) async-start(bf16[8,128,128]{2,1,0:T(8,128)(2,1)} %bitcast.12), calls=%async_computation | async-start | bytes 524288 | tf_op jit(solution)/shard_map/all_to_all | solution.py:283
  10.9 0.8 maximum_bitcast_fusion
  11.6 0.7 collective-permute-start.2
  12.3 2.2 %collective-permute-start.3 = (bf16[1,2,128,128]{3,2,1,0:T(8,128)(2,1)S(1)}, bf16[1,2,128,128]{3,2,1,0:T(8,128)(2,1)S(1)}, u32[]{:S(2)}, u32[]{:S(2)}) collective-permute-start(bf16[1,2,128,128]{3,2,1,0:T(8,128)(2,1)S(1)} %maximum_bitcast_fusion), channel_id=1, source_target_pairs={{0,64},{1,192},{128,65},{129,193},{64,0},{65,128},{192,1},{193,129... | collective-permute-start | bytes 196616 | tf_op jit(solution)/shard_map/ppermute | solution.py:279
  14.5 8.8 %collective-permute-done.3 = bf16[1,2,128,128]{3,2,1,0:T(8,128)(2,1)S(1)} collective-permute-done((bf16[1,2,128,128]{3,2,1,0:T(8,128)(2,1)S(1)}, bf16[1,2,128,128]{3,2,1,0:T(8,128)(2,1)S(1)}, u32[]{:S(2)}, u32[]{:S(2)}) %collective-permute-start.3) | collective-permute-done | bytes 65568 | tf_op jit(solution)/shard_map/ppermute | solution.py:279
  23.3 3.7 %collective-permute-start.4 = (bf16[2,2,128,128]{3,2,1,0:T(8,128)(2,1)S(1)}, bf16[2,2,128,128]{3,2,1,0:T(8,128)(2,1)S(1)}, u32[]{:S(2)}, u32[]{:S(2)}) collective-permute-start(bf16[2,2,128,128]{3,2,1,0:T(8,128)(2,1)S(1)} %pad_maximum_fusion.1), channel_id=1, source_target_pairs={{0,256},{128,384},{256,0},{384,128},{1,257},{129,385},{257,1},{385... | collective-permute-start | bytes 393224 | tf_op jit(solution)/shard_map/ppermute | solution.py:27
  27.0 3.5 %collective-permute-done.4 = bf16[2,2,128,128]{3,2,1,0:T(8,128)(2,1)S(1)} collective-permute-done((bf16[2,2,128,128]{3,2,1,0:T(8,128)(2,1)S(1)}, bf16[2,2,128,128]{3,2,1,0:T(8,128)(2,1)S(1)}, u32[]{:S(2)}, u32[]{:S(2)}) %collective-permute-start.4) | collective-permute-done | bytes 131104 | tf_op jit(solution)/shard_map/ppermute | solution.py:27
  30.6 4.0 %collective-permute-start.5 = (bf16[8,2,128,128]{3,2,1,0:T(8,128)(2,1)S(1)}, bf16[8,2,128,128]{3,2,1,0:T(8,128)(2,1)S(1)}, u32[]{:S(2)}, u32[]{:S(2)}) collective-permute-start(bf16[8,2,128,128]{3,2,1,0:T(8,128)(2,1)S(1)} %pad_maximum_fusion.refs_3_), channel_id=1, source_target_pairs={{0,8},{8,16},{16,24},{24,32},{32,40},{40,48},{48,56},{56,0},{1,9},... | collective-permute-start | bytes 1572872 | tf_op jit(solution)/shard_map/ppermute | solution.py:27
  34.6 8.6 %collective-permute-start.9 = (bf16[8,2,128,128]{3,2,1,0:T(8,128)(2,1)S(1)}, bf16[8,2,128,128]{3,2,1,0:T(8,128)(2,1)S(1)}, u32[]{:S(2)}, u32[]{:S(2)}) collective-permute-start(bf16[8,2,128,128]{3,2,1,0:T(8,128)(2,1)S(1)} %pad_maximum_fusion.refs_3_), channel_id=1, source_target_pairs={{0,56},{8,0},{16,8},{24,16},{32,24},{40,32},{48,40},{56,48},{1,57}... | collective-permute-start | bytes 1572872 | tf_op jit(solution)/shard_map/ppermute | solution.py:27
  43.2 7.2 %collective-permute-done.5.refs_3_ = bf16[8,2,128,128]{3,2,1,0:T(8,128)(2,1)S(1)} collective-permute-done((bf16[8,2,128,128]{3,2,1,0:T(8,128)(2,1)S(1)}, bf16[8,2,128,128]{3,2,1,0:T(8,128)(2,1)S(1)}, u32[]{:S(2)}, u32[]{:S(2)}) %collective-permute-start.5) | collective-permute-done | bytes 524320 | tf_op jit(solution)/shard_map/ppermute | solution.py:27
  50.4 1.9 %collective-permute-start.6 = (bf16[8,2,128,128]{3,2,1,0:T(8,128)(2,1)S(1)}, bf16[8,2,128,128]{3,2,1,0:T(8,128)(2,1)}, u32[]{:S(2)}, u32[]{:S(2)}) collective-permute-start(bf16[8,2,128,128]{3,2,1,0:T(8,128)(2,1)S(1)} %collective-permute-done.5.refs_3_), channel_id=1, source_target_pairs={{0,8},{8,16},{16,24},{24,32},{32,40},{40,48},{48,56},{56,0},{1,9},... | collective-permute-start | bytes 1572872 | tf_op jit(solution)/shard_map/ppermute | solution.py:27
  52.4 4.6 %collective-permute-start.10 = (bf16[8,2,128,128]{3,2,1,0:T(8,128)(2,1)S(1)}, bf16[8,2,128,128]{3,2,1,0:T(8,128)(2,1)}, u32[]{:S(2)}, u32[]{:S(2)}) collective-permute-start(bf16[8,2,128,128]{3,2,1,0:T(8,128)(2,1)S(1)} %collective-permute-done.9.refs_4_), channel_id=1, source_target_pairs={{0,56},{8,0},{16,8},{24,16},{32,24},{40,32},{48,40},{56,48},{1,57}... | collective-permute-start | bytes 1572872 | tf_op jit(solution)/shard_map/ppermute | solution.py:27
  57.0 0.7 collective-permute-start
  57.7 5.6 %collective-permute-done.6.refs_3_ = bf16[8,2,128,128]{3,2,1,0:T(8,128)(2,1)} collective-permute-done((bf16[8,2,128,128]{3,2,1,0:T(8,128)(2,1)S(1)}, bf16[8,2,128,128]{3,2,1,0:T(8,128)(2,1)}, u32[]{:S(2)}, u32[]{:S(2)}) %collective-permute-start.6) | collective-permute-done | bytes 524320 | tf_op jit(solution)/shard_map/ppermute | solution.py:27
  63.4 1.9 %collective-permute-start.7 = (bf16[8,2,128,128]{3,2,1,0:T(8,128)(2,1)}, bf16[8,2,128,128]{3,2,1,0:T(8,128)(2,1)S(1)}, u32[]{:S(2)}, u32[]{:S(2)}) collective-permute-start(bf16[8,2,128,128]{3,2,1,0:T(8,128)(2,1)} %collective-permute-done.6.refs_3_), channel_id=1, source_target_pairs={{0,8},{8,16},{16,24},{24,32},{32,40},{40,48},{48,56},{56,0},{1,9},... | collective-permute-start | bytes 1572872 | tf_op jit(solution)/shard_map/ppermute | solution.py:27
  65.3 6.5 %collective-permute-start.1 = (bf16[144,1024]{1,0:T(8,128)(2,1)S(1)}, bf16[144,1024]{1,0:T(8,128)(2,1)S(1)}, u32[]{:S(2)}, u32[]{:S(2)}) collective-permute-start(bf16[144,1024]{1,0:T(8,128)(2,1)S(1)} %collective-permute-done.refs_1_), channel_id=1, source_target_pairs={{0,1},{1,0},{2,3},{3,2},{4,5},{5,4},{6,7},{7,6},{8,9},{9,8},{10,11... | collective-permute-start | bytes 884744 | tf_op jit(solution)/shard_map/ppermute | solution.py:27
  71.9 4.8 %collective-permute-start.11 = (bf16[8,2,128,128]{3,2,1,0:T(8,128)(2,1)}, bf16[8,2,128,128]{3,2,1,0:T(8,128)(2,1)}, u32[]{:S(2)}, u32[]{:S(2)}) collective-permute-start(bf16[8,2,128,128]{3,2,1,0:T(8,128)(2,1)} %collective-permute-done.10.refs_4_), channel_id=1, source_target_pairs={{0,56},{8,0},{16,8},{24,16},{32,24},{40,32},{48,40},{56,48},{1,57}... | collective-permute-start | bytes 1572872 | tf_op jit(solution)/shard_map/ppermute | solution.py:27
  76.9 2.4 %shard_map.82 = (bf16[2048,128]{1,0:T(8,128)(2,1)S(1)}, f32[1,2048]{1,0:T(1,128)S(1)}, f32[8,2048]{1,0:T(8,128)S(1)}, f32[128,2048]{1,0:T(8,128)S(1)}) custom-call(s32[32]{0:T(128)S(1)} %add.127.refs_0_, bf16[144,1024]{1,0:T(8,128)(2,1)S(1)} %collective-permute-done.refs_1_, bf16[144,1024]{1,0:T(8,128)(2,1)S(1)} %collective-permute-done.1.refs_2_, ...), custom_call_target="tpu_custom_call" | custom-call | flops 536870912 | bytes 3407872 | tf_op jit(solution)/shard_map/pallas_call | solution.py:163
  79.4 2.1 %collective-permute-start.8 = (bf16[4,2,128,128]{3,2,1,0:T(8,128)(2,1)S(1)}, bf16[4,2,128,128]{3,2,1,0:T(8,128)(2,1)S(1)}, u32[]{:S(2)}, u32[]{:S(2)}) collective-permute-start(bf16[4,2,128,128]{3,2,1,0:T(8,128)(2,1)S(1)} %get-tuple-element.35), channel_id=1, source_target_pairs={{0,8},{8,16},{16,24},{24,32},{32,40},{40,48},{48,56},{56,0},{1,9},... | collective-permute-start | bytes 786440 | tf_op jit(solution)/shard_map/ppermute | solution.py:27
  81.5 3.6 %shard_map.83 = (f32[1,2048]{1,0:T(1,128)S(1)}, f32[8,2048]{1,0:T(8,128)S(1)}, f32[128,2048]{1,0:T(8,128)S(1)}) custom-call(s32[32]{0:T(128)S(1)} %add.127.refs_0_, bf16[144,1024]{1,0:T(8,128)(2,1)S(1)} %collective-permute-done.refs_1_, bf16[144,1024]{1,0:T(8,128)(2,1)S(1)} %collective-permute-done.1.refs_2_, ...), custom_call_target="tpu_custom_call" | custom-call | flops 1073741824 | bytes 3670016 | tf_op jit(solution)/shard_map/pallas_call | solution.py:163
  85.1 4.3 %shard_map.84 = (f32[1,2048]{1,0:T(1,128)S(1)}, f32[8,2048]{1,0:T(8,128)S(1)}, f32[128,2048]{1,0:T(8,128)S(1)}) custom-call(s32[32]{0:T(128)S(1)} %add.127.refs_0_, bf16[144,1024]{1,0:T(8,128)(2,1)S(1)} %collective-permute-done.refs_1_, bf16[144,1024]{1,0:T(8,128)(2,1)S(1)} %collective-permute-done.1.refs_2_, ...), custom_call_target="tpu_custom_call" | custom-call | flops 1073741824 | bytes 3670016 | tf_op jit(solution)/shard_map/pallas_call | solution.py:163
  89.4 4.1 %shard_map.85 = (f32[1,2048]{1,0:T(1,128)S(1)}, f32[8,2048]{1,0:T(8,128)S(1)}, f32[128,2048]{1,0:T(8,128)S(1)}) custom-call(s32[32]{0:T(128)S(1)} %add.127.refs_0_, bf16[144,1024]{1,0:T(8,128)(2,1)S(1)} %collective-permute-done.refs_1_, bf16[144,1024]{1,0:T(8,128)(2,1)S(1)} %collective-permute-done.1.refs_2_, ...), custom_call_target="tpu_custom_call" | custom-call | flops 1073741824 | bytes 3670016 | tf_op jit(solution)/shard_map/pallas_call | solution.py:163
  93.5 1.6 shard_map.87
  95.1 3.6 %collective-permute-start.12 = (f32[144,1024]{1,0:T(8,128)S(1)}, f32[144,1024]{1,0:T(8,128)S(1)}, u32[]{:S(2)}, u32[]{:S(2)}) collective-permute-start(f32[144,1024]{1,0:T(8,128)S(1)} %shard_map.87), channel_id=1, source_target_pairs={{0,1},{1,0},{2,3},{3,2},{4,5},{5,4},{6,7},{7,6},{8,9},{9,8},{10,11... | collective-permute-start | bytes 1769480 | tf_op jit(solution)/shard_map/ppermute | solution.py:27
  98.7 1.0 slice.67.refs_6_
  99.7 4.8 %collective-permute-start.17 = (bf16[4,2,128,128]{3,2,1,0:T(8,128)(2,1)S(1)}, bf16[4,2,128,128]{3,2,1,0:T(8,128)(2,1)S(1)}, u32[]{:S(2)}, u32[]{:S(2)}) collective-permute-start(bf16[4,2,128,128]{3,2,1,0:T(8,128)(2,1)S(1)} %slice.67.refs_6_), channel_id=1, source_target_pairs={{0,56},{8,0},{16,8},{24,16},{32,24},{40,32},{48,40},{56,48},{1,57}... | collective-permute-start | bytes 786440 | tf_op jit(solution)/shard_map/ppermute | solution.py:27
  104.5 1.6 shard_map.86.a_ref
  106.4 12.3 %collective-permute-start.13 = (bf16[128,1024]{1,0:T(8,128)(2,1)S(1)}, bf16[128,1024]{1,0:T(8,128)(2,1)S(1)}, u32[]{:S(2)}, u32[]{:S(2)}) collective-permute-start(bf16[128,1024]{1,0:T(8,128)(2,1)S(1)} %shard_map.88), channel_id=1, source_target_pairs={{0,0},{1,128},{128,129},{129,257},{256,256},{257,384},{384,385},{3... | collective-permute-start | bytes 786440 | tf_op jit(solution)/shard_map/ppermute | solution.py:334
  118.7 2.2 %collective-permute-start.14 = (bf16[128,1024]{1,0:T(8,128)(2,1)S(1)}, bf16[128,1024]{1,0:T(8,128)(2,1)S(1)}, u32[]{:S(2)}, u32[]{:S(2)}) collective-permute-start(bf16[128,1024]{1,0:T(8,128)(2,1)S(1)} %shard_map.88), channel_id=1, source_target_pairs={{0,128},{1,256},{128,257},{129,385},{256,384},{257,0},{384,1},{385... | collective-permute-start | bytes 786440 | tf_op jit(solution)/shard_map/ppermute | solution.py:334
  120.9 2.3 %collective-permute-start.15 = (bf16[128,1024]{1,0:T(8,128)(2,1)S(1)}, bf16[128,1024]{1,0:T(8,128)(2,1)S(1)}, u32[]{:S(2)}, u32[]{:S(2)}) collective-permute-start(bf16[128,1024]{1,0:T(8,128)(2,1)S(1)} %shard_map.88), channel_id=1, source_target_pairs={{0,256},{1,384},{128,385},{129,1},{256,0},{257,128},{384,129},{385... | collective-permute-start | bytes 786440 | tf_op jit(solution)/shard_map/ppermute | solution.py:334
  123.2 0.7 collective-permute-start.16
  124.0 1.0 slice.64.refs_3_
  125.0 1.0 slice.65.refs_4_
  126.0 0.9 shard_map.89.w_ref
  127.5 5.4 %collective-permute-done.15.a2 = bf16[128,1024]{1,0:T(8,128)(2,1)S(1)} collective-permute-done((bf16[128,1024]{1,0:T(8,128)(2,1)S(1)}, bf16[128,1024]{1,0:T(8,128)(2,1)S(1)}, u32[]{:S(2)}, u32[]{:S(2)}) %collective-permute-start.15) | collective-permute-done | bytes 262176 | tf_op jit(solution)/shard_map/ppermute | solution.py:334
  132.9 0.7 shard_map.91
  133.6 5.4 %collective-permute-start.18 = (f32[4,128,512]{2,1,0:T(8,128)S(1)}, f32[4,128,512]{2,1,0:T(8,128)S(1)}, u32[]{:S(2)}, u32[]{:S(2)}) collective-permute-start(f32[4,128,512]{2,1,0:T(8,128)S(1)} %shard_map.91), channel_id=1, source_target_pairs={{0,1},{1,0},{2,3},{3,2},{4,5},{5,4},{6,7},{7,6},{8,9},{9,8},{10,11... | collective-permute-start | bytes 3145736 | tf_op jit(solution)/shard_map/ppermute | solution.py:27
  139.0 0.7 shard_map.90
  139.8 1.6 collective-permute-done.18
  141.5 4.1 %collective-permute-start.19 = (bf16[128,512]{1,0:T(8,128)(2,1)S(1)}, bf16[128,512]{1,0:T(8,128)(2,1)S(1)}, u32[]{:S(2)}, u32[]{:S(2)}) collective-permute-start(bf16[128,512]{1,0:T(8,128)(2,1)S(1)} %get-tuple-element.31), channel_id=1, source_target_pairs={{0,2},{2,4},{4,6},{6,0},{1,3},{3,5},{5,7},{7,1},{8,10},{10,12},{12... | collective-permute-start | bytes 393224 | tf_op jit(solution)/shard_map/ppermute | solution.py:27
  145.6 1.9 %collective-permute-start.20 = (bf16[128,512]{1,0:T(8,128)(2,1)S(1)}, bf16[128,512]{1,0:T(8,128)(2,1)S(1)}, u32[]{:S(2)}, u32[]{:S(2)}) collective-permute-start(bf16[128,512]{1,0:T(8,128)(2,1)S(1)} %get-tuple-element.33), channel_id=1, source_target_pairs={{0,4},{2,6},{4,0},{6,2},{1,5},{3,7},{5,1},{7,3},{8,12},{10,14},{12... | collective-permute-start | bytes 393224 | tf_op jit(solution)/shard_map/ppermute | solution.py:27
  147.5 3.3 %collective-permute-start.21 = (bf16[128,512]{1,0:T(8,128)(2,1)S(1)}, bf16[128,512]{1,0:T(8,128)(2,1)S(1)}, u32[]{:S(2)}, u32[]{:S(2)}) collective-permute-start(bf16[128,512]{1,0:T(8,128)(2,1)S(1)} %get-tuple-element.32), channel_id=1, source_target_pairs={{0,6},{2,0},{4,2},{6,4},{1,7},{3,1},{5,3},{7,5},{8,14},{10,8},{12,... | collective-permute-start | bytes 393224 | tf_op jit(solution)/shard_map/ppermute | solution.py:27
  151.5 7.3 %collective-permute-done.20 = bf16[128,512]{1,0:T(8,128)(2,1)S(1)} collective-permute-done((bf16[128,512]{1,0:T(8,128)(2,1)S(1)}, bf16[128,512]{1,0:T(8,128)(2,1)S(1)}, u32[]{:S(2)}, u32[]{:S(2)}) %collective-permute-start.20) | collective-permute-done | bytes 131104 | tf_op jit(solution)/shard_map/ppermute | solution.py:27
  158.9 3.2 %collective-permute-start.22 = (bf16[128,512]{1,0:T(8,128)(2,1)S(1)}, bf16[128,512]{1,0:T(8,128)(2,1)S(1)}, u32[]{:S(2)}, u32[]{:S(2)}) collective-permute-start(bf16[128,512]{1,0:T(8,128)(2,1)S(1)} %fusion.10), channel_id=1, source_target_pairs={{0,0},{2,384},{4,256},{6,128},{128,130},{130,2},{132,386},{134,258... | collective-permute-start | bytes 393224 | tf_op jit(solution)/shard_map/ppermute | solution.py:352
  162.1 11.3 %collective-permute-done.22 = bf16[128,512]{1,0:T(8,128)(2,1)S(1)} collective-permute-done((bf16[128,512]{1,0:T(8,128)(2,1)S(1)}, bf16[128,512]{1,0:T(8,128)(2,1)S(1)}, u32[]{:S(2)}, u32[]{:S(2)}) %collective-permute-start.22) | collective-permute-done | bytes 131104 | tf_op jit(solution)/shard_map/ppermute | solution.py:352
  173.4 0.7 copy.14
  (39 shorter events, 1.5 us)
Async XLA Ops:
  0.0 65.3 %copy-start.3 = (s32[8]{0:T(128)S(1)}, s32[8]{0:T(128)}, u32[]{:S(2)}) copy-start(s32[8]{0:T(128)} %constant.109.clone) | copy-start | bytes 100
  0.0 52.3 %copy-start.2 = (s32[2,128]{1,0:T(2,128)S(1)}, s32[2,128]{1,0:T(2,128)}, u32[]{:S(2)}) copy-start(s32[2,128]{1,0:T(2,128)} %param.12) | copy-start | bytes 3076
  0.0 56.9 %copy-start.1 = (bf16[128,1024]{1,0:T(8,128)(2,1)S(1)}, bf16[128,1024]{1,0:T(8,128)(2,1)}, u32[]{:S(2)}) copy-start(bf16[128,1024]{1,0:T(8,128)(2,1)} %param.8) | copy-start | bytes 786436
  0.0 76.9 %copy-start = (f32[128]{0:T(128)S(1)}, f32[128]{0:T(128)}, u32[]{:S(2)}) copy-start(f32[128]{0:T(128)} %param.11) | copy-start | bytes 1540
  1.8 28.8 %all-to-all-start = ((bf16[8,128,128]{2,1,0:T(8,128)(2,1)}), bf16[8,128,128]{2,1,0:T(8,128)(2,1)S(1)}, u32[]{:S(2)}, u32[]{:S(2)}) async-start(bf16[8,128,128]{2,1,0:T(8,128)(2,1)} %bitcast.12), calls=%async_computation | async-start | bytes 524288 | tf_op jit(solution)/shard_map/all_to_all | solution.py:283
  11.6 2.9 %collective-permute-start.2 = (bf16[1,2,128,128]{3,2,1,0:T(8,128)(2,1)S(1)}, bf16[1,2,128,128]{3,2,1,0:T(8,128)(2,1)S(1)}, u32[]{:S(2)}, u32[]{:S(2)}) collective-permute-start(bf16[1,2,128,128]{3,2,1,0:T(8,128)(2,1)S(1)} %maximum_bitcast_fusion), channel_id=1, source_target_pairs={{0,0},{1,128},{128,1},{129,129},{64,64},{65,192},{192,65},{193,193... | collective-permute-start | bytes 196616 | tf_op jit(solution)/shard_map/ppermute | solution.py:279
  12.3 11.0 %collective-permute-start.3 = (bf16[1,2,128,128]{3,2,1,0:T(8,128)(2,1)S(1)}, bf16[1,2,128,128]{3,2,1,0:T(8,128)(2,1)S(1)}, u32[]{:S(2)}, u32[]{:S(2)}) collective-permute-start(bf16[1,2,128,128]{3,2,1,0:T(8,128)(2,1)S(1)} %maximum_bitcast_fusion), channel_id=1, source_target_pairs={{0,64},{1,192},{128,65},{129,193},{64,0},{65,128},{192,1},{193,129... | collective-permute-start | bytes 196616 | tf_op jit(solution)/shard_map/ppermute | solution.py:279
  23.3 7.2 %collective-permute-start.4 = (bf16[2,2,128,128]{3,2,1,0:T(8,128)(2,1)S(1)}, bf16[2,2,128,128]{3,2,1,0:T(8,128)(2,1)S(1)}, u32[]{:S(2)}, u32[]{:S(2)}) collective-permute-start(bf16[2,2,128,128]{3,2,1,0:T(8,128)(2,1)S(1)} %pad_maximum_fusion.1), channel_id=1, source_target_pairs={{0,256},{128,384},{256,0},{384,128},{1,257},{129,385},{257,1},{385... | collective-permute-start | bytes 393224 | tf_op jit(solution)/shard_map/ppermute | solution.py:27
  30.6 19.8 %collective-permute-start.5 = (bf16[8,2,128,128]{3,2,1,0:T(8,128)(2,1)S(1)}, bf16[8,2,128,128]{3,2,1,0:T(8,128)(2,1)S(1)}, u32[]{:S(2)}, u32[]{:S(2)}) collective-permute-start(bf16[8,2,128,128]{3,2,1,0:T(8,128)(2,1)S(1)} %pad_maximum_fusion.refs_3_), channel_id=1, source_target_pairs={{0,8},{8,16},{16,24},{24,32},{32,40},{40,48},{48,56},{56,0},{1,9},... | collective-permute-start | bytes 1572872 | tf_op jit(solution)/shard_map/ppermute | solution.py:27
  34.6 17.8 %collective-permute-start.9 = (bf16[8,2,128,128]{3,2,1,0:T(8,128)(2,1)S(1)}, bf16[8,2,128,128]{3,2,1,0:T(8,128)(2,1)S(1)}, u32[]{:S(2)}, u32[]{:S(2)}) collective-permute-start(bf16[8,2,128,128]{3,2,1,0:T(8,128)(2,1)S(1)} %pad_maximum_fusion.refs_3_), channel_id=1, source_target_pairs={{0,56},{8,0},{16,8},{24,16},{32,24},{40,32},{48,40},{56,48},{1,57}... | collective-permute-start | bytes 1572872 | tf_op jit(solution)/shard_map/ppermute | solution.py:27
  50.4 13.0 %collective-permute-start.6 = (bf16[8,2,128,128]{3,2,1,0:T(8,128)(2,1)S(1)}, bf16[8,2,128,128]{3,2,1,0:T(8,128)(2,1)}, u32[]{:S(2)}, u32[]{:S(2)}) collective-permute-start(bf16[8,2,128,128]{3,2,1,0:T(8,128)(2,1)S(1)} %collective-permute-done.5.refs_3_), channel_id=1, source_target_pairs={{0,8},{8,16},{16,24},{24,32},{32,40},{40,48},{48,56},{56,0},{1,9},... | collective-permute-start | bytes 1572872 | tf_op jit(solution)/shard_map/ppermute | solution.py:27
  52.4 19.5 %collective-permute-start.10 = (bf16[8,2,128,128]{3,2,1,0:T(8,128)(2,1)S(1)}, bf16[8,2,128,128]{3,2,1,0:T(8,128)(2,1)}, u32[]{:S(2)}, u32[]{:S(2)}) collective-permute-start(bf16[8,2,128,128]{3,2,1,0:T(8,128)(2,1)S(1)} %collective-permute-done.9.refs_4_), channel_id=1, source_target_pairs={{0,56},{8,0},{16,8},{24,16},{32,24},{40,32},{48,40},{56,48},{1,57}... | collective-permute-start | bytes 1572872 | tf_op jit(solution)/shard_map/ppermute | solution.py:27
  57.0 8.3 %collective-permute-start = (bf16[144,1024]{1,0:T(8,128)(2,1)S(1)}, bf16[144,1024]{1,0:T(8,128)(2,1)S(1)}, u32[]{:S(2)}, u32[]{:S(2)}) collective-permute-start(bf16[144,1024]{1,0:T(8,128)(2,1)S(1)} %fusion.1), channel_id=1, source_target_pairs={{0,0},{1,128},{128,1},{129,129},{64,64},{65,192},{192,65},{193,193... | collective-permute-start | bytes 884744 | tf_op jit(solution)/shard_map/ppermute | solution.py:279
  63.4 16.0 %collective-permute-start.7 = (bf16[8,2,128,128]{3,2,1,0:T(8,128)(2,1)}, bf16[8,2,128,128]{3,2,1,0:T(8,128)(2,1)S(1)}, u32[]{:S(2)}, u32[]{:S(2)}) collective-permute-start(bf16[8,2,128,128]{3,2,1,0:T(8,128)(2,1)} %collective-permute-done.6.refs_3_), channel_id=1, source_target_pairs={{0,8},{8,16},{16,24},{24,32},{32,40},{40,48},{48,56},{56,0},{1,9},... | collective-permute-start | bytes 1572872 | tf_op jit(solution)/shard_map/ppermute | solution.py:27
  65.3 11.6 %collective-permute-start.1 = (bf16[144,1024]{1,0:T(8,128)(2,1)S(1)}, bf16[144,1024]{1,0:T(8,128)(2,1)S(1)}, u32[]{:S(2)}, u32[]{:S(2)}) collective-permute-start(bf16[144,1024]{1,0:T(8,128)(2,1)S(1)} %collective-permute-done.refs_1_), channel_id=1, source_target_pairs={{0,1},{1,0},{2,3},{3,2},{4,5},{5,4},{6,7},{7,6},{8,9},{9,8},{10,11... | collective-permute-start | bytes 884744 | tf_op jit(solution)/shard_map/ppermute | solution.py:27
  71.9 17.5 %collective-permute-start.11 = (bf16[8,2,128,128]{3,2,1,0:T(8,128)(2,1)}, bf16[8,2,128,128]{3,2,1,0:T(8,128)(2,1)}, u32[]{:S(2)}, u32[]{:S(2)}) collective-permute-start(bf16[8,2,128,128]{3,2,1,0:T(8,128)(2,1)} %collective-permute-done.10.refs_4_), channel_id=1, source_target_pairs={{0,56},{8,0},{16,8},{24,16},{32,24},{40,32},{48,40},{56,48},{1,57}... | collective-permute-start | bytes 1572872 | tf_op jit(solution)/shard_map/ppermute | solution.py:27
  79.4 14.1 %collective-permute-start.8 = (bf16[4,2,128,128]{3,2,1,0:T(8,128)(2,1)S(1)}, bf16[4,2,128,128]{3,2,1,0:T(8,128)(2,1)S(1)}, u32[]{:S(2)}, u32[]{:S(2)}) collective-permute-start(bf16[4,2,128,128]{3,2,1,0:T(8,128)(2,1)S(1)} %get-tuple-element.35), channel_id=1, source_target_pairs={{0,8},{8,16},{16,24},{24,32},{32,40},{40,48},{48,56},{56,0},{1,9},... | collective-permute-start | bytes 786440 | tf_op jit(solution)/shard_map/ppermute | solution.py:27
  95.1 11.1 %collective-permute-start.12 = (f32[144,1024]{1,0:T(8,128)S(1)}, f32[144,1024]{1,0:T(8,128)S(1)}, u32[]{:S(2)}, u32[]{:S(2)}) collective-permute-start(f32[144,1024]{1,0:T(8,128)S(1)} %shard_map.87), channel_id=1, source_target_pairs={{0,1},{1,0},{2,3},{3,2},{4,5},{5,4},{6,7},{7,6},{8,9},{9,8},{10,11... | collective-permute-start | bytes 1769480 | tf_op jit(solution)/shard_map/ppermute | solution.py:27
  99.7 26.3 %collective-permute-start.17 = (bf16[4,2,128,128]{3,2,1,0:T(8,128)(2,1)S(1)}, bf16[4,2,128,128]{3,2,1,0:T(8,128)(2,1)S(1)}, u32[]{:S(2)}, u32[]{:S(2)}) collective-permute-start(bf16[4,2,128,128]{3,2,1,0:T(8,128)(2,1)S(1)} %slice.67.refs_6_), channel_id=1, source_target_pairs={{0,56},{8,0},{16,8},{24,16},{32,24},{40,32},{48,40},{56,48},{1,57}... | collective-permute-start | bytes 786440 | tf_op jit(solution)/shard_map/ppermute | solution.py:27
  106.4 20.5 %collective-permute-start.13 = (bf16[128,1024]{1,0:T(8,128)(2,1)S(1)}, bf16[128,1024]{1,0:T(8,128)(2,1)S(1)}, u32[]{:S(2)}, u32[]{:S(2)}) collective-permute-start(bf16[128,1024]{1,0:T(8,128)(2,1)S(1)} %shard_map.88), channel_id=1, source_target_pairs={{0,0},{1,128},{128,129},{129,257},{256,256},{257,384},{384,385},{3... | collective-permute-start | bytes 786440 | tf_op jit(solution)/shard_map/ppermute | solution.py:334
  118.7 8.8 %collective-permute-start.14 = (bf16[128,1024]{1,0:T(8,128)(2,1)S(1)}, bf16[128,1024]{1,0:T(8,128)(2,1)S(1)}, u32[]{:S(2)}, u32[]{:S(2)}) collective-permute-start(bf16[128,1024]{1,0:T(8,128)(2,1)S(1)} %shard_map.88), channel_id=1, source_target_pairs={{0,128},{1,256},{128,257},{129,385},{256,384},{257,0},{384,1},{385... | collective-permute-start | bytes 786440 | tf_op jit(solution)/shard_map/ppermute | solution.py:334
  120.9 12.0 %collective-permute-start.15 = (bf16[128,1024]{1,0:T(8,128)(2,1)S(1)}, bf16[128,1024]{1,0:T(8,128)(2,1)S(1)}, u32[]{:S(2)}, u32[]{:S(2)}) collective-permute-start(bf16[128,1024]{1,0:T(8,128)(2,1)S(1)} %shard_map.88), channel_id=1, source_target_pairs={{0,256},{1,384},{128,385},{129,1},{256,0},{257,128},{384,129},{385... | collective-permute-start | bytes 786440 | tf_op jit(solution)/shard_map/ppermute | solution.py:334
  123.2 9.7 %collective-permute-start.16 = (bf16[128,1024]{1,0:T(8,128)(2,1)S(1)}, bf16[128,1024]{1,0:T(8,128)(2,1)S(1)}, u32[]{:S(2)}, u32[]{:S(2)}) collective-permute-start(bf16[128,1024]{1,0:T(8,128)(2,1)S(1)} %shard_map.88), channel_id=1, source_target_pairs={{0,384},{1,0},{128,1},{129,129},{256,128},{257,256},{384,257},{385... | collective-permute-start | bytes 786440 | tf_op jit(solution)/shard_map/ppermute | solution.py:334
  133.6 7.7 %collective-permute-start.18 = (f32[4,128,512]{2,1,0:T(8,128)S(1)}, f32[4,128,512]{2,1,0:T(8,128)S(1)}, u32[]{:S(2)}, u32[]{:S(2)}) collective-permute-start(f32[4,128,512]{2,1,0:T(8,128)S(1)} %shard_map.91), channel_id=1, source_target_pairs={{0,1},{1,0},{2,3},{3,2},{4,5},{5,4},{6,7},{7,6},{8,9},{9,8},{10,11... | collective-permute-start | bytes 3145736 | tf_op jit(solution)/shard_map/ppermute | solution.py:27
  141.5 10.0 %collective-permute-start.19 = (bf16[128,512]{1,0:T(8,128)(2,1)S(1)}, bf16[128,512]{1,0:T(8,128)(2,1)S(1)}, u32[]{:S(2)}, u32[]{:S(2)}) collective-permute-start(bf16[128,512]{1,0:T(8,128)(2,1)S(1)} %get-tuple-element.31), channel_id=1, source_target_pairs={{0,2},{2,4},{4,6},{6,0},{1,3},{3,5},{5,7},{7,1},{8,10},{10,12},{12... | collective-permute-start | bytes 393224 | tf_op jit(solution)/shard_map/ppermute | solution.py:27
  145.6 13.2 %collective-permute-start.20 = (bf16[128,512]{1,0:T(8,128)(2,1)S(1)}, bf16[128,512]{1,0:T(8,128)(2,1)S(1)}, u32[]{:S(2)}, u32[]{:S(2)}) collective-permute-start(bf16[128,512]{1,0:T(8,128)(2,1)S(1)} %get-tuple-element.33), channel_id=1, source_target_pairs={{0,4},{2,6},{4,0},{6,2},{1,5},{3,7},{5,1},{7,3},{8,12},{10,14},{12... | collective-permute-start | bytes 393224 | tf_op jit(solution)/shard_map/ppermute | solution.py:27
  147.5 11.3 %collective-permute-start.21 = (bf16[128,512]{1,0:T(8,128)(2,1)S(1)}, bf16[128,512]{1,0:T(8,128)(2,1)S(1)}, u32[]{:S(2)}, u32[]{:S(2)}) collective-permute-start(bf16[128,512]{1,0:T(8,128)(2,1)S(1)} %get-tuple-element.32), channel_id=1, source_target_pairs={{0,6},{2,0},{4,2},{6,4},{1,7},{3,1},{5,3},{7,5},{8,14},{10,8},{12,... | collective-permute-start | bytes 393224 | tf_op jit(solution)/shard_map/ppermute | solution.py:27
  158.9 14.5 %collective-permute-start.22 = (bf16[128,512]{1,0:T(8,128)(2,1)S(1)}, bf16[128,512]{1,0:T(8,128)(2,1)S(1)}, u32[]{:S(2)}, u32[]{:S(2)}) collective-permute-start(bf16[128,512]{1,0:T(8,128)(2,1)S(1)} %fusion.10), channel_id=1, source_target_pairs={{0,0},{2,384},{4,256},{6,128},{128,130},{130,2},{132,386},{134,258... | collective-permute-start | bytes 393224 | tf_op jit(solution)/shard_map/ppermute | solution.py:352
